TPU v7x, 32 devices: a whole 2x2x4 slice. The times are simulated.
32 devices in a mesh: wide: 8 (over z, x), narrow: 4 (over y, core).
Axes of the slice: x: 2, y: 2, z: 4, core: 2. Of those that a mesh axis runs over, the one named last changes fastest.
Arguments:
- inputs: bfloat16 [256, 14, 14, 768], P(('wide', 'narrow')), may hold values from -6 to 6
- heights: int32 [256], P(('wide', 'narrow')), may hold values from 8 to 14, as said below
- widths: int32 [256], P(('wide', 'narrow')), may hold values from 8 to 14, as said below
- conv_weight: bfloat16 [4, 9, 768], P('narrow', None, 'wide'), may hold values from -2 to 2
- conv_bias: bfloat16 [4, 768], P('narrow', 'wide'), may hold values from -0.59765625 to 0.59765625
- norm_gain: bfloat16 [4, 768], P('narrow', 'wide'), may hold values from 0.099609375 to 1.8984375
- norm_bias: bfloat16 [4, 768], P('narrow', 'wide'), may hold values from -0.59765625 to 0.59765625
- spatial_qkv: bfloat16 [2304, 768], P('wide', 'narrow'), may hold values from -0.21875 to 0.21875
- channel_qkv: bfloat16 [2304, 768], P('wide', 'narrow'), may hold values from -0.102062073 to 0.102062073
- projection: bfloat16 [2, 768, 768], P(None, 'wide', 'narrow'), may hold values from -0.875 to 0.875
- mlp_in: bfloat16 [2, 3072, 768], P(None, 'wide', 'narrow'), may hold values from -0.21875 to 0.21875
- mlp_out: bfloat16 [2, 768, 3072], P(None, 'wide', 'narrow'), may hold values from -0.15625 to 0.15625
- attn_bias: bfloat16 [5, 768], P(None, 'wide'), may hold values from -0.59765625 to 0.59765625
- hidden_bias: bfloat16 [2, 3072], P(None, 'wide'), may hold values from -3 to 3
- out_bias: bfloat16 [4, 768], P('narrow', 'wide'), may hold values from -0.59765625 to 0.59765625
- cotangent: bfloat16 [256, 14, 14, 768], P(('wide', 'narrow')), may hold values from -6 to 6
Outputs:
- block_out: bfloat16 [256, 14, 14, 768], P(('wide', 'narrow'))
- input_grad: bfloat16 [256, 14, 14, 768], P(('wide', 'narrow'))
- conv_weight_grad: float32 [4, 9, 768], P('narrow', None, 'wide')
- conv_bias_grad: float32 [4, 768], P('narrow', 'wide')
- norm_gain_grad: float32 [4, 768], P('narrow', 'wide')
- norm_bias_grad: float32 [4, 768], P('narrow', 'wide')
- spatial_qkv_grad: float32 [2304, 768], P('wide', 'narrow')
- channel_qkv_grad: float32 [2304, 768], P('wide', 'narrow')
- projection_grad: float32 [2, 768, 768], P(None, 'wide', 'narrow')
- mlp_in_grad: float32 [2, 3072, 768], P(None, 'wide', 'narrow')
- mlp_out_grad: float32 [2, 768, 3072], P(None, 'wide', 'narrow')
- attn_bias_grad: float32 [5, 768], P(None, 'wide')
- hidden_bias_grad: float32 [2, 3072], P(None, 'wide')
- out_bias_grad: float32 [4, 768], P('narrow', 'wide')
Inputs may be any that keep to these rules, and one draw needn't show every extreme that they name: `heights`: every value from 8 to 14 occurs. `widths`: every value from 8 to 14 occurs.
All inputs are finite; a program needn't handle non-finite values.
Results may differ from a plain program's by a relative error of at most 0.018.
Values may be sent and summed in bfloat16 or wider, within the bound.
A program may use at most 576 MiB of HBM per device.

v0:
```python
import jax
import jax.numpy as jnp
from jax import lax
from jax.sharding import PartitionSpec as P

HD = 32
WIN = 7
HEADS = 24


epsilon = 1e-05
masked_score = -1e30


def layer_norm(values, gain_row, bias_row):
    center = values - jnp.mean(values, axis=-1, keepdims=True)
    spread = jnp.mean(center * center, axis=-1, keepdims=True)
    return center * lax.rsqrt(spread + epsilon) * gain_row + bias_row


def depthwise(values, kernel, bias_row):
    tile_rows, tile_cols = (values.shape[1], values.shape[2])
    padded = jnp.pad(values, ((0, 0), (1, 1), (1, 1), (0, 0)))
    summed = jnp.zeros_like(values) + bias_row
    for row_step in range(3):
        for col_step in range(3):
            summed = (
                summed
                + kernel[3 * row_step + col_step]
                * padded[:, row_step : row_step + tile_rows, col_step : col_step + tile_cols, :]
            )
    return summed


def gelu_exact(values):
    return 0.5 * values * (1.0 + lax.erf(values * 0.7071067811865476))


def softmax_last(scores):
    row_max = jnp.max(scores, axis=-1, keepdims=True)
    exponent = jnp.exp(scores - row_max)
    return exponent / jnp.sum(exponent, axis=-1, keepdims=True)


def to_windows(tile_cells):
    images, tile_rows, tile_cols, features = tile_cells.shape
    blocks = tile_cells.reshape(images, tile_rows // WIN, WIN, tile_cols // WIN, WIN, features)
    return blocks.transpose(0, 1, 3, 2, 4, 5).reshape(-1, WIN * WIN, features)


def from_windows(windows, images, tile_rows, tile_cols):
    features = windows.shape[-1]
    blocks = windows.reshape(images, tile_rows // WIN, tile_cols // WIN, WIN, WIN, features)
    return blocks.transpose(0, 1, 3, 2, 4, 5).reshape(images, tile_rows, tile_cols, features)


def linear_map(rows_in, weight):
    return lax.dot_general(
        rows_in, weight, (((1,), (1,)), ((), ())), preferred_element_type=jnp.float32
    )


def weight_grad(grad_rows, rows_in):
    return lax.dot_general(
        grad_rows, rows_in, (((0,), (0,)), ((), ())), preferred_element_type=jnp.float32
    )


def input_back(grad_rows, weight):
    return jnp.dot(grad_rows, weight, preferred_element_type=jnp.float32)


def column_sums(grad_rows):
    return jnp.sum(grad_rows, axis=0, dtype=jnp.float32)


def spatial_forward(normed, valid_cells, weight, bias_vec, proj_weight, out_row):
    images, tile_rows, tile_cols, features = normed.shape
    flat_rows = normed.reshape(-1, features)
    qkv_rows = (linear_map(flat_rows, weight) + bias_vec).astype(jnp.bfloat16)
    qkv_parts = to_windows(qkv_rows.reshape(images, tile_rows, tile_cols, 3 * features))
    windows_count = qkv_parts.shape[0]
    qkv_parts = qkv_parts.reshape(windows_count, WIN * WIN, 3, HEADS, HD)
    queries, key_part, value_part = (qkv_parts[:, :, 0], qkv_parts[:, :, 1], qkv_parts[:, :, 2])
    scores = jnp.einsum(
        "wqhd,wkhd->whqk", queries, key_part, preferred_element_type=jnp.float32
    ) * HD ** (-0.5)
    key_valid = to_windows(valid_cells[..., None])[:, :, 0]
    scores = jnp.where(key_valid[:, None, None, :], scores, masked_score)
    prob_exact = softmax_last(scores)
    attn_prob = prob_exact.astype(jnp.bfloat16)
    mixed_out = jnp.einsum(
        "whqk,wkhd->wqhd", attn_prob, value_part, preferred_element_type=jnp.float32
    ).astype(jnp.bfloat16)
    merged = from_windows(
        mixed_out.reshape(windows_count, WIN * WIN, features), images, tile_rows, tile_cols
    ).reshape(-1, features)
    branch = (linear_map(merged, proj_weight) + out_row).reshape(normed.shape)
    return (branch, (flat_rows, queries, key_part, value_part, prob_exact, attn_prob, merged))


def spatial_backward(grad_in, kept, weight, proj_weight):
    flat_rows, queries, key_part, value_part, prob_exact, attn_prob, merged = kept
    images, tile_rows, tile_cols, features = grad_in.shape
    windows_count = queries.shape[0]
    score_scale = HD ** (-0.5)
    grad_low = grad_in.reshape(-1, features).astype(jnp.bfloat16)
    proj_grad = weight_grad(grad_low, merged)
    out_grad = column_sums(grad_low)
    grad_mixed = input_back(grad_low, proj_weight).astype(jnp.bfloat16)
    grad_mixed = to_windows(grad_mixed.reshape(images, tile_rows, tile_cols, features)).reshape(
        windows_count, WIN * WIN, HEADS, HD
    )
    grad_prob = jnp.einsum(
        "wqhd,wkhd->whqk", grad_mixed, value_part, preferred_element_type=jnp.float32
    )
    grad_value = jnp.einsum(
        "whqk,wqhd->wkhd", attn_prob, grad_mixed, preferred_element_type=jnp.float32
    )
    grad_score = (
        prob_exact * (grad_prob - jnp.sum(grad_prob * prob_exact, axis=-1, keepdims=True))
    ).astype(jnp.bfloat16)
    grad_query = (
        jnp.einsum("whqk,wkhd->wqhd", grad_score, key_part, preferred_element_type=jnp.float32)
        * score_scale
    )
    grad_key = (
        jnp.einsum("whqk,wqhd->wkhd", grad_score, queries, preferred_element_type=jnp.float32)
        * score_scale
    )
    grad_qkv = jnp.stack([grad_query, grad_key, grad_value], axis=2).astype(jnp.bfloat16)
    grad_qkv = from_windows(
        grad_qkv.reshape(windows_count, WIN * WIN, 3 * features), images, tile_rows, tile_cols
    ).reshape(-1, 3 * features)
    qkv_grad = weight_grad(grad_qkv, flat_rows)
    bias_grad = column_sums(grad_qkv)
    normed_grad = input_back(grad_qkv, weight).reshape(grad_in.shape)
    return (
        normed_grad,
        qkv_grad,
        jnp.stack([bias_grad[:features], bias_grad[2 * features :]]),
        proj_grad,
        out_grad,
    )


def channel_forward(normed, cell_mask, weight, bias_vec, proj_weight, out_row):
    images, tile_rows, tile_cols, features = normed.shape
    tokens = tile_rows * tile_cols
    flat_rows = normed.reshape(-1, features)
    qkv_rows = (
        (linear_map(flat_rows, weight) + bias_vec)
        .astype(jnp.bfloat16)
        .reshape(images, tokens, 3, HEADS, HD)
    )
    queries, value_part = (qkv_rows[:, :, 0], qkv_rows[:, :, 2])
    token_mask = cell_mask.reshape(images, tokens, 1, 1).astype(jnp.bfloat16)
    masked_keys = qkv_rows[:, :, 1] * token_mask
    scores = jnp.einsum(
        "gnhd,gnhe->ghde", queries, masked_keys, preferred_element_type=jnp.float32
    ) * HD ** (-0.5)
    prob_exact = softmax_last(scores)
    attn_prob = prob_exact.astype(jnp.bfloat16)
    mixed_out = (
        jnp.einsum("ghde,gnhe->gnhd", attn_prob, value_part, preferred_element_type=jnp.float32)
        .astype(jnp.bfloat16)
        .reshape(-1, features)
    )
    branch = (linear_map(mixed_out, proj_weight) + out_row).reshape(normed.shape)
    return (
        branch,
        (flat_rows, queries, masked_keys, value_part, token_mask, prob_exact, attn_prob, mixed_out),
    )


def channel_backward(grad_in, kept, weight, proj_weight):
    flat_rows, queries, masked_keys, value_part, token_mask, prob_exact, attn_prob, mixed_out = kept
    images, tile_rows, tile_cols, features = grad_in.shape
    tokens = tile_rows * tile_cols
    score_scale = HD ** (-0.5)
    grad_low = grad_in.reshape(-1, features).astype(jnp.bfloat16)
    proj_grad = weight_grad(grad_low, mixed_out)
    out_grad = column_sums(grad_low)
    grad_mixed = (
        input_back(grad_low, proj_weight).astype(jnp.bfloat16).reshape(images, tokens, HEADS, HD)
    )
    grad_prob = jnp.einsum(
        "gnhd,gnhe->ghde", grad_mixed, value_part, preferred_element_type=jnp.float32
    )
    grad_value = jnp.einsum(
        "ghde,gnhd->gnhe", attn_prob, grad_mixed, preferred_element_type=jnp.float32
    )
    grad_score = (
        prob_exact * (grad_prob - jnp.sum(grad_prob * prob_exact, axis=-1, keepdims=True))
    ).astype(jnp.bfloat16)
    grad_query = (
        jnp.einsum("ghde,gnhe->gnhd", grad_score, masked_keys, preferred_element_type=jnp.float32)
        * score_scale
    )
    grad_key = (
        jnp.einsum("ghde,gnhd->gnhe", grad_score, queries, preferred_element_type=jnp.float32)
        * score_scale
        * token_mask
    )
    grad_qkv = (
        jnp.stack([grad_query, grad_key, grad_value], axis=2)
        .astype(jnp.bfloat16)
        .reshape(-1, 3 * features)
    )
    qkv_grad = weight_grad(grad_qkv, flat_rows)
    bias_grad = column_sums(grad_qkv).reshape(3, features)
    normed_grad = input_back(grad_qkv, weight).reshape(grad_in.shape)
    return (normed_grad, qkv_grad, bias_grad, proj_grad, out_grad)


def mlp_forward(normed, in_weight, hidden_row, out_weight, out_row):
    features = normed.shape[-1]
    flat_rows = normed.reshape(-1, features)
    hidden = linear_map(flat_rows, in_weight) + hidden_row
    active = gelu_exact(hidden).astype(jnp.bfloat16)
    branch = (linear_map(active, out_weight) + out_row).reshape(normed.shape)
    return (branch, (flat_rows, hidden, active))


def mlp_backward(grad_in, kept, in_weight, out_weight):
    flat_rows, hidden, active = kept
    grad_low = grad_in.reshape(-1, grad_in.shape[-1]).astype(jnp.bfloat16)
    reduce_grad = weight_grad(grad_low, active)
    out_grad = column_sums(grad_low)
    grad_active = input_back(grad_low, out_weight)
    grad_hidden = jax.vjp(gelu_exact, hidden)[1](grad_active)[0].astype(jnp.bfloat16)
    expand_grad = weight_grad(grad_hidden, flat_rows)
    hidden_grad = column_sums(grad_hidden)
    normed_grad = input_back(grad_hidden, in_weight).reshape(grad_in.shape)
    return (normed_grad, expand_grad, hidden_grad, reduce_grad, out_grad)


def norm_backward(stream, gain_row, bias_row, grad_normed):
    return jax.vjp(layer_norm, stream, gain_row, bias_row)[1](grad_normed)


def conv_backward(stream, mask_cells, kernel, bias_row, grad_out):

    def masked_conv(values, kernel_in, shift_row):
        return depthwise(values * mask_cells, kernel_in, shift_row)

    return jax.vjp(masked_conv, stream, kernel, bias_row)[1](grad_out)


def unpack_params(gathered):
    return (
        gathered[0],
        gathered[1],
        gathered[2],
        gathered[3],
        gathered[4],
        gathered[5].astype(jnp.float32),
        gathered[6].astype(jnp.float32),
        gathered[7].astype(jnp.float32),
        gathered[8].astype(jnp.float32),
        gathered[9].astype(jnp.float32),
        gathered[10].astype(jnp.float32),
        gathered[11].astype(jnp.float32),
    )


def to_front(values, dims):
    return [jnp.moveaxis(item, place, 0) for item, place in zip(values, dims)]


def from_front(values, dims):
    return [jnp.moveaxis(item, 0, place) for item, place in zip(values, dims)]


def local(
    inputs,
    heights,
    widths,
    conv_weight,
    conv_bias,
    norm_gain,
    norm_bias,
    spatial_qkv,
    channel_qkv,
    projection,
    mlp_in,
    mlp_out,
    attn_bias,
    hidden_bias,
    out_bias,
    cotangent,
):
    cols_part = (
        lax.all_gather(spatial_qkv, "narrow", axis=1, tiled=True),
        lax.all_gather(channel_qkv, "narrow", axis=1, tiled=True),
        lax.all_gather(projection, "narrow", axis=2, tiled=True),
        lax.all_gather(mlp_in, "narrow", axis=2, tiled=True),
        lax.all_gather(mlp_out, "narrow", axis=2, tiled=True),
        lax.all_gather(conv_weight, "narrow", axis=0, tiled=True),
        lax.all_gather(conv_bias, "narrow", axis=0, tiled=True),
        lax.all_gather(norm_gain, "narrow", axis=0, tiled=True),
        lax.all_gather(norm_bias, "narrow", axis=0, tiled=True),
        lax.all_gather(out_bias, "narrow", axis=0, tiled=True),
    )
    gathered = (
        lax.all_gather(cols_part[0], "wide", axis=0, tiled=True),
        lax.all_gather(cols_part[1], "wide", axis=0, tiled=True),
        lax.all_gather(cols_part[2], "wide", axis=1, tiled=True),
        lax.all_gather(cols_part[3], "wide", axis=1, tiled=True),
        lax.all_gather(cols_part[4], "wide", axis=1, tiled=True),
        lax.all_gather(cols_part[5], "wide", axis=2, tiled=True),
        lax.all_gather(cols_part[6], "wide", axis=1, tiled=True),
        lax.all_gather(cols_part[7], "wide", axis=1, tiled=True),
        lax.all_gather(cols_part[8], "wide", axis=1, tiled=True),
        lax.all_gather(cols_part[9], "wide", axis=1, tiled=True),
        lax.all_gather(attn_bias, "wide", axis=1, tiled=True),
        lax.all_gather(hidden_bias, "wide", axis=1, tiled=True),
    )
    (
        spatial_full,
        channel_full,
        proj_full,
        expand_full,
        reduce_full,
        conv_kernels,
        conv_shifts,
        norm_gains,
        norm_shifts,
        out_shifts,
        attn_shifts,
        hidden_shifts,
    ) = unpack_params(gathered)
    images, tile_rows, tile_cols, features = inputs.shape
    row_ids = jnp.arange(tile_rows, dtype=jnp.int32)
    col_ids = jnp.arange(tile_cols, dtype=jnp.int32)
    valid_cells = (row_ids[None, :, None] < heights[:, None, None]) & (
        col_ids[None, None, :] < widths[:, None, None]
    )
    cell_mask = valid_cells.astype(jnp.float32)
    mask_cells = cell_mask[..., None]
    stream0 = inputs.astype(jnp.float32)
    stream1 = stream0 + depthwise(stream0 * mask_cells, conv_kernels[0], conv_shifts[0])
    normed1 = layer_norm(stream1, norm_gains[0], norm_shifts[0]).astype(jnp.bfloat16)
    spatial_bias = jnp.concatenate([attn_shifts[0], jnp.zeros_like(attn_shifts[0]), attn_shifts[1]])
    branch, spatial_kept = spatial_forward(
        normed1, valid_cells, spatial_full, spatial_bias, proj_full[0], out_shifts[0]
    )
    stream2 = stream1 + branch
    stream3 = stream2 + depthwise(stream2 * mask_cells, conv_kernels[1], conv_shifts[1])
    normed2 = layer_norm(stream3, norm_gains[1], norm_shifts[1]).astype(jnp.bfloat16)
    branch, first_kept = mlp_forward(
        normed2, expand_full[0], hidden_shifts[0], reduce_full[0], out_shifts[1]
    )
    stream4 = stream3 + branch
    stream5 = stream4 + depthwise(stream4 * mask_cells, conv_kernels[2], conv_shifts[2])
    normed3 = layer_norm(stream5, norm_gains[2], norm_shifts[2]).astype(jnp.bfloat16)
    branch, channel_kept = channel_forward(
        normed3, cell_mask, channel_full, attn_shifts[2:5].reshape(-1), proj_full[1], out_shifts[2]
    )
    stream6 = stream5 + branch
    stream7 = stream6 + depthwise(stream6 * mask_cells, conv_kernels[3], conv_shifts[3])
    normed4 = layer_norm(stream7, norm_gains[3], norm_shifts[3]).astype(jnp.bfloat16)
    branch, second_kept = mlp_forward(
        normed4, expand_full[1], hidden_shifts[1], reduce_full[1], out_shifts[3]
    )
    stream8 = stream7 + branch
    block_out = (stream8 * mask_cells).astype(jnp.bfloat16)
    gradient = cotangent.astype(jnp.float32) * mask_cells
    (
        spatial_back,
        channel_back,
        proj_back,
        expand_back,
        reduce_back,
        kernels_back,
        conv_shift_back,
        gains_back,
        norm_shift_back,
        out_shift_back,
        attn_shift_back,
        hidden_shift_back,
    ) = unpack_params(gathered)
    normed_grad, expand_grad1, hidden_grad1, reduce_grad1, out_grad3 = mlp_backward(
        gradient, second_kept, expand_back[1], reduce_back[1]
    )
    stream_grad, gain_grad3, shift_grad3 = norm_backward(
        stream7, gains_back[3], norm_shift_back[3], normed_grad
    )
    gradient = gradient + stream_grad
    conv_grad, kernel_grad3, bias_grad3 = conv_backward(
        stream6, mask_cells, kernels_back[3], conv_shift_back[3], gradient
    )
    gradient = gradient + conv_grad
    normed_grad, channel_grad, channel_bias_grad, proj_grad1, out_grad2 = channel_backward(
        gradient, channel_kept, channel_back, proj_back[1]
    )
    stream_grad, gain_grad2, shift_grad2 = norm_backward(
        stream5, gains_back[2], norm_shift_back[2], normed_grad
    )
    gradient = gradient + stream_grad
    conv_grad, kernel_grad2, bias_grad2 = conv_backward(
        stream4, mask_cells, kernels_back[2], conv_shift_back[2], gradient
    )
    gradient = gradient + conv_grad
    normed_grad, expand_grad0, hidden_grad0, reduce_grad0, out_grad1 = mlp_backward(
        gradient, first_kept, expand_back[0], reduce_back[0]
    )
    stream_grad, gain_grad1, shift_grad1 = norm_backward(
        stream3, gains_back[1], norm_shift_back[1], normed_grad
    )
    gradient = gradient + stream_grad
    conv_grad, kernel_grad1, bias_grad1 = conv_backward(
        stream2, mask_cells, kernels_back[1], conv_shift_back[1], gradient
    )
    gradient = gradient + conv_grad
    normed_grad, spatial_grad, spatial_bias_grad, proj_grad0, out_grad0 = spatial_backward(
        gradient, spatial_kept, spatial_back, proj_back[0]
    )
    stream_grad, gain_grad0, shift_grad0 = norm_backward(
        stream1, gains_back[0], norm_shift_back[0], normed_grad
    )
    gradient = gradient + stream_grad
    conv_grad, kernel_grad0, bias_grad0 = conv_backward(
        stream0, mask_cells, kernels_back[0], conv_shift_back[0], gradient
    )
    gradient = gradient + conv_grad
    input_grad = gradient.astype(jnp.bfloat16)
    grad_terms = [
        spatial_grad,
        channel_grad,
        proj_grad0,
        proj_grad1,
        expand_grad0,
        expand_grad1,
        reduce_grad0,
        reduce_grad1,
        jnp.stack([kernel_grad0, kernel_grad1, kernel_grad2, kernel_grad3]),
        jnp.stack([bias_grad0, bias_grad1, bias_grad2, bias_grad3]),
        jnp.stack([gain_grad0, gain_grad1, gain_grad2, gain_grad3]),
        jnp.stack([shift_grad0, shift_grad1, shift_grad2, shift_grad3]),
        jnp.stack([out_grad0, out_grad1, out_grad2, out_grad3]),
    ]
    wide_dims = [0, 0, 0, 0, 0, 0, 0, 0, 2, 1, 1, 1, 1]
    narrow_dims = [1, 1, 1, 1, 1, 1, 1, 1, 0, 0, 0, 0, 0]
    bias_terms = [
        jnp.concatenate([spatial_bias_grad, channel_bias_grad]),
        jnp.stack([hidden_grad0, hidden_grad1]),
    ]
    moved = to_front(grad_terms + bias_terms, wide_dims + [1, 1])
    rows_sum = (
        lax.psum_scatter(moved[0], "wide", scatter_dimension=0, tiled=True),
        lax.psum_scatter(moved[1], "wide", scatter_dimension=0, tiled=True),
        lax.psum_scatter(moved[2], "wide", scatter_dimension=0, tiled=True),
        lax.psum_scatter(moved[3], "wide", scatter_dimension=0, tiled=True),
        lax.psum_scatter(moved[4], "wide", scatter_dimension=0, tiled=True),
        lax.psum_scatter(moved[5], "wide", scatter_dimension=0, tiled=True),
        lax.psum_scatter(moved[6], "wide", scatter_dimension=0, tiled=True),
        lax.psum_scatter(moved[7], "wide", scatter_dimension=0, tiled=True),
        lax.psum_scatter(moved[8], "wide", scatter_dimension=0, tiled=True),
        lax.psum_scatter(moved[9], "wide", scatter_dimension=0, tiled=True),
        lax.psum_scatter(moved[10], "wide", scatter_dimension=0, tiled=True),
        lax.psum_scatter(moved[11], "wide", scatter_dimension=0, tiled=True),
        lax.psum_scatter(moved[12], "wide", scatter_dimension=0, tiled=True),
        lax.psum_scatter(moved[13], "wide", scatter_dimension=0, tiled=True),
        lax.psum_scatter(moved[14], "wide", scatter_dimension=0, tiled=True),
    )
    partial_value = from_front(list(rows_sum), wide_dims + [1, 1])
    moved = to_front(partial_value[:13], narrow_dims)
    cols_sum = (
        lax.psum_scatter(
            moved[0].astype(jnp.bfloat16), "narrow", scatter_dimension=0, tiled=True
        ).astype(jnp.float32),
        lax.psum_scatter(
            moved[1].astype(jnp.bfloat16), "narrow", scatter_dimension=0, tiled=True
        ).astype(jnp.float32),
        lax.psum_scatter(
            moved[2].astype(jnp.bfloat16), "narrow", scatter_dimension=0, tiled=True
        ).astype(jnp.float32),
        lax.psum_scatter(
            moved[3].astype(jnp.bfloat16), "narrow", scatter_dimension=0, tiled=True
        ).astype(jnp.float32),
        lax.psum_scatter(
            moved[4].astype(jnp.bfloat16), "narrow", scatter_dimension=0, tiled=True
        ).astype(jnp.float32),
        lax.psum_scatter(
            moved[5].astype(jnp.bfloat16), "narrow", scatter_dimension=0, tiled=True
        ).astype(jnp.float32),
        lax.psum_scatter(
            moved[6].astype(jnp.bfloat16), "narrow", scatter_dimension=0, tiled=True
        ).astype(jnp.float32),
        lax.psum_scatter(
            moved[7].astype(jnp.bfloat16), "narrow", scatter_dimension=0, tiled=True
        ).astype(jnp.float32),
        lax.psum_scatter(
            moved[8].astype(jnp.bfloat16), "narrow", scatter_dimension=0, tiled=True
        ).astype(jnp.float32),
        lax.psum_scatter(
            moved[9].astype(jnp.bfloat16), "narrow", scatter_dimension=0, tiled=True
        ).astype(jnp.float32),
        lax.psum_scatter(
            moved[10].astype(jnp.bfloat16), "narrow", scatter_dimension=0, tiled=True
        ).astype(jnp.float32),
        lax.psum_scatter(
            moved[11].astype(jnp.bfloat16), "narrow", scatter_dimension=0, tiled=True
        ).astype(jnp.float32),
        lax.psum_scatter(
            moved[12].astype(jnp.bfloat16), "narrow", scatter_dimension=0, tiled=True
        ).astype(jnp.float32),
    )
    sharded_sums = from_front(list(cols_sum), narrow_dims)
    bias_sums = lax.psum((partial_value[13], partial_value[14]), "narrow")
    proj_total = jnp.stack([sharded_sums[2], sharded_sums[3]])
    expand_total = jnp.stack([sharded_sums[4], sharded_sums[5]])
    reduce_total = jnp.stack([sharded_sums[6], sharded_sums[7]])
    return (
        block_out,
        input_grad,
        sharded_sums[8],
        sharded_sums[9],
        sharded_sums[10],
        sharded_sums[11],
        sharded_sums[0],
        sharded_sums[1],
        proj_total,
        expand_total,
        reduce_total,
        bias_sums[0],
        bias_sums[1],
        sharded_sums[12],
    )


def solution(mesh):
    in_specs = (
        P(("wide", "narrow"), None, None, None),
        P(("wide", "narrow")),
        P(("wide", "narrow")),
        P("narrow", None, "wide"),
        P("narrow", "wide"),
        P("narrow", "wide"),
        P("narrow", "wide"),
        P("wide", "narrow"),
        P("wide", "narrow"),
        P(None, "wide", "narrow"),
        P(None, "wide", "narrow"),
        P(None, "wide", "narrow"),
        P(None, "wide"),
        P(None, "wide"),
        P("narrow", "wide"),
        P(("wide", "narrow"), None, None, None),
    )
    out_specs = (
        P(("wide", "narrow"), None, None, None),
        P(("wide", "narrow"), None, None, None),
        P("narrow", None, "wide"),
        P("narrow", "wide"),
        P("narrow", "wide"),
        P("narrow", "wide"),
        P("wide", "narrow"),
        P("wide", "narrow"),
        P(None, "wide", "narrow"),
        P(None, "wide", "narrow"),
        P(None, "wide", "narrow"),
        P(None, "wide"),
        P(None, "wide"),
        P("narrow", "wide"),
    )
    return jax.shard_map(local, mesh=mesh, in_specs=in_specs, out_specs=out_specs, check_vma=False)
```

profile of v0, /device:TPU:0, one launch (start us, length us, event | category | flops | bytes accessed | tf_op | source)
XLA Modules:
  0.0 3350.4 jit_solution(8333000823960603545)
XLA Ops:
  60.4 26.1 all-gather.6
  92.0 34.0 %all_gather.69 = bf16[4,9,768]{1,0,2:T(4,128)(2,1)S(1)} all-gather(bf16[4,9,96]{1,0,2:T(4,128)(2,1)S(1)} %copy.195), channel_id=1, replica_groups=mesh['wide'=8,'narrow'=4] {'wide'}, dimensions={2}, use_global_device_ids=true | all-gather | bytes 62208 | tf_op jit(solution)/shard_map/all_gather | solution.py:311
  126.2 50.7 %slice_reduce_fusion.26 = (f32[768]{0:T(1024)}, f32[768]{0:T(1024)}, f32[768]{0:T(1024)}, f32[768]{0:T(1024)}, f32[768]{0:T(1024)}, /*index=5*/f32[768]{0:T(1024...) fusion(f32[4,9,768]{1,0,2:T(4,128)S(1)} %convert_element_type.331), kind=kLoop, calls=%fused_computation.317 | loop fusion | bytes 104448 | tf_op jit(solution)/shard_map/slice | solution.py:29
  176.9 57.8 %slice_reduce_fusion.8 = (f32[768]{0:T(1024)}, f32[768]{0:T(1024)}, f32[768]{0:T(1024)}, f32[768]{0:T(1024)}, f32[768]{0:T(1024)}, /*index=5*/f32[768]{0:T(1024)...) fusion(f32[4,9,768]{1,0,2:T(4,128)S(1)} %convert_element_type.331), kind=kLoop, calls=%fused_computation.299 | loop fusion | bytes 116736 | tf_op jit(solution)/shard_map/slice | solution.py:29
  254.9 18.9 all-gather.8
  328.4 26.4 all_gather.83
  360.2 21.7 fusion.112
  425.4 36.2 %reshape_reshape.23 = bf16[32,49,3,24,32]{4,3,2,0,1:T(8,128)(2,1)} reshape(bf16[8,2,2,7,7,2304]{5,2,1,0,4,3:T(2,128)(2,1)} %copy.201) | data formatting | bytes 14450688 | tf_op jit(solution)/shard_map/reshape;reshape | solution.py:83
  461.6 23.6 fusion.113
  535.5 29.0 fusion.117
  630.4 23.7 fusion.111
  710.0 23.1 fusion.110
  762.5 19.0 reshape.612
  827.7 23.6 fusion.109
  894.1 19.8 convert_reduce_fusion
  951.7 27.1 multiply_reduce_fusion.13
  1062.2 31.8 copy.255
  1094.0 31.4 reshape.646
  1141.9 29.2 multiply_reduce_fusion.22
  1219.5 20.8 convert_reduce_fusion.1
  1272.5 29.6 multiply_reduce_fusion.31
  1329.7 18.9 convert_reduce_fusion.7
  1403.3 21.9 multiply_reduce_fusion
  1425.1 18.8 multiply_convert_fusion
  1482.6 33.1 copy.235
  1515.7 39.2 %convert_element_type.373 = bf16[8,2,2,7,7,2304]{5,2,1,0,4,3:T(2,128)(2,1)} reshape(bf16[32,49,3,24,32]{4,3,2,0,1:T(8,128)(2,1)} %copy.235) | data formatting | bytes 14450688 | tf_op jit(solution)/shard_map/convert_element_type | solution.py:131
  1577.4 25.2 fusion.105
  1789.6 23.7 reduce-scatter.57.cloned.1.call-done
  1815.1 129.9 %reduce-scatter.55.cloned.1.call-done = f32[288,768]{1,0:T(8,128)} async-done(((f32[2304,768]{1,0:T(8,128)}), f32[288,768]{1,0:T(8,128)}) %reduce-scatter.55.cloned.1.call-update) | async-done | bytes 884752 | tf_op jit(solution)/shard_map/reduce_scatter | solution.py:452
  1947.4 129.7 %reduce-scatter.53.cloned.1.call-done = f32[288,768]{1,0:T(8,128)} async-done(((f32[2304,768]{1,0:T(8,128)}), f32[288,768]{1,0:T(8,128)}) %reduce-scatter.53.cloned.1.call-update) | async-done | bytes 884752 | tf_op jit(solution)/shard_map/reduce_scatter | solution.py:451
  2079.5 163.7 %reduce-scatter.63.cloned.1.call-done = f32[384,768]{1,0:T(8,128)} async-done(((f32[3072,768]{1,0:T(8,128)}), f32[384,768]{1,0:T(8,128)}) %reduce-scatter.63.cloned.1.call-update) | async-done | bytes 1179664 | tf_op jit(solution)/shard_map/reduce_scatter | solution.py:456
  2245.7 163.6 %reduce-scatter.61.cloned.1.call-done = f32[384,768]{1,0:T(8,128)} async-done(((f32[3072,768]{1,0:T(8,128)}), f32[384,768]{1,0:T(8,128)}) %reduce-scatter.61.cloned.1.call-update) | async-done | bytes 1179664 | tf_op jit(solution)/shard_map/reduce_scatter | solution.py:455
  2412.4 162.8 %reduce-scatter.69.cloned.1.call-done = f32[96,3072]{1,0:T(8,128)} async-done(((f32[768,3072]{1,0:T(8,128)}), f32[96,3072]{1,0:T(8,128)}) %reduce-scatter.69.cloned.1.call-update) | async-done | bytes 1179664 | tf_op jit(solution)/shard_map/reduce_scatter | solution.py:458
  2605.3 135.8 %reduce-scatter.65.cloned.1.call-done = f32[96,3072]{1,0:T(8,128)} async-done(((f32[768,3072]{1,0:T(8,128)}), f32[96,3072]{1,0:T(8,128)}) %reduce-scatter.65.cloned.1.call-update) | async-done | bytes 1179664 | tf_op jit(solution)/shard_map/reduce_scatter | solution.py:457
  2766.3 38.4 %reduce-scatter.97.cloned.1.call-done = f32[96,4]{1,0:T(8,128)} async-done(((f32[768,4]{1,0:T(8,128)}), f32[96,4]{1,0:T(8,128)}) %reduce-scatter.97.cloned.1.call-update) | async-done | bytes 1552
  2805.6 62.6 %reduce-scatter.75.cloned.1.call-done = f32[96,4]{1,0:T(8,128)} async-done(((f32[768,4]{1,0:T(8,128)}), f32[96,4]{1,0:T(8,128)}) %reduce-scatter.75.cloned.1.call-update) | async-done | bytes 1552
  2869.1 62.8 %reduce-scatter.77.cloned.1.call-done = f32[96,4]{1,0:T(8,128)} async-done(((f32[768,4]{1,0:T(8,128)}), f32[96,4]{1,0:T(8,128)}) %reduce-scatter.77.cloned.1.call-update) | async-done | bytes 1552
  2932.8 62.7 %reduce-scatter.79.cloned.1.call-done = f32[96,4]{1,0:T(8,128)} async-done(((f32[768,4]{1,0:T(8,128)}), f32[96,4]{1,0:T(8,128)}) %reduce-scatter.79.cloned.1.call-update) | async-done | bytes 1552
  3006.7 52.5 %reduce-scatter.93.cloned.1.call-done = f32[96,5]{1,0:T(8,128)} async-done(((f32[768,5]{1,0:T(8,128)}), f32[96,5]{1,0:T(8,128)}) %reduce-scatter.93.cloned.1.call-update) | async-done | bytes 1936
  3060.0 66.5 %reduce-scatter.95.cloned.1.call-done = f32[384,2]{1,0:T(8,128)} async-done(((f32[3072,2]{1,0:T(8,128)}), f32[384,2]{1,0:T(8,128)}) %reduce-scatter.95.cloned.1.call-update) | async-done | bytes 3088
  3149.2 21.3 reduce-scatter.87.cloned.1.call-done
  3171.4 21.9 reduce-scatter.85.cloned.1.call-done
  3194.9 23.4 reduce-scatter.83.cloned.1.call-done
  3219.3 24.0 reduce-scatter.81.cloned.1.call-done
  3245.8 22.1 reduce-scatter.91.cloned.1.call-done
  3268.9 23.5 reduce-scatter.89.cloned.1.call-done
  3294.7 22.2 reduce-scatter.71.cloned.1.call-done
  3316.9 24.6 reduce-scatter.67.cloned.1.call-done
  (795 shorter events, 1134.1 us)
Async XLA Ops:
  7.2 25.3 all-gather.21.cloned.1.call-start
  9.3 42.2 %all-gather.25.cloned.1.call-start = ((), (), s32[]{:S(2)}) async-start(), calls=%async_computation.28 | async-start | bytes 1474560 | tf_op jit(solution)/shard_map/all_gather | solution.py:298
  10.0 380.5 %all-gather.17.cloned.1.call-start = ((), (), s32[]{:S(2)}) async-start(), calls=%async_computation.24 | async-start | bytes 3981312 | tf_op jit(solution)/shard_map/all_gather | solution.py:306
  21.2 588.0 %all-gather.19.cloned.1.call-start = ((), (), s32[]{:S(2)}) async-start(), calls=%async_computation.25 | async-start | bytes 2654208 | tf_op jit(solution)/shard_map/all_gather | solution.py:308
  32.3 633.0 %all-gather.23.cloned.1.call-start = ((), (), s32[]{:S(2)}) async-start(), calls=%async_computation.27 | async-start | bytes 10616832 | tf_op jit(solution)/shard_map/all_gather | solution.py:309
  37.3 644.1 %all-gather.27.cloned.1.call-start = ((), (), s32[]{:S(2)}) async-start(), calls=%async_computation.29 | async-start | bytes 10616832 | tf_op jit(solution)/shard_map/all_gather | solution.py:310
  51.5 689.0 %all-gather.29.cloned.1.call-start = ((), (), s32[]{:S(2)}) async-start(), calls=%async_computation.30 | async-start | bytes 3981312 | tf_op jit(solution)/shard_map/all_gather | solution.py:307
  60.3 1725.3 %reduce-scatter.73.cloned.1.call-start = ((), (), s32[]{:S(2)}) async-start(), calls=%async_computation.42 | async-start | bytes 442368
  126.2 199.2 %copy-start.186 = (s32[8]{0:T(128)S(1)}, s32[8]{0:T(128)}, u32[]{:S(2)}) copy-start(s32[8]{0:T(128)} %param.18) | copy-start | bytes 100
  126.2 199.2 %copy-start.187 = (s32[8]{0:T(128)S(1)}, s32[8]{0:T(128)}, u32[]{:S(2)}) copy-start(s32[8]{0:T(128)} %param.17) | copy-start | bytes 100
  176.9 183.2 %copy-start.100 = (f32[768]{0:T(1024)}, f32[768]{0:T(1024)S(1)}, u32[]{:S(2)}) copy-start(f32[768]{0:T(1024)S(1)} %get-tuple-element.179) | copy-start | bytes 9220
  176.9 183.2 %copy-start.102 = (f32[768]{0:T(1024)}, f32[768]{0:T(1024)S(1)}, u32[]{:S(2)}) copy-start(f32[768]{0:T(1024)S(1)} %get-tuple-element.180) | copy-start | bytes 9220
  176.9 183.2 %copy-start.104 = (f32[768]{0:T(1024)}, f32[768]{0:T(1024)S(1)}, u32[]{:S(2)}) copy-start(f32[768]{0:T(1024)S(1)} %get-tuple-element.181) | copy-start | bytes 9220
  176.9 183.2 %copy-start.106 = (f32[768]{0:T(1024)}, f32[768]{0:T(1024)S(1)}, u32[]{:S(2)}) copy-start(f32[768]{0:T(1024)S(1)} %get-tuple-element.182) | copy-start | bytes 9220
  176.9 183.2 %copy-start.108 = (f32[768]{0:T(1024)}, f32[768]{0:T(1024)S(1)}, u32[]{:S(2)}) copy-start(f32[768]{0:T(1024)S(1)} %get-tuple-element.183) | copy-start | bytes 9220
  1612.9 174.8 %reduce-scatter.59.cloned.1.call-start = ((), (), s32[]{:S(2)}) async-start(), calls=%async_computation.35 | async-start | bytes 2654208 | tf_op jit(solution)/shard_map/reduce_scatter | solution.py:454
  1618.4 194.9 %reduce-scatter.57.cloned.1.call-start = ((), (), s32[]{:S(2)}) async-start(), calls=%async_computation.34 | async-start | bytes 2654208 | tf_op jit(solution)/shard_map/reduce_scatter | solution.py:453
  1624.6 320.4 %reduce-scatter.55.cloned.1.call-start = ((), (), s32[]{:S(2)}) async-start(), calls=%async_computation.33 | async-start | bytes 7962624 | tf_op jit(solution)/shard_map/reduce_scatter | solution.py:452
  1670.8 406.2 %reduce-scatter.53.cloned.1.call-start = ((), (), s32[]{:S(2)}) async-start(), calls=%async_computation.32 | async-start | bytes 7962624 | tf_op jit(solution)/shard_map/reduce_scatter | solution.py:451
  1707.7 535.6 %reduce-scatter.63.cloned.1.call-start = ((), (), s32[]{:S(2)}) async-start(), calls=%async_computation.37 | async-start | bytes 10616832 | tf_op jit(solution)/shard_map/reduce_scatter | solution.py:456
  1722.9 686.4 %reduce-scatter.61.cloned.1.call-start = ((), (), s32[]{:S(2)}) async-start(), calls=%async_computation.36 | async-start | bytes 10616832 | tf_op jit(solution)/shard_map/reduce_scatter | solution.py:455
  1738.6 836.5 %reduce-scatter.69.cloned.1.call-start = ((), (), s32[]{:S(2)}) async-start(), calls=%async_computation.40 | async-start | bytes 10616832 | tf_op jit(solution)/shard_map/reduce_scatter | solution.py:458
  1754.0 987.1 %reduce-scatter.65.cloned.1.call-start = ((), (), s32[]{:S(2)}) async-start(), calls=%async_computation.38 | async-start | bytes 10616832 | tf_op jit(solution)/shard_map/reduce_scatter | solution.py:457
  1769.9 1034.8 %reduce-scatter.97.cloned.1.call-start = ((), (), s32[]{:S(2)}) async-start(), calls=%async_computation.54 | async-start | bytes 442368
  1779.2 1089.0 %reduce-scatter.75.cloned.1.call-start = ((), (), s32[]{:S(2)}) async-start(), calls=%async_computation.43 | async-start | bytes 442368
  1780.3 1151.6 %reduce-scatter.77.cloned.1.call-start = ((), (), s32[]{:S(2)}) async-start(), calls=%async_computation.44 | async-start | bytes 442368
  1781.5 1214.0 %reduce-scatter.79.cloned.1.call-start = ((), (), s32[]{:S(2)}) async-start(), calls=%async_computation.45 | async-start | bytes 442368
  1782.6 1276.6 %reduce-scatter.93.cloned.1.call-start = ((), (), s32[]{:S(2)}) async-start(), calls=%async_computation.52 | async-start | bytes 442368
  1783.7 1342.9 %reduce-scatter.95.cloned.1.call-start = ((), (), s32[]{:S(2)}) async-start(), calls=%async_computation.53 | async-start | bytes 1769472
  1785.5 1362.4 %reduce-scatter.51.cloned.1.call-start = ((), (), s32[]{:S(2)}) async-start(), calls=%async_computation.31 | async-start | bytes 20480 | tf_op jit(solution)/shard_map/reduce_scatter | solution.py:494
  1787.6 1382.9 %reduce-scatter.87.cloned.1.call-start = ((), (), s32[]{:S(2)}) async-start(), calls=%async_computation.49 | async-start | bytes 245760
  1789.5 1403.7 %reduce-scatter.85.cloned.1.call-start = ((), (), s32[]{:S(2)}) async-start(), calls=%async_computation.48 | async-start | bytes 245760
  1815.1 1403.2 %reduce-scatter.83.cloned.1.call-start = ((), (), s32[]{:S(2)}) async-start(), calls=%async_computation.47 | async-start | bytes 737280
  1947.3 464.5 %copy-start.194 = (u32[32]{0:T(128)S(1)}, u32[32]{0:T(128)}, u32[]{:S(2)}) copy-start(u32[32]{0:T(128)} %constant.215) | copy-start | bytes 388
  1947.3 1296.0 %reduce-scatter.81.cloned.1.call-start = ((), (), s32[]{:S(2)}) async-start(), calls=%async_computation.46 | async-start | bytes 737280
  2078.3 499.1 %copy-start.93 = (f32[768]{0:T(1024)S(1)}, f32[768]{0:T(1024)}, u32[]{:S(2)}) copy-start(f32[768]{0:T(1024)} %copy-done.92) | copy-start | bytes 9220
  2078.3 499.1 %copy-start.95 = (f32[768]{0:T(1024)S(1)}, f32[768]{0:T(1024)}, u32[]{:S(2)}) copy-start(f32[768]{0:T(1024)} %copy-done.94) | copy-start | bytes 9220
  2078.3 499.1 %copy-start.97 = (f32[768]{0:T(1024)S(1)}, f32[768]{0:T(1024)}, u32[]{:S(2)}) copy-start(f32[768]{0:T(1024)} %copy-done.96) | copy-start | bytes 9220
  2078.3 499.1 %copy-start.99 = (f32[768]{0:T(1024)S(1)}, f32[768]{0:T(1024)}, u32[]{:S(2)}) copy-start(f32[768]{0:T(1024)} %copy-done.98) | copy-start | bytes 9220
  2078.3 499.1 %copy-start.101 = (f32[768]{0:T(1024)S(1)}, f32[768]{0:T(1024)}, u32[]{:S(2)}) copy-start(f32[768]{0:T(1024)} %copy-done.100) | copy-start | bytes 9220
  2078.3 499.1 %copy-start.103 = (f32[768]{0:T(1024)S(1)}, f32[768]{0:T(1024)}, u32[]{:S(2)}) copy-start(f32[768]{0:T(1024)} %copy-done.102) | copy-start | bytes 9220
  2078.3 499.1 %copy-start.105 = (f32[768]{0:T(1024)S(1)}, f32[768]{0:T(1024)}, u32[]{:S(2)}) copy-start(f32[768]{0:T(1024)} %copy-done.104) | copy-start | bytes 9220
  2078.4 499.1 %copy-start.107 = (f32[768]{0:T(1024)S(1)}, f32[768]{0:T(1024)}, u32[]{:S(2)}) copy-start(f32[768]{0:T(1024)} %copy-done.106) | copy-start | bytes 9220
  2078.4 499.1 %copy-start.109 = (f32[768]{0:T(1024)S(1)}, f32[768]{0:T(1024)}, u32[]{:S(2)}) copy-start(f32[768]{0:T(1024)} %copy-done.108) | copy-start | bytes 9220
  2079.5 1188.4 %reduce-scatter.91.cloned.1.call-start = ((), (), s32[]{:S(2)}) async-start(), calls=%async_computation.51 | async-start | bytes 737280
  2245.7 1046.8 %reduce-scatter.89.cloned.1.call-start = ((), (), s32[]{:S(2)}) async-start(), calls=%async_computation.50 | async-start | bytes 737280
  2411.7 905.2 %reduce-scatter.71.cloned.1.call-start = ((), (), s32[]{:S(2)}) async-start(), calls=%async_computation.41 | async-start | bytes 737280 | tf_op jit(solution)/shard_map/reduce_scatter | solution.py:491
  2577.3 764.2 %reduce-scatter.67.cloned.1.call-start = ((), (), s32[]{:S(2)}) async-start(), calls=%async_computation.39 | async-start | bytes 737280 | tf_op jit(solution)/shard_map/reduce_scatter | solution.py:488
  (191 other events, 3946.2 us)
Sparse Core Ops, SparseCore 0:
  10.2 22.2 all-gather.20
  34.0 17.4 all-gather.24
  54.3 79.1 all-gather.16
  136.1 51.0 all-gather.18
  189.3 137.0 all-gather.22
  328.4 136.3 all-gather.26
  467.6 63.3 all-gather.28
  1613.0 57.2 reduce-scatter.72
  1673.8 68.0 reduce-scatter.58
  1745.2 67.9 reduce-scatter.56
  1817.0 128.0 reduce-scatter.54
  1949.0 128.0 reduce-scatter.52
  2080.7 162.5 reduce-scatter.62
  2246.7 162.5 reduce-scatter.60
  2412.7 162.3 reduce-scatter.68
  2578.6 162.3 reduce-scatter.64
  2744.2 60.4 reduce-scatter.96
  2807.8 60.3 reduce-scatter.74
  2871.5 60.3 reduce-scatter.76
  2935.0 60.3 reduce-scatter.78
  2998.7 60.3 reduce-scatter.92
  3062.6 63.9 reduce-scatter.94
  3129.7 18.1 reduce-scatter.50
  3150.8 19.7 reduce-scatter.86
  3173.5 19.7 reduce-scatter.84
  3196.2 22.0 reduce-scatter.82
  3221.2 22.0 reduce-scatter.80
  3245.8 22.0 reduce-scatter.90
  3270.4 22.0 reduce-scatter.88
  3294.8 22.0 reduce-scatter.70
  3319.4 22.0 reduce-scatter.66
where the time goes:
time: 3370 us; the launch traced here: 3350 us
  waiting for transfers between devices  1470 us (44%)
  local copies, waits for them, and re-layouts  695 us (21%)
  other arithmetic  569 us (17%)
  matrix products  379 us (11%)
  blocking collectives  220 us (7%)
    unnamed x44, waiting for transfers between devices  483 us
    reduce_scatter x1, waiting for transfers between devices, local(): lax.psum_scatter(moved[5], 'wide', scatter_dimension=0, tiled=True)  164 us
    reduce_scatter x1, waiting for transfers between devices, local(): lax.psum_scatter(moved[4], 'wide', scatter_dimension=0, tiled=True)  164 us
    reduce_scatter x1, waiting for transfers between devices, local(): lax.psum_scatter(moved[7], 'wide', scatter_dimension=0, tiled=True)  163 us
    reduce_scatter x1, waiting for transfers between devices, local(): lax.psum_scatter(moved[6], 'wide', scatter_dimension=0, tiled=True)  136 us
    reduce_scatter x1, waiting for transfers between devices, local(): lax.psum_scatter(moved[1], 'wide', scatter_dimension=0, tiled=True)  130 us
    reduce_scatter x1, waiting for transfers between devices, local(): lax.psum_scatter(moved[0], 'wide', scatter_dimension=0, tiled=True)  130 us
    slice x2, local copies, waits for them, and re-layouts, depthwise(): kernel[3 * row_step + col_step]  108 us
  transfers between devices with their start and end apart: 31, of which 24 were waited for; matrix products, arithmetic and copies ran while one was open for 23% of the time, Pallas kernels for 0%

commit v1 on v0

v1 whole, which is shorter than its diff:
```python
import functools

import jax
import jax.numpy as jnp
from jax import lax
from jax.experimental import pallas as pl
from jax.experimental.pallas import tpu as pltpu
from jax.sharding import PartitionSpec as P

HD = 32
WIN = 7
LANES = 128
SUB = 8
GROUP = 256
WTOK = WIN * SUB
FFC = 512
SCALE = HD ** (-0.5)
EPS = 1e-05
NEG = -1e30
F32 = jnp.float32
BF16 = jnp.bfloat16
VMEM_LIMIT = 60 * 1024 * 1024
DIMS_NN = (((1,), (0,)), ((), ()))
DIMS_NT = (((1,), (1,)), ((), ()))
DIMS_TN = (((0,), (0,)), ((), ()))


def dot(a, b, dims):
    return lax.dot_general(a, b, dims, preferred_element_type=F32)


def tok(r, half):
    return ((r // WIN) * 2 + half) * WTOK + (r % WIN) * SUB


def load_cells(src, dst):
    for r in range(2 * WIN):
        row = src[0, r].astype(F32)
        dst[pl.ds(tok(r, 0), WIN), :] = row[:WIN]
        dst[pl.ds(tok(r, 1), WIN), :] = row[WIN:]


def store_cells(value_at, dst, stage):
    for r in range(2 * WIN):
        stage[pl.ds(0, SUB), :] = value_at(tok(r, 0))
        stage[pl.ds(WIN, SUB), :] = value_at(tok(r, 1))
        dst[0, r] = stage[pl.ds(0, 2 * WIN), :].astype(BF16)


def neighbours(left, right):
    last = lax.broadcasted_iota(jnp.int32, (SUB, LANES), 0) == SUB - 1
    up_right = pltpu.roll(right, SUB - 1, 0)
    up_left = pltpu.roll(jnp.where(last, up_right, left), SUB - 1, 0)
    down_left = pltpu.roll(left, 1, 0)
    down_right = pltpu.roll(jnp.where(last, down_left, right), 1, 0)
    return ((down_left, left, up_left), (down_right, right, up_right))


def masked_row(src, mask, r, lanes):
    pair = []
    for half in range(2):
        rows = pl.ds(tok(r, half), SUB)
        pair.append(src[rows, lanes] * mask[0, rows, :])
    return neighbours(*pair)


def plain_row(src, r, lanes):
    return neighbours(*[src[pl.ds(tok(r, half), SUB), lanes] for half in range(2)])


def taps(weight, lanes):
    return [jnp.broadcast_to(weight[pl.ds(k, 1), lanes], (SUB, LANES)) for k in range(9)]


def conv_forward(src, mask, weight, bias, dst):
    rows = 2 * WIN

    @pl.loop(0, src.shape[1] // LANES)
    def _(j):
        lanes = pl.ds(pl.multiple_of(j * LANES, LANES), LANES)
        w = taps(weight, lanes)
        shift = jnp.broadcast_to(bias[:, lanes], (SUB, LANES))
        window = [None, masked_row(src, mask, 0, lanes), masked_row(src, mask, 1, lanes)]
        for r in range(rows):
            for half in range(2):
                total = shift
                for a in range(3):
                    if window[a] is None:
                        continue
                    for b in range(3):
                        total = total + w[3 * a + b] * window[a][half][b]
                at = pl.ds(tok(r, half), SUB)
                dst[at, lanes] = src[at, lanes] + total
            following = masked_row(src, mask, r + 2, lanes) if r + 2 < rows else None
            window = [window[1], window[2], following]


def conv_backward(x_src, g_src, mask, weight, sums, dst):
    rows = 2 * WIN

    @pl.loop(0, x_src.shape[1] // LANES)
    def _(j):
        lanes = pl.ds(pl.multiple_of(j * LANES, LANES), LANES)
        w = taps(weight, lanes)
        g_win = [None, plain_row(g_src, 0, lanes), plain_row(g_src, 1, lanes)]
        x_win = [None, masked_row(x_src, mask, 0, lanes), masked_row(x_src, mask, 1, lanes)]
        grads = [sums[pl.ds(SUB * k, SUB), lanes] for k in range(10)]
        for r in range(rows):
            for half in range(2):
                center = g_win[1][half][1]
                total = None
                for a in range(3):
                    for b in range(3):
                        if x_win[a] is not None:
                            grads[3 * a + b] = grads[3 * a + b] + center * x_win[a][half][b]
                        if g_win[2 - a] is not None:
                            term = w[3 * a + b] * g_win[2 - a][half][2 - b]
                            total = term if total is None else total + term
                grads[9] = grads[9] + center
                at = pl.ds(tok(r, half), SUB)
                dst[at, lanes] = center + mask[0, at, :] * total
            more = r + 2 < rows
            g_win = [g_win[1], g_win[2], plain_row(g_src, r + 2, lanes) if more else None]
            x_win = [x_win[1], x_win[2], masked_row(x_src, mask, r + 2, lanes) if more else None]
        for k in range(10):
            sums[pl.ds(SUB * k, SUB), lanes] = grads[k]


def norm_forward(src, gain, bias, z_out, r_out, n_out):
    features = src.shape[1]

    @pl.loop(0, src.shape[0] // 16)
    def _(i):
        rows = pl.ds(pl.multiple_of(i * 16, 16), 16)
        x = src[rows, :]
        center = x - jnp.sum(x, axis=1, keepdims=True) * (1.0 / features)
        var = jnp.sum(center * center, axis=1, keepdims=True) * (1.0 / features)
        rstd = lax.rsqrt(var + EPS)
        z = center * rstd
        z_out[rows, :] = z
        r_out[rows, :] = jnp.broadcast_to(rstd, (16, LANES))
        n_out[rows, :] = (z * gain[...] + bias[...]).astype(BF16)


def norm_backward(dn, z_src, r_src, gain, g_src, sums, first, dst):
    features = dn.shape[1]
    gain_sum = sums[pl.ds(first, SUB), :]
    bias_sum = sums[pl.ds(first + SUB, SUB), :]

    def step(i, carry):
        gain_sum, bias_sum = carry
        rows = pl.ds(pl.multiple_of(i * SUB, SUB), SUB)
        d = dn[rows, :]
        z = z_src[rows, :]
        t = d * gain[...]
        m1 = jnp.sum(t, axis=1, keepdims=True) * (1.0 / features)
        m2 = jnp.sum(t * z, axis=1, keepdims=True) * (1.0 / features)
        dst[rows, :] = g_src[rows, :] + (t - m1 - z * m2) * r_src[rows, 0:1]
        return (gain_sum + d * z, bias_sum + d)

    gain_sum, bias_sum = lax.fori_loop(0, dn.shape[0] // SUB, step, (gain_sum, bias_sum))
    sums[pl.ds(first, SUB), :] = gain_sum
    sums[pl.ds(first + SUB, SUB), :] = bias_sum


def fold_rows(value):
    total = value[:SUB]
    for i in range(1, value.shape[0] // SUB):
        total = total + value[SUB * i : SUB * (i + 1)]
    return total


def finish_sums(sums, out):
    for k in range(sums.shape[0] // SUB):
        out[pl.ds(k, 1), :] = jnp.sum(sums[pl.ds(SUB * k, SUB), :], axis=0, keepdims=True)


def head_masks():
    lane = lax.broadcasted_iota(jnp.int32, (WTOK, GROUP), 1) // HD
    return [lane == h for h in range(GROUP // HD)]


def spread_heads(value, masks):
    return jnp.concatenate([jnp.where(m, value, 0.0) for m in masks], axis=0).astype(BF16)


def collect_heads(full, masks):
    total = full[:WTOK]
    for h in range(1, len(masks)):
        total = jnp.where(masks[h], full[WTOK * h : WTOK * (h + 1)], total)
    return total


def rounded(value):
    return value.astype(BF16).astype(F32)


def gelu_pair(h):
    cdf = 0.5 * (1.0 + lax.erf(h * 0.7071067811865476))
    pdf = jnp.exp(h * h * -0.5) * 0.3989422804014327
    return h * cdf, cdf + h * pdf


def first_step():
    return pl.program_id(0) == 0


def last_step():
    return pl.program_id(0) == pl.num_programs(0) - 1


def window_forward_kernel(
    inp, mask, conv_w, conv_b, gain, bias, wq, qb, wp, ob,
    n_out, z_out, r_out, q_out, o_out, p_out, x_out,
    x0, x1, qf, of,
):
    features = x0.shape[1]

    @pl.when(first_step())
    def _():
        x0[...] = jnp.zeros_like(x0)

    load_cells(inp, x0)
    conv_forward(x0, mask, conv_w, conv_b, x1)
    norm_forward(x1, gain, bias, z_out.at[0], r_out.at[0], n_out.at[0])
    chunk = features
    for c in range(3):
        lanes = pl.ds(c * chunk, chunk)
        part = (dot(n_out[0], wq[:, lanes], DIMS_NN) + qb[:, lanes]).astype(BF16)
        q_out[0, :, lanes] = part
        qf[:, lanes] = part.astype(F32)

    @pl.loop(0, 4)
    def _(w):
        rows = pl.ds(pl.multiple_of(w * WTOK, SUB), WTOK)
        valid = mask[0, rows, 0:1] > 0.0
        masks = head_masks()
        for g in range(features // GROUP):
            q = qf[rows, pl.ds(g * GROUP, GROUP)]
            k = qf[rows, pl.ds(features + g * GROUP, GROUP)].astype(BF16)
            v = qf[rows, pl.ds(2 * features + g * GROUP, GROUP)].astype(BF16)
            s = dot(k, spread_heads(q, masks), DIMS_NT) * SCALE
            s = jnp.where(valid, s, NEG)
            e = jnp.exp(s - jnp.max(s, axis=0, keepdims=True))
            p = (e / jnp.sum(e, axis=0, keepdims=True)).astype(BF16)
            p_out[0, w, g] = p
            of[rows, pl.ds(g * GROUP, GROUP)] = collect_heads(dot(p, v, DIMS_TN), masks)

    o_out[0] = of[...].astype(BF16)
    x_out[0] = x1[...] + (dot(o_out[0], wp[...], DIMS_NN) + ob[...])


def mlp_forward_kernel(
    x_in, mask, conv_w, conv_b, gain, bias, w_in, hb, w_out, ob,
    n_out, z_out, r_out, u_out, d_out, x_out,
    x1, acc,
):
    conv_forward(x_in.at[0], mask, conv_w, conv_b, x1)
    norm_forward(x1, gain, bias, z_out.at[0], r_out.at[0], n_out.at[0])
    for c in range(w_in.shape[1] // FFC):
        lanes = pl.ds(c * FFC, FFC)
        h = dot(n_out[0], w_in[:, lanes], DIMS_NN) + hb[:, lanes]
        u, d = gelu_pair(h)
        u = u.astype(BF16)
        u_out[0, :, lanes] = u
        d_out[0, :, lanes] = d.astype(BF16)
        y = dot(u, w_out[:, lanes], DIMS_NT)
        acc[...] = y if c == 0 else acc[...] + y
    x_out[0] = x1[...] + (acc[...] + ob[...])


def group_mask():
    row = lax.broadcasted_iota(jnp.int32, (GROUP, GROUP), 0) // HD
    col = lax.broadcasted_iota(jnp.int32, (GROUP, GROUP), 1) // HD
    return row == col


def channel_forward_kernel(
    x_in, mask, conv_w, conv_b, gain, bias, wq, qb, wp, ob,
    n_out, z_out, r_out, q_out, o_out, a_out, x_out,
    x1,
):
    features = x1.shape[1]
    conv_forward(x_in.at[0], mask, conv_w, conv_b, x1)
    norm_forward(x1, gain, bias, z_out.at[0], r_out.at[0], n_out.at[0])
    for c in range(3):
        lanes = pl.ds(c * features, features)
        part = dot(n_out[0], wq[:, lanes], DIMS_NN) + qb[:, lanes]
        if c == 1:
            part = part * mask[0, :, 0:1]
        q_out[0, :, lanes] = part.astype(BF16)
    same = group_mask()
    for g in range(features // GROUP):
        q = q_out[0, :, pl.ds(g * GROUP, GROUP)]
        k = q_out[0, :, pl.ds(features + g * GROUP, GROUP)]
        v = q_out[0, :, pl.ds(2 * features + g * GROUP, GROUP)]
        s = jnp.where(same, dot(k, q, DIMS_TN) * SCALE, -jnp.inf)
        e = jnp.exp(s - jnp.max(s, axis=0, keepdims=True))
        a = (e / jnp.sum(e, axis=0, keepdims=True)).astype(BF16)
        a_out[0, g] = a
        o_out[0, :, pl.ds(g * GROUP, GROUP)] = dot(v, a, DIMS_NN).astype(BF16)
    x_out[0] = x1[...] + (dot(o_out[0], wp[...], DIMS_NN) + ob[...])


def last_mlp_kernel(
    x_in, cot, mask, conv_w, conv_b, gain, bias, w_in, hb, w_out, ob,
    out, g_out, n_out, u_out, gy_out, gh_out, small_out, hidden_out,
    x1, z, r, acc, dn, g8, stage, sums, hsums,
):
    @pl.when(first_step())
    def _():
        g8[...] = jnp.zeros_like(g8)
        sums[...] = jnp.zeros_like(sums)
        hsums[...] = jnp.zeros_like(hsums)

    x6 = x_in.at[0]
    load_cells(cot, g8)
    conv_forward(x6, mask, conv_w, conv_b, x1)
    norm_forward(x1, gain, bias, z, r, n_out.at[0])
    g8[...] = g8[...] * mask[0, :, 0:1]
    gy_out[0] = g8[...].astype(BF16)
    sums[pl.ds(12 * SUB, SUB), :] = sums[pl.ds(12 * SUB, SUB), :] + fold_rows(gy_out[0].astype(F32))
    for c in range(w_in.shape[1] // FFC):
        lanes = pl.ds(c * FFC, FFC)
        h = dot(n_out[0], w_in[:, lanes], DIMS_NN) + hb[:, lanes]
        du = dot(gy_out[0], w_out[:, lanes], DIMS_NN)
        u, d = gelu_pair(h)
        u = u.astype(BF16)
        u_out[0, :, lanes] = u
        gh = (du * d).astype(BF16)
        gh_out[0, :, lanes] = gh
        hsums[:, lanes] = hsums[:, lanes] + fold_rows(gh.astype(F32))
        y = dot(u, w_out[:, lanes], DIMS_NT)
        dx = dot(gh, w_in[:, lanes], DIMS_NT)
        acc[...] = y if c == 0 else acc[...] + y
        dn[...] = dx if c == 0 else dn[...] + dx
    acc[...] = (x1[...] + (acc[...] + ob[...])) * mask[0, :, 0:1]
    store_cells(lambda at: acc[pl.ds(at, SUB), :], out, stage)
    norm_backward(dn, z, r, gain, g8, sums, 10 * SUB, x1)
    conv_backward(x6, x1, mask, conv_w, sums, g_out.at[0])

    @pl.when(last_step())
    def _():
        finish_sums(sums, small_out)
        finish_sums(hsums, hidden_out)


def mlp_backward_kernel(
    g_in, x_in, z_in, r_in, d_in, mask, conv_w, gain, w_in, w_out,
    g_out, gy_out, gh_out, small_out, hidden_out,
    dn, g1, sums, hsums,
):
    @pl.when(first_step())
    def _():
        sums[...] = jnp.zeros_like(sums)
        hsums[...] = jnp.zeros_like(hsums)

    gy_out[0] = g_in[0].astype(BF16)
    sums[pl.ds(12 * SUB, SUB), :] = sums[pl.ds(12 * SUB, SUB), :] + fold_rows(gy_out[0].astype(F32))
    for c in range(w_in.shape[1] // FFC):
        lanes = pl.ds(c * FFC, FFC)
        du = dot(gy_out[0], w_out[:, lanes], DIMS_NN)
        gh = (du * d_in[0, :, lanes].astype(F32)).astype(BF16)
        gh_out[0, :, lanes] = gh
        hsums[:, lanes] = hsums[:, lanes] + fold_rows(gh.astype(F32))
        dx = dot(gh, w_in[:, lanes], DIMS_NT)
        dn[...] = dx if c == 0 else dn[...] + dx
    norm_backward(dn, z_in.at[0], r_in.at[0], gain, g_in.at[0], sums, 10 * SUB, g1)
    conv_backward(x_in.at[0], g1, mask, conv_w, sums, g_out.at[0])

    @pl.when(last_step())
    def _():
        finish_sums(sums, small_out)
        finish_sums(hsums, hidden_out)


def channel_backward_kernel(
    g_in, x_in, z_in, r_in, q_in, a_in, mask, conv_w, gain, wq, wp,
    g_out, ga_out, dq_out, small_out, bias_out,
    dn, g1, sums, bsums,
):
    features = dn.shape[1]

    @pl.when(first_step())
    def _():
        sums[...] = jnp.zeros_like(sums)
        bsums[...] = jnp.zeros_like(bsums)

    ga_out[0] = g_in[0].astype(BF16)
    sums[pl.ds(12 * SUB, SUB), :] = sums[pl.ds(12 * SUB, SUB), :] + fold_rows(ga_out[0].astype(F32))
    go = dot(ga_out[0], wp[...], DIMS_NT).astype(BF16)
    for g in range(features // GROUP):
        at = [pl.ds(i * features + g * GROUP, GROUP) for i in range(3)]
        q, k, v = (q_in[0, :, lanes] for lanes in at)
        gog = go[:, g * GROUP : (g + 1) * GROUP]
        a = a_in[0, g]
        af = a.astype(F32)
        dp = dot(v, gog, DIMS_TN)
        ds = (af * (dp - jnp.sum(dp * af, axis=0, keepdims=True))).astype(BF16)
        dq_out[0, :, at[0]] = (dot(k, ds, DIMS_NN) * SCALE).astype(BF16)
        dq_out[0, :, at[1]] = (dot(q, ds, DIMS_NT) * SCALE * mask[0, :, 0:1]).astype(BF16)
        dq_out[0, :, at[2]] = dot(gog, a, DIMS_NT).astype(BF16)
    bsums[...] = bsums[...] + fold_rows(dq_out[0].astype(F32))
    dn[...] = dot(dq_out[0], wq[...], DIMS_NT)
    norm_backward(dn, z_in.at[0], r_in.at[0], gain, g_in.at[0], sums, 10 * SUB, g1)
    conv_backward(x_in.at[0], g1, mask, conv_w, sums, g_out.at[0])

    @pl.when(last_step())
    def _():
        finish_sums(sums, small_out)
        finish_sums(bsums, bias_out)


def window_backward_kernel(
    g_in, inp, z_in, r_in, q_in, p_in, mask, conv_w, gain, wq, wp,
    g_out, ga_out, dq_out, small_out, bias_out,
    x0, qf, gof, dqf, dn, g1, stage, sums, bsums,
):
    features = dn.shape[1]

    @pl.when(first_step())
    def _():
        x0[...] = jnp.zeros_like(x0)
        sums[...] = jnp.zeros_like(sums)
        bsums[...] = jnp.zeros_like(bsums)

    load_cells(inp, x0)
    ga_out[0] = g_in[0].astype(BF16)
    sums[pl.ds(12 * SUB, SUB), :] = sums[pl.ds(12 * SUB, SUB), :] + fold_rows(ga_out[0].astype(F32))
    gof[...] = rounded(dot(ga_out[0], wp[...], DIMS_NT))
    qf[...] = q_in[0].astype(F32)

    @pl.loop(0, 4)
    def _(w):
        rows = pl.ds(pl.multiple_of(w * WTOK, SUB), WTOK)
        masks = head_masks()
        for g in range(features // GROUP):
            at = [pl.ds(i * features + g * GROUP, GROUP) for i in range(3)]
            qe = spread_heads(qf[rows, at[0]], masks)
            k = qf[rows, at[1]].astype(BF16)
            v = qf[rows, at[2]].astype(BF16)
            goe = spread_heads(gof[rows, at[0]], masks)
            p = p_in[0, w, g]
            pf = p.astype(F32)
            dp = dot(v, goe, DIMS_NT)
            ds = (pf * (dp - jnp.sum(dp * pf, axis=0, keepdims=True))).astype(BF16)
            dqf[rows, at[0]] = collect_heads(dot(ds, k, DIMS_TN), masks) * SCALE
            dqf[rows, at[1]] = dot(ds, qe, DIMS_NN) * SCALE
            dqf[rows, at[2]] = dot(p, goe, DIMS_NN)

    dq_out[0] = dqf[...].astype(BF16)
    bsums[...] = bsums[...] + fold_rows(dq_out[0].astype(F32))
    dn[...] = dot(dq_out[0], wq[...], DIMS_NT)
    norm_backward(dn, z_in.at[0], r_in.at[0], gain, g_in.at[0], sums, 10 * SUB, g1)
    conv_backward(x0, g1, mask, conv_w, sums, dn)
    store_cells(lambda at: dn[pl.ds(at, SUB), :], g_out, stage)

    @pl.when(last_step())
    def _():
        finish_sums(sums, small_out)
        finish_sums(bsums, bias_out)


def per_image(shape):
    rest = (0,) * (len(shape) - 1)
    return pl.BlockSpec((1,) + tuple(shape[1:]), lambda i: (i,) + rest)


def whole(shape):
    zeros = (0,) * len(shape)
    return pl.BlockSpec(tuple(shape), lambda i: zeros, pipeline_mode=pl.Buffered(1))


def image_call(kernel, name, images, args, outs, scratch, flops):
    ins = [per_image(a.shape) if batched else whole(a.shape) for a, batched in args]
    out_specs = [
        per_image(s) if batched else pl.BlockSpec(tuple(s), lambda i, n=len(s): (0,) * n)
        for s, _, batched in outs
    ]
    size = sum(a.size * a.dtype.itemsize for a, _ in args)
    size += sum(jnp.dtype(d).itemsize * functools.reduce(lambda p, q: p * q, s) for s, d, _ in outs)
    return pl.pallas_call(
        kernel,
        grid=(images,),
        in_specs=ins,
        out_specs=out_specs,
        out_shape=[jax.ShapeDtypeStruct(s, d) for s, d, _ in outs],
        scratch_shapes=[pltpu.VMEM(s, d) for s, d in scratch],
        compiler_params=pltpu.CompilerParams(
            dimension_semantics=("arbitrary",), vmem_limit_bytes=VMEM_LIMIT
        ),
        cost_estimate=pl.CostEstimate(flops=int(flops), bytes_accessed=int(size), transcendentals=0),
        name=name,
    )(*[a for a, _ in args])


def token_mask(heights, widths):
    t = jnp.arange(4 * WTOK, dtype=jnp.int32)
    window = t // WTOK
    row = (window // 2) * WIN + (t % WTOK) // SUB
    col8 = t % SUB
    col = (window % 2) * WIN + col8
    valid = (row[None] < heights[:, None]) & (col[None] < widths[:, None]) & (col8 < WIN)[None]
    return jnp.broadcast_to(valid.astype(F32)[..., None], valid.shape + (LANES,))


def forward_window(inputs, mask, conv_w, conv_b, gain, bias, wq, qb, wp, ob):
    images, _, _, c = inputs.shape
    t = 4 * WTOK
    rows = images * t
    args = [(inputs, 1), (mask, 1)] + [(a, 0) for a in (conv_w, conv_b, gain, bias, wq, qb, wp, ob)]
    outs = [
        ((images, t, c), BF16, 1), ((images, t, c), F32, 1), ((images, t, LANES), F32, 1),
        ((images, t, 3 * c), BF16, 1), ((images, t, c), BF16, 1),
        ((images, 4, c // GROUP, WTOK, WTOK * GROUP // HD), BF16, 1), ((images, t, c), F32, 1),
    ]
    scratch = [((t, c), F32), ((t, c), F32), ((t, 3 * c), F32), ((t, c), F32)]
    return image_call(window_forward_kernel, "window_forward", images, args, outs, scratch, 10 * rows * c * c)


def forward_mlp(x, mask, conv_w, conv_b, gain, bias, w_in, hb, w_out, ob):
    images, t, c = x.shape
    ff = w_in.shape[1]
    args = [(x, 1), (mask, 1)] + [(a, 0) for a in (conv_w, conv_b, gain, bias, w_in, hb, w_out, ob)]
    outs = [
        ((images, t, c), BF16, 1), ((images, t, c), F32, 1), ((images, t, LANES), F32, 1),
        ((images, t, ff), BF16, 1), ((images, t, ff), BF16, 1), ((images, t, c), F32, 1),
    ]
    scratch = [((t, c), F32), ((t, c), F32)]
    return image_call(mlp_forward_kernel, "mlp_forward", images, args, outs, scratch, 4 * images * t * c * ff)


def forward_channel(x, mask, conv_w, conv_b, gain, bias, wq, qb, wp, ob):
    images, t, c = x.shape
    args = [(x, 1), (mask, 1)] + [(a, 0) for a in (conv_w, conv_b, gain, bias, wq, qb, wp, ob)]
    outs = [
        ((images, t, c), BF16, 1), ((images, t, c), F32, 1), ((images, t, LANES), F32, 1),
        ((images, t, 3 * c), BF16, 1), ((images, t, c), BF16, 1),
        ((images, c // GROUP, GROUP, GROUP), BF16, 1), ((images, t, c), F32, 1),
    ]
    return image_call(channel_forward_kernel, "channel_forward", images, args, outs, [((t, c), F32)], 9 * images * t * c * c)


def last_mlp(x, cot, mask, conv_w, conv_b, gain, bias, w_in, hb, w_out, ob):
    images, t, c = x.shape
    ff = w_in.shape[1]
    args = [(x, 1), (cot, 1), (mask, 1)] + [(a, 0) for a in (conv_w, conv_b, gain, bias, w_in, hb, w_out, ob)]
    outs = [
        (cot.shape, BF16, 1), ((images, t, c), F32, 1), ((images, t, c), BF16, 1), ((images, t, ff), BF16, 1),
        ((images, t, c), BF16, 1), ((images, t, ff), BF16, 1), ((13, c), F32, 0), ((1, ff), F32, 0),
    ]
    scratch = [
        ((t, c), F32), ((t, c), F32), ((t, LANES), F32), ((t, c), F32), ((t, c), F32), ((t, c), F32),
        ((16, c), F32), ((13 * SUB, c), F32), ((SUB, ff), F32),
    ]
    return image_call(last_mlp_kernel, "last_mlp", images, args, outs, scratch, 8 * images * t * c * ff)


def backward_mlp(g, x, z, r, d, mask, conv_w, gain, w_in, w_out):
    images, t, c = x.shape
    ff = w_in.shape[1]
    args = [(g, 1), (x, 1), (z, 1), (r, 1), (d, 1), (mask, 1)] + [(a, 0) for a in (conv_w, gain, w_in, w_out)]
    outs = [
        ((images, t, c), F32, 1), ((images, t, c), BF16, 1), ((images, t, ff), BF16, 1),
        ((13, c), F32, 0), ((1, ff), F32, 0),
    ]
    scratch = [((t, c), F32), ((t, c), F32), ((13 * SUB, c), F32), ((SUB, ff), F32)]
    return image_call(mlp_backward_kernel, "mlp_backward", images, args, outs, scratch, 4 * images * t * c * ff)


def backward_channel(g, x, z, r, q, a, mask, conv_w, gain, wq, wp):
    images, t, c = x.shape
    args = [(v, 1) for v in (g, x, z, r, q, a, mask)] + [(v, 0) for v in (conv_w, gain, wq, wp)]
    outs = [
        ((images, t, c), F32, 1), ((images, t, c), BF16, 1), ((images, t, 3 * c), BF16, 1),
        ((13, c), F32, 0), ((1, 3 * c), F32, 0),
    ]
    scratch = [((t, c), F32), ((t, c), F32), ((13 * SUB, c), F32), ((SUB, 3 * c), F32)]
    return image_call(channel_backward_kernel, "channel_backward", images, args, outs, scratch, 10 * images * t * c * c)


def backward_window(g, inputs, z, r, q, p, mask, conv_w, gain, wq, wp):
    images, t, c = g.shape
    args = [(v, 1) for v in (g, inputs, z, r, q, p, mask)] + [(v, 0) for v in (conv_w, gain, wq, wp)]
    outs = [
        (inputs.shape, BF16, 1), ((images, t, c), BF16, 1), ((images, t, 3 * c), BF16, 1),
        ((13, c), F32, 0), ((1, 3 * c), F32, 0),
    ]
    scratch = [
        ((t, c), F32), ((t, 3 * c), F32), ((t, c), F32), ((t, 3 * c), F32), ((t, c), F32), ((t, c), F32),
        ((16, c), F32), ((13 * SUB, c), F32), ((SUB, 3 * c), F32),
    ]
    return image_call(window_backward_kernel, "window_backward", images, args, outs, scratch, 12 * images * t * c * c)


def weight_grad(left, right):
    rows = left.shape[0] * left.shape[1]
    return dot(left.reshape(rows, -1), right.reshape(rows, -1), DIMS_TN)


BOTH = ("narrow", "wide")


def spread(pieces):
    return lax.all_gather(pieces, BOTH, axis=0, tiled=False)


def pack_small(conv_weight, conv_bias, norm_gain, norm_bias, out_bias, attn_bias, hidden_bias, lanes):
    width = conv_bias.shape[1]
    rows = [conv_weight, conv_bias, norm_gain, norm_bias, out_bias, attn_bias, hidden_bias]
    flat = jnp.concatenate([item.reshape(-1, width) for item in rows])
    return pad_rows(flat, lanes)


def pad_rows(flat, lanes):
    per_row = lanes // flat.shape[-1]
    height = -(-flat.shape[-2] // (16 * per_row)) * 16
    pad = [(0, 0)] * (flat.ndim - 2) + [(0, height * per_row - flat.shape[-2]), (0, 0)]
    return jnp.pad(flat, pad).reshape(flat.shape[:-2] + (height, lanes))


def local(wide, narrow, inputs, heights, widths, conv_weight, conv_bias, norm_gain, norm_bias, spatial_qkv,
          channel_qkv, projection, mlp_in, mlp_out, attn_bias, hidden_bias, out_bias, cotangent):
    c = inputs.shape[-1]
    ff = hidden_bias.shape[1] * wide
    layers = 4 // narrow
    cw, fw, cn = c // wide, ff // wide, c // narrow
    halves = wide // narrow

    def attention_piece(qkv, proj):
        return jnp.concatenate([qkv.T, proj.T], axis=1)

    def mlp_piece(first, second):
        second = second.reshape(cw, halves, fw).transpose(1, 0, 2).reshape(cn, fw)
        return jnp.concatenate([first.T, second], axis=0)

    def attention_full(got):
        got = got.reshape(narrow, wide, cn, 4 * cw).transpose(0, 2, 1, 3)
        wq = got[..., : 3 * cw].reshape(c, 3 * c)
        wp = got[..., 3 * cw :].reshape(c, c)
        return wq, wp

    def mlp_full(got):
        got = got.reshape(narrow, wide, 2, cn, fw)
        w_in = got[:, :, 0].transpose(0, 2, 1, 3).reshape(c, ff)
        w_out = got[:, :, 1].reshape(narrow, wide, halves, cw, fw).transpose(1, 3, 0, 2, 4).reshape(c, ff)
        return w_in, w_out

    small = pack_small(conv_weight, conv_bias, norm_gain, norm_bias, out_bias, attn_bias, hidden_bias, 4 * cw)
    first = spread(jnp.concatenate([small, attention_piece(spatial_qkv, projection[0])]))
    mlp0 = spread(mlp_piece(mlp_in[0], mlp_out[0]))
    chan = spread(attention_piece(channel_qkv, projection[1]))
    mlp1 = spread(mlp_piece(mlp_in[1], mlp_out[1]))

    srows = small.shape[0]
    sm = first[:, :srows].reshape(narrow, wide, -1, cw)
    count = 13 * layers
    by_layer = sm[:, :, :count].astype(F32)
    shared = sm[0, :, count : count + 5 + 2 * fw // cw].astype(F32)

    def layer_rows(start, size):
        part = by_layer[:, :, start * layers : (start + size) * layers]
        return part.reshape(narrow, wide, layers, size, cw).transpose(0, 2, 3, 1, 4).reshape(4, size, c)

    kernels = layer_rows(0, 9)
    shifts, gains, norm_shifts, out_shifts = (layer_rows(k, 1) for k in range(9, 13))
    attn = shared[:, :5].transpose(1, 0, 2).reshape(5, c)
    hidden = shared[:, 5:].reshape(wide, 2, fw).transpose(1, 0, 2).reshape(2, 1, ff)
    qb0 = jnp.concatenate([attn[0], jnp.zeros_like(attn[0]), attn[1]])[None]
    qb1 = attn[2:5].reshape(1, 3 * c)

    wq0, wp0 = attention_full(first[:, srows:])
    win0, wout0 = mlp_full(mlp0)
    wq1, wp1 = attention_full(chan)
    win1, wout1 = mlp_full(mlp1)

    mask = token_mask(heights, widths)
    n1, z1, r1, q1, o1, p1, x2 = forward_window(
        inputs, mask, kernels[0], shifts[0], gains[0], norm_shifts[0], wq0, qb0, wp0, out_shifts[0])
    n2, z2, r2, u1, d1, x4 = forward_mlp(
        x2, mask, kernels[1], shifts[1], gains[1], norm_shifts[1], win0, hidden[0], wout0, out_shifts[1])
    n3, z3, r3, q3, o3, a3, x6 = forward_channel(
        x4, mask, kernels[2], shifts[2], gains[2], norm_shifts[2], wq1, qb1, wp1, out_shifts[2])
    out, g6, n4, u2, gy2, gh2, small3, hid1 = last_mlp(
        x6, cotangent, mask, kernels[3], shifts[3], gains[3], norm_shifts[3], win1, hidden[1], wout1, out_shifts[3])

    def mlp_pack(n, gh, gy, u):
        g_in = weight_grad(n, gh).astype(BF16).reshape(narrow, cn, wide, fw).transpose(0, 2, 1, 3)
        g_out = weight_grad(gy, u).astype(BF16).reshape(wide, cw, narrow, halves, fw).transpose(2, 0, 3, 1, 4)
        return jnp.concatenate([g_in, g_out.reshape(narrow, wide, cn, fw)], axis=2)

    def attention_pack(n, dq, o, ga):
        g_q = weight_grad(n, dq).astype(BF16).reshape(narrow, cn, wide, 3 * cw)
        g_p = weight_grad(o, ga).astype(BF16).reshape(narrow, cn, wide, cw)
        return jnp.concatenate([g_q, g_p], axis=3).transpose(0, 2, 1, 3)

    def reduce(packed):
        flat = packed.reshape((-1, packed.shape[-1]))
        return lax.psum_scatter(flat, BOTH, scatter_dimension=0, tiled=True)

    red1 = reduce(mlp_pack(n4, gh2, gy2, u2))
    g4, ga3, dq3, small2, cb = backward_channel(
        g6, x4, z3, r3, q3, a3, mask, kernels[2], gains[2], wq1, wp1)
    redc = reduce(attention_pack(n3, dq3, o3, ga3))
    g2, gy1, gh1, small1, hid0 = backward_mlp(
        g4, x2, z2, r2, d1, mask, kernels[1], gains[1], win0, wout0)
    red0 = reduce(mlp_pack(n2, gh1, gy1, u1))
    input_grad, ga1, dq1, small0, sb = backward_window(
        g2, inputs, z1, r1, q1, p1, mask, kernels[0], gains[0], wq0, wp0)

    smalls = jnp.stack([small0, small1, small2, small3])
    per_layer = jnp.concatenate([smalls[:, a:b].reshape(narrow, layers * (b - a), wide, cw)
                                 for a, b in ((0, 9), (9, 10), (10, 11), (11, 12), (12, 13))], axis=1)
    per_layer = per_layer.transpose(0, 2, 1, 3)
    sb = sb.reshape(3, c)
    attn_grad = jnp.concatenate([sb[0:1], sb[2:3], cb.reshape(3, c)]).reshape(5, wide, cw).transpose(1, 0, 2)
    hid_grad = jnp.concatenate([hid0, hid1]).reshape(2, wide, fw).transpose(1, 0, 2).reshape(wide, -1, cw)
    common = jnp.concatenate([attn_grad, hid_grad], axis=1)
    common = jnp.broadcast_to(common[None], (narrow,) + common.shape)
    small_pack = pad_rows(jnp.concatenate([per_layer, common], axis=2), 4 * cw).astype(BF16)
    reds = reduce(jnp.concatenate([small_pack, attention_pack(n1, dq1, o1, ga1)], axis=2))

    sm = reds[:srows].reshape(-1, cw).astype(F32)
    kernel_g = sm[: 9 * layers].reshape(layers, 9, cw)
    one = [sm[k * layers : (k + 1) * layers] for k in range(9, 13)]
    attn_g = sm[count : count + 5]
    hidden_g = sm[count + 5 : count + 5 + 2 * fw // cw].reshape(2, fw)

    def attention_split(red):
        red = red.astype(F32)
        return red[:, : 3 * cw].T, red[:, 3 * cw :].T

    def mlp_split(red):
        red = red.astype(F32)
        second = red[cn:].reshape(halves, cw, fw).transpose(1, 0, 2).reshape(cw, halves * fw)
        return red[:cn].T, second

    gq0, gp0 = attention_split(reds[srows:])
    gq1, gp1 = attention_split(redc)
    gi0, go0 = mlp_split(red0)
    gi1, go1 = mlp_split(red1)
    return (
        out, input_grad, kernel_g, one[0], one[1], one[2], gq0, gq1, jnp.stack([gp0, gp1]),
        jnp.stack([gi0, gi1]), jnp.stack([go0, go1]), attn_g, hidden_g, one[3],
    )


def solution(mesh):
    matrix = P("wide", "narrow")
    cells = P(("wide", "narrow"), None, None, None)
    stacked = P(None, "wide", "narrow")
    row = P("narrow", "wide")
    shared = P(None, "wide")
    images = P(("wide", "narrow"))
    kernels = P("narrow", None, "wide")
    in_specs = (
        cells, images, images, kernels, row, row, row, matrix, matrix,
        stacked, stacked, stacked, shared, shared, row, cells,
    )
    out_specs = (
        cells, cells, kernels, row, row, row, matrix, matrix, stacked, stacked, stacked, shared, shared, row,
    )
    body = functools.partial(local, mesh.shape["wide"], mesh.shape["narrow"])
    return jax.shard_map(body, mesh=mesh, in_specs=in_specs, out_specs=out_specs, check_vma=False)
```

time: 3370 us -> 1270 us (0.38)
  waiting for transfers between devices: 1470 us -> 360 us
  other arithmetic: 569 us -> 35.7 us
  Pallas kernels: 0 us -> 500 us
  local copies, waits for them, and re-layouts: 695 us -> 270 us
  matrix products: 379 us -> 82.9 us
  blocking collectives: 220 us -> 0 us
    reduce_scatter x11 -> x4, waiting for transfers between devices: 970 us -> 247 us  [reduce(): return lax.psum_scatter(flat, BOTH, scatter_dimension=0, tiled=True)]
    pallas_call x0 -> x7, Pallas kernels: none -> 500 us  [image_call(): pl.pallas_call(kernel, grid=(images,), in_specs=ins, out_specs=out_specs,...]
    unnamed x44 -> x8, waiting for transfers between devices: 483 us -> 0.13 us
    reduce_sum x21 -> x0, other arithmetic: 307 us -> none  [the longest x4 92.1 us: layer_norm(): center = values - jnp.mean(values, axis=-1, keepdims=True)]
    dot_general x36 -> x8, matrix products: 379 us -> 82.9 us  [dot(): return lax.dot_general(a, b, dims, preferred_element_type=F32)]
    all_gather x15 -> x0, blocking collectives: 208 us -> none  [the longest x1 34 us: local(): lax.all_gather(cols_part[5], 'wide', axis=2, tiled=True)]
    convert_element_type x20 -> x2, local copies, waits for them, and re-layouts: 178 us -> 0.43 us  [the longest x1 0.36 us: local(): pad_rows(jnp.concatenate([per_layer, common], axis=2), 4 * cw).astype(BF16)]
    another operation x31 -> x10, local copies, waits for them, and re-layouts: 138 us -> 0.8 us  [the longest x2 0.47 us: local(): jnp.stack([go0, go1])]
  transfers between devices with their start and end apart: 31 -> 8, of which waited for: 24 -> 5; matrix products, arithmetic and copies ran while one was open for 23% -> 24% of each run, Pallas kernels for 0% -> 18%
where the time goes in v1:
time: 1270 us; the launch traced here: 1260 us
  Pallas kernels  500 us (39%)
  waiting for transfers between devices  360 us (28%)
  local copies, waits for them, and re-layouts  270 us (21%)
  matrix products  82.9 us (7%)
  other arithmetic  35.7 us (3%)
  between operations  15.2 us (1%)
    pallas_call x7, Pallas kernels, image_call(): pl.pallas_call(kernel, grid=(images,), in_specs=ins, out_specs=out_specs,...  500 us
    reduce_scatter x4, waiting for transfers between devices, reduce(): return lax.psum_scatter(flat, BOTH, scatter_dimension=0, tiled=True)  247 us
    all_gather x4, waiting for transfers between devices, spread(): return lax.all_gather(pieces, BOTH, axis=0, tiled=False)  113 us
    dot_general x8, matrix products, dot(): return lax.dot_general(a, b, dims, preferred_element_type=F32)  82.9 us
    unnamed x62, local copies, waits for them, and re-layouts  29.5 us
    reshape x2, local copies, waits for them, and re-layouts, attention_full(): wq = got[..., :3 * cw].reshape(c, 3 * c)  27.3 us
    reshape x4, local copies, waits for them, and re-layouts, attention_pack(): g_q = weight_grad(n, dq).astype(BF16).reshape(narrow, cn, wide, 3 * cw)  26.5 us
  transfers between devices with their start and end apart: 8, of which 5 were waited for; matrix products, arithmetic and copies ran while one was open for 24% of the time, Pallas kernels for 18%

profile of v1, /device:TPU:0, one launch (start us, length us, event | category | flops | bytes accessed | tf_op | source)
XLA Modules:
  0.0 1264.4 jit_solution(4075906272227391455)
XLA Ops:
  23.6 54.4 %all-gather.13.cloned.1.call-done = bf16[6144,384]{1,0:T(8,128)(2,1)} async-done(((bf16[192,384]{1,0:T(8,128)(2,1)}), bf16[6144,384]{1,0:T(8,128)(2,1)}) %all-gather.13.cloned.1.call-update) | async-done | bytes 4718608 | tf_op jit(solution)/shard_map/all_gather | solution.py:605
  83.5 7.3 copy.154
  90.7 8.0 reshape.417.wq
  98.7 46.5 %all-gather.9.cloned.1.call-done = bf16[6656,384]{1,0:T(8,128)(2,1)} async-done(((bf16[208,384]{1,0:T(8,128)(2,1)}), bf16[6656,384]{1,0:T(8,128)(2,1)}) %all-gather.9.cloned.1.call-update) | async-done | bytes 5111824 | tf_op jit(solution)/shard_map/all_gather | solution.py:605
  146.3 5.0 slice.345
  172.2 7.3 copy.144
  179.5 19.3 %reshape.409.wq = bf16[768,2304]{1,0:T(8,128)(2,1)} reshape(bf16[4,192,8,288]{3,2,1,0:T(8,128)(2,1)} %copy.144) | data formatting | bytes 7077888 | tf_op jit(solution)/shard_map/reshape | solution.py:639
  200.7 71.5 %window_forward.1 = (bf16[8,224,768]{2,1,0:T(8,128)(2,1)}, f32[8,224,768]{2,1,0:T(8,128)}, f32[8,224,128]{2,1,0:T(8,128)}, bf16[8,224,2304]{2,1,0:T(8,128)(2,1)}...) custom-call(bf16[8,14,14,768]{3,2,1,0:T(8,128)(2,1)} %copy.146.inp, ...), custom_call_target="tpu_custom_call" | custom-call | flops 10569646080 | bytes 38600704 | tf_op jit(solution)/shard_map/window_forward/pallas_call | solution.py:482
  272.3 8.5 fusion.6
  280.8 9.4 copy.160
  290.3 11.3 reshape.423.w_out
  301.5 12.4 all-gather.11.cloned.1.call-done
  314.0 8.6 fusion.7
  322.6 8.4 copy.150
  331.0 11.6 reshape.415.w_out
  342.7 5.3 copy.149
  348.0 3.3 copy.185
  354.1 3.3 copy.186
  357.4 58.7 %mlp_forward.1 = (bf16[8,224,768]{2,1,0:T(8,128)(2,1)}, f32[8,224,768]{2,1,0:T(8,128)}, f32[8,224,128]{2,1,0:T(8,128)}, bf16[8,224,3072]{2,1,0:T(8,128)(2,1)}, b...) custom-call(f32[8,224,768]{2,1,0:T(8,128)} %get-tuple-element.57.x_in, f32[8,224,128]{2,1,0:T(8,128)} %broadcast_in_dim.8.mask, ...), custom_call_target="tpu_custom_call" | custom-call | flops 16911433728 | bytes 52612096 | tf_op jit(solution)/shard_map/mlp_forward/pallas_call | solution.py:482
  416.1 45.7 %channel_forward.1 = (bf16[8,224,768]{2,1,0:T(8,128)(2,1)}, f32[8,224,768]{2,1,0:T(8,128)}, f32[8,224,128]{2,1,0:T(8,128)}, bf16[8,224,2304]{2,1,0:T(8,128)(2,1)...) custom-call(f32[8,224,768]{2,1,0:T(8,128)} %get-tuple-element.58.x_in, ...), custom_call_target="tpu_custom_call" | custom-call | flops 9512681472 | bytes 40026112 | tf_op jit(solution)/shard_map/channel_forward/pallas_call | solution.py:482
  461.8 109.4 %last_mlp.1 = (bf16[8,14,14,768]{3,2,1,0:T(8,128)(2,1)}, f32[8,224,768]{2,1,0:T(8,128)}, bf16[8,224,768]{2,1,0:T(8,128)(2,1)}, bf16[8,224,3072]{2,1,0:T(8,128)(2...) custom-call(f32[8,224,768]{2,1,0:T(8,128)} %get-tuple-element.59.x_in, ...), custom_call_target="tpu_custom_call" | custom-call | flops 33822867456 | bytes 53811200 | tf_op jit(solution)/shard_map/last_mlp/pallas_call | solution.py:482
  571.3 58.9 %channel_backward.1 = (f32[8,224,768]{2,1,0:T(8,128)}, bf16[8,224,768]{2,1,0:T(8,128)(2,1)}, bf16[8,224,2304]{2,1,0:T(8,128)(2,1)}, f32[13,768]{1,0:T(8,128)}, f32[1,2304]{1,0:T(1,128)}) custom-call(f32[8,224,768]{2,1,0:T(8,128)} %get-tuple-element.61.g_in, f32[8,224,768]{2,1,0:T(8,128)} %get-tuple-element.58.x_in, f32[8,224,768]{2,1,0:T(8,128)} %get-tuple-element.62.z_in, ...), custom_call_target="tpu_custom_call" | custom-call | flops 10569646080 | bytes 51066880 | tf_op jit(solution)/shard_map/channel_backward/pallas_call | solution.py:482
  630.2 5.0 bitcast_convert_fusion.6
  637.3 11.9 bitcast_convert_fusion.4
  649.1 10.0 reshape.435
  659.2 3.2 copy.169
  662.4 3.4 pad_maximum_fusion.3
  665.9 64.1 %mlp_backward.1 = (f32[8,224,768]{2,1,0:T(8,128)}, bf16[8,224,768]{2,1,0:T(8,128)(2,1)}, bf16[8,224,3072]{2,1,0:T(8,128)(2,1)}, f32[13,768]{1,0:T(8,128)}, f32[1,3072]{1,0:T(1,128)}) custom-call(f32[8,224,768]{2,1,0:T(8,128)} %get-tuple-element.66.g_in, f32[8,224,768]{2,1,0:T(8,128)} %get-tuple-element.57.x_in, f32[8,224,768]{2,1,0:T(8,128)} %get-tuple-element.67.z_in, ...), custom_call_target="tpu_custom_call" | custom-call | flops 16911433728 | bytes 58147840 | tf_op jit(solution)/shard_map/mlp_backward/pallas_call | solution.py:482
  730.9 91.7 %window_backward.1 = (bf16[8,14,14,768]{3,2,1,0:T(8,128)(2,1)}, bf16[8,224,768]{2,1,0:T(8,128)(2,1)}, bf16[8,224,2304]{2,1,0:T(8,128)(2,1)}, f32[13,768]{1,0:T(8,128)}, f32[1,2304]{1,0:T(1,128)}) custom-call(f32[8,224,768]{2,1,0:T(8,128)} %get-tuple-element.70.g_in, bf16[8,14,14,768]{3,2,1,0:T(8,128)(2,1)} %copy.146.inp, ...), custom_call_target="tpu_custom_call" | custom-call | flops 12683575296 | bytes 46544896 | tf_op jit(solution)/shard_map/window_backward/pallas_call | solution.py:482
  826.9 5.0 bitcast_convert_fusion.7
  833.9 12.0 bitcast_convert_fusion.5
  846.0 10.0 reshape.431
  856.0 3.2 copy.167
  864.9 13.3 %bitcast_convert_fusion.2 = bf16[768,3072]{1,0:T(8,128)(2,1)} fusion(bf16[8,224,768]{2,1,0:T(8,128)(2,1)S(1)} %copy-done.13, bf16[8,224,3072]{2,1,0:T(8,128)(2,1)} %get-tuple-element.95), kind=kOutput, calls=%fused_computation.4 | convolution fusion | flops 8458076160 | bytes 18481152 | tf_op jit(solution)/shard_map/dot_general | solution.py:29
  878.2 11.7 reshape.439
  889.9 5.4 copy.171
  895.3 12.0 bitcast_convert_fusion.3
  909.0 8.1 pad_maximum_fusion
  917.1 9.2 copy.172
  926.4 13.3 %bitcast_convert_fusion.1 = bf16[768,3072]{1,0:T(8,128)(2,1)S(1)} fusion(bf16[8,224,768]{2,1,0:T(8,128)(2,1)} %get-tuple-element.96, bf16[8,224,3072]{2,1,0:T(8,128)(2,1)} %get-tuple-element.97), kind=kOutput, calls=%fused_computation.3 | convolution fusion | flops 8458076160 | bytes 18481152 | tf_op jit(solution)/shard_map/dot_general | solution.py:29
  939.7 3.4 copy.188
  943.1 10.4 bitcast_convert_fusion
  953.5 11.8 reshape.443
  965.4 5.3 copy.173
  971.2 8.1 pad_maximum_fusion.1
  979.3 9.4 copy.174
  1004.0 107.6 %reduce-scatter.9.cloned.1.call-done = bf16[384,384]{1,0:T(8,128)(2,1)} async-done(((bf16[12288,384]{1,0:T(8,128)(2,1)}), bf16[384,384]{1,0:T(8,128)(2,1)}) %reduce-scatter.9.cloned.1.call-update) | async-done | bytes 294928 | tf_op jit(solution)/shard_map/reduce_scatter | solution.py:699
  1114.1 139.1 %reduce-scatter.11.cloned.1.call-done = bf16[384,384]{1,0:T(8,128)(2,1)} async-done(((bf16[12288,384]{1,0:T(8,128)(2,1)}), bf16[384,384]{1,0:T(8,128)(2,1)}) %reduce-scatter.11.cloned.1.call-update) | async-done | bytes 294928 | tf_op jit(solution)/shard_map/reduce_scatter | solution.py:699
  (209 shorter events, 87.2 us)
Async XLA Ops:
  7.2 12.0 copy-start.2
  7.2 70.8 %all-gather.13.cloned.1.call-start = ((), (), s32[]{:S(2)}) async-start(), calls=%async_computation.10 | async-start | bytes 4866048 | tf_op jit(solution)/shard_map/all_gather | solution.py:605
  10.2 135.1 %all-gather.9.cloned.1.call-start = ((), (), s32[]{:S(2)}) async-start(), calls=%async_computation.8 | async-start | bytes 5271552 | tf_op jit(solution)/shard_map/all_gather | solution.py:605
  15.3 256.9 %all-gather.15.cloned.1.call-start = ((), (), s32[]{:S(2)}) async-start(), calls=%async_computation.11 | async-start | bytes 9732096 | tf_op jit(solution)/shard_map/all_gather | solution.py:605
  18.3 295.7 %all-gather.11.cloned.1.call-start = ((), (), s32[]{:S(2)}) async-start(), calls=%async_computation.9 | async-start | bytes 9732096 | tf_op jit(solution)/shard_map/all_gather | solution.py:605
  19.1 4.4 copy-start.9
  19.2 4.4 copy-start.10
  19.2 977.0 %reduce-scatter.7.cloned.1.call-start = ((), (), s32[]{:S(2)}) async-start(), calls=%async_computation.5 | async-start | bytes 4866048 | tf_op jit(solution)/shard_map/reduce_scatter | solution.py:699
  19.2 2.1 copy-start.3
  342.7 8.6 slice-start.2
  348.0 3.3 slice-start.3
  665.8 332.3 %reduce-scatter.5.cloned.1.call-start = ((), (), s32[]{:S(2)}) async-start(), calls=%async_computation.4 | async-start | bytes 5271552 | tf_op jit(solution)/shard_map/reduce_scatter | solution.py:699
  665.9 64.2 %copy-start.7 = (f32[1,3072]{1,0:T(1,128)S(1)}, f32[1,3072]{1,0:T(1,128)}, u32[]{:S(2)}) copy-start(f32[1,3072]{1,0:T(1,128)} %get-tuple-element.83) | copy-start | bytes 36868
  730.9 92.6 %copy-start.8 = (f32[1,2304]{1,0:T(1,128)S(1)}, f32[1,2304]{1,0:T(1,128)}, u32[]{:S(2)}) copy-start(f32[1,2304]{1,0:T(1,128)} %get-tuple-element.81) | copy-start | bytes 27652
  730.9 92.8 %copy-start.4 = (f32[13,768]{1,0:T(8,128)S(1)}, f32[13,768]{1,0:T(8,128)}, u32[]{:S(2)}) copy-start(f32[13,768]{1,0:T(8,128)} %get-tuple-element.79) | copy-start | bytes 119812
  730.9 92.7 %copy-start.5 = (f32[13,768]{1,0:T(8,128)S(1)}, f32[13,768]{1,0:T(8,128)}, u32[]{:S(2)}) copy-start(f32[13,768]{1,0:T(8,128)} %get-tuple-element.78) | copy-start | bytes 119812
  730.9 92.7 %copy-start.6 = (f32[13,768]{1,0:T(8,128)S(1)}, f32[13,768]{1,0:T(8,128)}, u32[]{:S(2)}) copy-start(f32[13,768]{1,0:T(8,128)} %get-tuple-element.77) | copy-start | bytes 119812
  863.2 1.8 copy-start.13
  863.2 248.4 %reduce-scatter.9.cloned.1.call-start = ((), (), s32[]{:S(2)}) async-start(), calls=%async_computation.6 | async-start | bytes 9732096 | tf_op jit(solution)/shard_map/reduce_scatter | solution.py:699
  889.9 5.4 copy-start.12
  926.3 16.7 %slice-start.4 = ((s8[11010048]{0:T(1024)(128)(4,1)}), s8[2621440]{0:T(1024)(128)(4,1)S(1)}, s32[]{:S(2)}) async-start(s8[11010048]{0:T(1024)(128)(4,1)} %bitcast.241), calls=%async_computation.16 | async-start | bytes 5242880
  926.4 326.8 %reduce-scatter.11.cloned.1.call-start = ((), (), s32[]{:S(2)}) async-start(), calls=%async_computation.7 | async-start | bytes 9732096 | tf_op jit(solution)/shard_map/reduce_scatter | solution.py:699
  926.4 16.7 %slice-start.5 = ((s8[11010048]{0:T(1024)(128)(4,1)}), s8[4194304]{0:T(1024)(128)(4,1)S(1)}, s32[]{:S(2)}) async-start(s8[11010048]{0:T(1024)(128)(4,1)} %bitcast.241), calls=%async_computation.17 | async-start | bytes 8388608
  926.4 16.7 %slice-start.6 = ((s8[11010048]{0:T(1024)(128)(4,1)}), s8[4194304]{0:T(1024)(128)(4,1)S(1)}, s32[]{:S(2)}) async-start(s8[11010048]{0:T(1024)(128)(4,1)} %bitcast.241), calls=%async_computation.18 | async-start | bytes 8388608
  939.7 3.4 copy-start.11
  953.5 17.2 %slice-start = ((s8[4718592]{0:T(1024)(128)(4,1)}), s8[524288]{0:T(1024)(128)(4,1)S(1)}, s32[]{:S(2)}) async-start(s8[4718592]{0:T(1024)(128)(4,1)} %bitcast.190), calls=%async_computation.12 | async-start | bytes 1048576
  965.4 5.3 slice-start.1
  988.7 1.9 copy-start
  988.8 4.6 copy-start.1
Sparse Core Ops, SparseCore 0:
  11.6 66.3 all-gather.12
  81.6 63.6 all-gather.8
  148.8 80.9 all-gather.14
  233.2 80.7 all-gather.10
  666.0 105.6 reduce-scatter.6
  863.3 107.5 reduce-scatter.4
  976.8 134.7 reduce-scatter.8
  1118.5 134.5 reduce-scatter.10

commit v2 on v1

v2 whole, which is shorter than its diff:
```python
import functools

import jax
import jax.numpy as jnp
from jax import lax
from jax.experimental import pallas as pl
from jax.experimental.pallas import tpu as pltpu
from jax.sharding import PartitionSpec as P

HD = 32
WIN = 7
LANES = 128
SUB = 8
GROUP = 256
WTOK = WIN * SUB
FFC = 1024
NROWS = 112
SCALE = HD ** (-0.5)
EPS = 1e-05
NEG = -1e30
F32 = jnp.float32
BF16 = jnp.bfloat16
VMEM_LIMIT = 60 * 1024 * 1024
DIMS_NN = (((1,), (0,)), ((), ()))
DIMS_NT = (((1,), (1,)), ((), ()))
DIMS_TN = (((0,), (0,)), ((), ()))


def dot(a, b, dims):
    return lax.dot_general(a, b, dims, preferred_element_type=F32)


def tok(r, half):
    return ((r // WIN) * 2 + half) * WTOK + (r % WIN) * SUB


def load_cells(src, dst):
    for r in range(2 * WIN):
        row = src[0, r].astype(F32)
        dst[pl.ds(tok(r, 0), WIN), :] = row[:WIN]
        dst[pl.ds(tok(r, 1), WIN), :] = row[WIN:]


def store_cells(value_at, dst, stage):
    for r in range(2 * WIN):
        stage[pl.ds(0, SUB), :] = value_at(tok(r, 0))
        stage[pl.ds(WIN, SUB), :] = value_at(tok(r, 1))
        dst[0, r] = stage[pl.ds(0, 2 * WIN), :].astype(BF16)


def neighbours(left, right):
    last = lax.broadcasted_iota(jnp.int32, (SUB, LANES), 0) == SUB - 1
    up_right = pltpu.roll(right, SUB - 1, 0)
    up_left = pltpu.roll(jnp.where(last, up_right, left), SUB - 1, 0)
    down_left = pltpu.roll(left, 1, 0)
    down_right = pltpu.roll(jnp.where(last, down_left, right), 1, 0)
    return ((down_left, left, up_left), (down_right, right, up_right))


def masked_row(src, mask, r, lanes):
    pair = []
    for half in range(2):
        rows = pl.ds(tok(r, half), SUB)
        pair.append(src[rows, lanes] * mask[0, rows, :])
    return neighbours(*pair)


def plain_row(src, r, lanes):
    return neighbours(*[src[pl.ds(tok(r, half), SUB), lanes] for half in range(2)])


def lay_row(lay, k):
    return lay[0, pl.ds(k, 1), :]


def taps(lay, lanes):
    return [jnp.broadcast_to(lay[0, pl.ds(k, 1), lanes], (SUB, LANES)) for k in range(10)]


def conv_forward(src, mask, lay, dst):
    rows = 2 * WIN

    @pl.loop(0, src.shape[1] // LANES)
    def _(j):
        lanes = pl.ds(pl.multiple_of(j * LANES, LANES), LANES)
        w = taps(lay, lanes)
        shift = w[9]
        window = [None, masked_row(src, mask, 0, lanes), masked_row(src, mask, 1, lanes)]
        for r in range(rows):
            for half in range(2):
                total = shift
                for a in range(3):
                    if window[a] is None:
                        continue
                    for b in range(3):
                        total = total + w[3 * a + b] * window[a][half][b]
                at = pl.ds(tok(r, half), SUB)
                dst[at, lanes] = src[at, lanes] + total
            following = masked_row(src, mask, r + 2, lanes) if r + 2 < rows else None
            window = [window[1], window[2], following]


def conv_backward(x_src, g_src, mask, lay, sums, dst):
    rows = 2 * WIN

    @pl.loop(0, x_src.shape[1] // LANES)
    def _(j):
        lanes = pl.ds(pl.multiple_of(j * LANES, LANES), LANES)
        w = taps(lay, lanes)
        g_win = [None, plain_row(g_src, 0, lanes), plain_row(g_src, 1, lanes)]
        x_win = [None, masked_row(x_src, mask, 0, lanes), masked_row(x_src, mask, 1, lanes)]
        grads = [sums[pl.ds(SUB * k, SUB), lanes] for k in range(10)]
        for r in range(rows):
            for half in range(2):
                center = g_win[1][half][1]
                total = None
                for a in range(3):
                    for b in range(3):
                        if x_win[a] is not None:
                            grads[3 * a + b] = grads[3 * a + b] + center * x_win[a][half][b]
                        if g_win[2 - a] is not None:
                            term = w[3 * a + b] * g_win[2 - a][half][2 - b]
                            total = term if total is None else total + term
                grads[9] = grads[9] + center
                at = pl.ds(tok(r, half), SUB)
                dst[at, lanes] = center + mask[0, at, :] * total
            more = r + 2 < rows
            g_win = [g_win[1], g_win[2], plain_row(g_src, r + 2, lanes) if more else None]
            x_win = [x_win[1], x_win[2], masked_row(x_src, mask, r + 2, lanes) if more else None]
        for k in range(10):
            sums[pl.ds(SUB * k, SUB), lanes] = grads[k]


def norm_forward(src, lay, z_out, r_out, n_out):
    features = src.shape[1]

    @pl.loop(0, src.shape[0] // (2 * NROWS))
    def _(i):
        for j in range(2):
            rows = pl.ds(pl.multiple_of(i * (2 * NROWS) + j * NROWS, NROWS), NROWS)
            x = src[rows, :]
            center = x - jnp.sum(x, axis=1, keepdims=True) * (1.0 / features)
            var = jnp.sum(center * center, axis=1, keepdims=True) * (1.0 / features)
            rstd = lax.rsqrt(var + EPS)
            z = center * rstd
            z_out[rows, :] = z
            r_out[rows, :] = jnp.broadcast_to(rstd, (NROWS, LANES))
            n_out[rows, :] = (z * lay_row(lay, 10) + lay_row(lay, 11)).astype(BF16)


def norm_backward(dn, z_src, r_src, lay, g_src, sums, first, dst):
    features = dn.shape[1]

    @pl.loop(0, dn.shape[0] // (2 * NROWS))
    def _(i):
        for j in range(2):
            rows = pl.ds(pl.multiple_of(i * (2 * NROWS) + j * NROWS, NROWS), NROWS)
            d = dn[rows, :]
            z = z_src[rows, :]
            t = d * lay_row(lay, 10)
            m1 = jnp.sum(t, axis=1, keepdims=True) * (1.0 / features)
            m2 = jnp.sum(t * z, axis=1, keepdims=True) * (1.0 / features)
            dst[rows, :] = g_src[rows, :] + (t - m1 - z * m2) * r_src[rows, 0:1]
            at = pl.ds(first, SUB)
            sums[at, :] = sums[at, :] + fold_rows(d * z)
            at = pl.ds(first + SUB, SUB)
            sums[at, :] = sums[at, :] + fold_rows(d)


def fold_rows(value):
    total = value[:SUB]
    for i in range(1, value.shape[0] // SUB):
        total = total + value[SUB * i : SUB * (i + 1)]
    return total


def finish_sums(sums, out):
    for k in range(sums.shape[0] // SUB):
        out[pl.ds(k, 1), :] = jnp.sum(sums[pl.ds(SUB * k, SUB), :], axis=0, keepdims=True)


def head_masks():
    lane = lax.broadcasted_iota(jnp.int32, (WTOK, GROUP), 1) // HD
    return [lane == h for h in range(GROUP // HD)]


def spread_heads(value, masks):
    return jnp.concatenate([jnp.where(m, value, 0.0) for m in masks], axis=0).astype(BF16)


def collect_heads(full, masks):
    total = full[:WTOK]
    for h in range(1, len(masks)):
        total = jnp.where(masks[h], full[WTOK * h : WTOK * (h + 1)], total)
    return total


def rounded(value):
    return value.astype(BF16).astype(F32)


def gelu_pair(h):
    cdf = 0.5 * (1.0 + lax.erf(h * 0.7071067811865476))
    pdf = jnp.exp(h * h * -0.5) * 0.3989422804014327
    return h * cdf, cdf + h * pdf


def first_step():
    return pl.program_id(0) == 0


def last_step():
    return pl.program_id(0) == pl.num_programs(0) - 1


def window_forward_kernel(
    inp, mask, lay, sh, watt,
    n_out, z_out, r_out, q_out, o_out, p_out, x_out,
    x0, x1, qf, of,
):
    features = x0.shape[1]

    @pl.when(first_step())
    def _():
        x0[...] = jnp.zeros_like(x0)

    load_cells(inp, x0)
    conv_forward(x0, mask, lay, x1)
    norm_forward(x1, lay, z_out.at[0], r_out.at[0], n_out.at[0])
    chunk = features
    for c in range(3):
        lanes = pl.ds(c * chunk, chunk)
        part = dot(n_out[0], watt[:, lanes], DIMS_NN)
        if c != 1:
            part = part + sh[pl.ds(c // 2, 1), :]
        part = part.astype(BF16)
        q_out[0, :, lanes] = part
        qf[:, lanes] = part.astype(F32)

    @pl.loop(0, 4)
    def _(w):
        rows = pl.ds(pl.multiple_of(w * WTOK, SUB), WTOK)
        valid = mask[0, rows, 0:1] > 0.0
        masks = head_masks()
        for g in range(features // GROUP):
            q = qf[rows, pl.ds(g * GROUP, GROUP)]
            k = qf[rows, pl.ds(features + g * GROUP, GROUP)].astype(BF16)
            v = qf[rows, pl.ds(2 * features + g * GROUP, GROUP)].astype(BF16)
            s = dot(k, spread_heads(q, masks), DIMS_NT) * SCALE
            s = jnp.where(valid, s, NEG)
            e = jnp.exp(s - jnp.max(s, axis=0, keepdims=True))
            p = (e / jnp.sum(e, axis=0, keepdims=True)).astype(BF16)
            p_out[0, w, g] = p
            of[rows, pl.ds(g * GROUP, GROUP)] = collect_heads(dot(p, v, DIMS_TN), masks)

    o_out[0] = of[...].astype(BF16)
    x_out[0] = x1[...] + (dot(o_out[0], watt[:, pl.ds(3 * features, features)], DIMS_NN) + lay_row(lay, 12))


def mlp_forward_kernel(
    x_in, mask, lay, hb, w_in, w_out,
    n_out, z_out, r_out, u_out, d_out, x_out,
    x1, acc,
):
    conv_forward(x_in.at[0], mask, lay, x1)
    norm_forward(x1, lay, z_out.at[0], r_out.at[0], n_out.at[0])
    for c in range(w_in.shape[1] // FFC):
        lanes = pl.ds(c * FFC, FFC)
        h = dot(n_out[0], w_in[:, lanes], DIMS_NN) + hb[0, :, lanes]
        u, d = gelu_pair(h)
        u = u.astype(BF16)
        u_out[0, :, lanes] = u
        d_out[0, :, lanes] = d.astype(BF16)
        y = dot(u, w_out[:, lanes], DIMS_NT)
        acc[...] = y if c == 0 else acc[...] + y
    x_out[0] = x1[...] + (acc[...] + lay_row(lay, 12))


def group_mask():
    row = lax.broadcasted_iota(jnp.int32, (GROUP, GROUP), 0) // HD
    col = lax.broadcasted_iota(jnp.int32, (GROUP, GROUP), 1) // HD
    return row == col


def channel_forward_kernel(
    x_in, mask, lay, sh, watt,
    n_out, z_out, r_out, q_out, o_out, a_out, x_out,
    x1,
):
    features = x1.shape[1]
    conv_forward(x_in.at[0], mask, lay, x1)
    norm_forward(x1, lay, z_out.at[0], r_out.at[0], n_out.at[0])
    for c in range(3):
        lanes = pl.ds(c * features, features)
        part = dot(n_out[0], watt[:, lanes], DIMS_NN) + sh[pl.ds(2 + c, 1), :]
        if c == 1:
            part = part * mask[0, :, 0:1]
        q_out[0, :, lanes] = part.astype(BF16)
    same = group_mask()
    for g in range(features // GROUP):
        q = q_out[0, :, pl.ds(g * GROUP, GROUP)]
        k = q_out[0, :, pl.ds(features + g * GROUP, GROUP)]
        v = q_out[0, :, pl.ds(2 * features + g * GROUP, GROUP)]
        s = jnp.where(same, dot(k, q, DIMS_TN) * SCALE, -jnp.inf)
        e = jnp.exp(s - jnp.max(s, axis=0, keepdims=True))
        a = (e / jnp.sum(e, axis=0, keepdims=True)).astype(BF16)
        a_out[0, g] = a
        o_out[0, :, pl.ds(g * GROUP, GROUP)] = dot(v, a, DIMS_NN).astype(BF16)
    x_out[0] = x1[...] + (dot(o_out[0], watt[:, pl.ds(3 * features, features)], DIMS_NN) + lay_row(lay, 12))


def last_mlp_kernel(
    x_in, cot, mask, lay, hb, w_in, w_out,
    out, g_out, n_out, u_out, gy_out, gh_out, small_out, hidden_out,
    x1, z, r, acc, dn, g8, stage, sums, hsums,
):
    @pl.when(first_step())
    def _():
        g8[...] = jnp.zeros_like(g8)
        sums[...] = jnp.zeros_like(sums)
        hsums[...] = jnp.zeros_like(hsums)

    x6 = x_in.at[0]
    load_cells(cot, g8)
    conv_forward(x6, mask, lay, x1)
    norm_forward(x1, lay, z, r, n_out.at[0])
    g8[...] = g8[...] * mask[0, :, 0:1]
    gy_out[0] = g8[...].astype(BF16)
    sums[pl.ds(12 * SUB, SUB), :] = sums[pl.ds(12 * SUB, SUB), :] + fold_rows(gy_out[0].astype(F32))
    for c in range(w_in.shape[1] // FFC):
        lanes = pl.ds(c * FFC, FFC)
        h = dot(n_out[0], w_in[:, lanes], DIMS_NN) + hb[0, :, lanes]
        du = dot(gy_out[0], w_out[:, lanes], DIMS_NN)
        u, d = gelu_pair(h)
        u = u.astype(BF16)
        u_out[0, :, lanes] = u
        gh = (du * d).astype(BF16)
        gh_out[0, :, lanes] = gh
        hsums[:, lanes] = hsums[:, lanes] + fold_rows(gh.astype(F32))
        y = dot(u, w_out[:, lanes], DIMS_NT)
        dx = dot(gh, w_in[:, lanes], DIMS_NT)
        acc[...] = y if c == 0 else acc[...] + y
        dn[...] = dx if c == 0 else dn[...] + dx
    acc[...] = (x1[...] + (acc[...] + lay_row(lay, 12))) * mask[0, :, 0:1]
    store_cells(lambda at: acc[pl.ds(at, SUB), :], out, stage)
    norm_backward(dn, z, r, lay, g8, sums, 10 * SUB, x1)
    conv_backward(x6, x1, mask, lay, sums, g_out.at[0])

    @pl.when(last_step())
    def _():
        finish_sums(sums, small_out)
        finish_sums(hsums, hidden_out)


def mlp_backward_kernel(
    g_in, x_in, z_in, r_in, d_in, mask, lay, w_in, w_out,
    g_out, gy_out, gh_out, small_out, hidden_out,
    dn, g1, sums, hsums,
):
    @pl.when(first_step())
    def _():
        sums[...] = jnp.zeros_like(sums)
        hsums[...] = jnp.zeros_like(hsums)

    gy_out[0] = g_in[0].astype(BF16)
    sums[pl.ds(12 * SUB, SUB), :] = sums[pl.ds(12 * SUB, SUB), :] + fold_rows(gy_out[0].astype(F32))
    for c in range(w_in.shape[1] // FFC):
        lanes = pl.ds(c * FFC, FFC)
        du = dot(gy_out[0], w_out[:, lanes], DIMS_NN)
        gh = (du * d_in[0, :, lanes].astype(F32)).astype(BF16)
        gh_out[0, :, lanes] = gh
        hsums[:, lanes] = hsums[:, lanes] + fold_rows(gh.astype(F32))
        dx = dot(gh, w_in[:, lanes], DIMS_NT)
        dn[...] = dx if c == 0 else dn[...] + dx
    norm_backward(dn, z_in.at[0], r_in.at[0], lay, g_in.at[0], sums, 10 * SUB, g1)
    conv_backward(x_in.at[0], g1, mask, lay, sums, g_out.at[0])

    @pl.when(last_step())
    def _():
        finish_sums(sums, small_out)
        finish_sums(hsums, hidden_out)


def channel_backward_kernel(
    g_in, x_in, z_in, r_in, q_in, a_in, mask, lay, watt,
    g_out, ga_out, dq_out, small_out, bias_out,
    dn, g1, sums, bsums,
):
    features = dn.shape[1]

    @pl.when(first_step())
    def _():
        sums[...] = jnp.zeros_like(sums)
        bsums[...] = jnp.zeros_like(bsums)

    ga_out[0] = g_in[0].astype(BF16)
    sums[pl.ds(12 * SUB, SUB), :] = sums[pl.ds(12 * SUB, SUB), :] + fold_rows(ga_out[0].astype(F32))
    go = dot(ga_out[0], watt[:, pl.ds(3 * features, features)], DIMS_NT).astype(BF16)
    for g in range(features // GROUP):
        at = [pl.ds(i * features + g * GROUP, GROUP) for i in range(3)]
        q, k, v = (q_in[0, :, lanes] for lanes in at)
        gog = go[:, g * GROUP : (g + 1) * GROUP]
        a = a_in[0, g]
        af = a.astype(F32)
        dp = dot(v, gog, DIMS_TN)
        ds = (af * (dp - jnp.sum(dp * af, axis=0, keepdims=True))).astype(BF16)
        dq_out[0, :, at[0]] = (dot(k, ds, DIMS_NN) * SCALE).astype(BF16)
        dq_out[0, :, at[1]] = (dot(q, ds, DIMS_NT) * SCALE * mask[0, :, 0:1]).astype(BF16)
        dq_out[0, :, at[2]] = dot(gog, a, DIMS_NT).astype(BF16)
    bsums[...] = bsums[...] + fold_rows(dq_out[0].astype(F32))
    dn[...] = dot(dq_out[0], watt[:, pl.ds(0, 3 * features)], DIMS_NT)
    norm_backward(dn, z_in.at[0], r_in.at[0], lay, g_in.at[0], sums, 10 * SUB, g1)
    conv_backward(x_in.at[0], g1, mask, lay, sums, g_out.at[0])

    @pl.when(last_step())
    def _():
        finish_sums(sums, small_out)
        finish_sums(bsums, bias_out)


def window_backward_kernel(
    g_in, inp, z_in, r_in, q_in, p_in, mask, lay, watt,
    g_out, ga_out, dq_out, small_out, bias_out,
    x0, qf, gof, dqf, dn, g1, stage, sums, bsums,
):
    features = dn.shape[1]

    @pl.when(first_step())
    def _():
        x0[...] = jnp.zeros_like(x0)
        sums[...] = jnp.zeros_like(sums)
        bsums[...] = jnp.zeros_like(bsums)

    load_cells(inp, x0)
    ga_out[0] = g_in[0].astype(BF16)
    sums[pl.ds(12 * SUB, SUB), :] = sums[pl.ds(12 * SUB, SUB), :] + fold_rows(ga_out[0].astype(F32))
    gof[...] = rounded(dot(ga_out[0], watt[:, pl.ds(3 * features, features)], DIMS_NT))
    qf[...] = q_in[0].astype(F32)

    @pl.loop(0, 4)
    def _(w):
        rows = pl.ds(pl.multiple_of(w * WTOK, SUB), WTOK)
        masks = head_masks()
        for g in range(features // GROUP):
            at = [pl.ds(i * features + g * GROUP, GROUP) for i in range(3)]
            qe = spread_heads(qf[rows, at[0]], masks)
            k = qf[rows, at[1]].astype(BF16)
            v = qf[rows, at[2]].astype(BF16)
            goe = spread_heads(gof[rows, at[0]], masks)
            p = p_in[0, w, g]
            pf = p.astype(F32)
            dp = dot(v, goe, DIMS_NT)
            ds = (pf * (dp - jnp.sum(dp * pf, axis=0, keepdims=True))).astype(BF16)
            dqf[rows, at[0]] = collect_heads(dot(ds, k, DIMS_TN), masks) * SCALE
            dqf[rows, at[1]] = dot(ds, qe, DIMS_NN) * SCALE
            dqf[rows, at[2]] = dot(p, goe, DIMS_NN)

    dq_out[0] = dqf[...].astype(BF16)
    bsums[...] = bsums[...] + fold_rows(dq_out[0].astype(F32))
    dn[...] = dot(dq_out[0], watt[:, pl.ds(0, 3 * features)], DIMS_NT)
    norm_backward(dn, z_in.at[0], r_in.at[0], lay, g_in.at[0], sums, 10 * SUB, g1)
    conv_backward(x0, g1, mask, lay, sums, dn)
    store_cells(lambda at: dn[pl.ds(at, SUB), :], g_out, stage)

    @pl.when(last_step())
    def _():
        finish_sums(sums, small_out)
        finish_sums(bsums, bias_out)


def per_image(shape):
    rest = (0,) * (len(shape) - 1)
    return pl.BlockSpec((1,) + tuple(shape[1:]), lambda i: (i,) + rest)


def whole(shape):
    zeros = (0,) * len(shape)
    return pl.BlockSpec(tuple(shape), lambda i: zeros, pipeline_mode=pl.Buffered(1))


def one_layer(shape, layer):
    return pl.BlockSpec((1,) + tuple(shape[1:]), lambda i: (layer, 0, 0), pipeline_mode=pl.Buffered(1))


def cost(flops, arrays):
    size = sum(jnp.dtype(d).itemsize * functools.reduce(lambda p, q: p * q, s) for s, d in arrays)
    return pl.CostEstimate(flops=int(flops), bytes_accessed=int(size), transcendentals=0)


def params():
    return pltpu.CompilerParams(dimension_semantics=("arbitrary",), vmem_limit_bytes=VMEM_LIMIT)


def image_call(kernel, name, layer, batched, lay, shared, outs, sums, scratch, flops):
    images = batched[0].shape[0]
    ins = [per_image(a.shape) for a in batched] + [one_layer(lay.shape, layer)]
    args = list(batched) + [lay]
    for item in shared:
        if isinstance(item, tuple):
            ins.append(one_layer(item[0].shape, item[1]))
            args.append(item[0])
        else:
            ins.append(whole(item.shape))
            args.append(item)
    out_specs = [per_image(s) for s, _ in outs]
    out_specs += [pl.BlockSpec(tuple(s), lambda i: (0, 0)) for s, _ in sums]
    arrays = [(a.shape, a.dtype) for a in args] + outs + sums
    return pl.pallas_call(
        kernel,
        grid=(images,),
        in_specs=ins,
        out_specs=out_specs,
        out_shape=[jax.ShapeDtypeStruct(s, d) for s, d in outs + sums],
        scratch_shapes=[pltpu.VMEM(s, d) for s, d in scratch],
        compiler_params=params(),
        cost_estimate=cost(flops, arrays),
        name=name,
    )(*args)


def token_mask(heights, widths):
    t = jnp.arange(4 * WTOK, dtype=jnp.int32)
    window = t // WTOK
    row = (window // 2) * WIN + (t % WTOK) // SUB
    col8 = t % SUB
    col = (window % 2) * WIN + col8
    valid = (row[None] < heights[:, None]) & (col[None] < widths[:, None]) & (col8 < WIN)[None]
    return jnp.broadcast_to(valid.astype(F32)[..., None], valid.shape + (LANES,))


def forward_window(inputs, mask, lay, sh, watt):
    images, _, _, c = inputs.shape
    t = 4 * WTOK
    outs = [
        ((images, t, c), BF16), ((images, t, c), F32), ((images, t, LANES), F32),
        ((images, t, 3 * c), BF16), ((images, t, c), BF16),
        ((images, 4, c // GROUP, WTOK, WTOK * GROUP // HD), BF16), ((images, t, c), F32),
    ]
    scratch = [((t, c), F32), ((t, c), F32), ((t, 3 * c), F32), ((t, c), F32)]
    return image_call(window_forward_kernel, "window_forward", 0, [inputs, mask], lay, [sh, watt],
                      outs, [], scratch, 10 * images * t * c * c)


def forward_mlp(x, mask, lay, hid, w_in, w_out):
    images, t, c = x.shape
    ff = w_in.shape[1]
    outs = [
        ((images, t, c), BF16), ((images, t, c), F32), ((images, t, LANES), F32),
        ((images, t, ff), BF16), ((images, t, ff), BF16), ((images, t, c), F32),
    ]
    scratch = [((t, c), F32), ((t, c), F32)]
    return image_call(mlp_forward_kernel, "mlp_forward", 1, [x, mask], lay, [(hid, 0), w_in, w_out],
                      outs, [], scratch, 4 * images * t * c * ff)


def forward_channel(x, mask, lay, sh, watt):
    images, t, c = x.shape
    outs = [
        ((images, t, c), BF16), ((images, t, c), F32), ((images, t, LANES), F32),
        ((images, t, 3 * c), BF16), ((images, t, c), BF16),
        ((images, c // GROUP, GROUP, GROUP), BF16), ((images, t, c), F32),
    ]
    return image_call(channel_forward_kernel, "channel_forward", 2, [x, mask], lay, [sh, watt],
                      outs, [], [((t, c), F32)], 9 * images * t * c * c)


def last_mlp(x, cot, mask, lay, hid, w_in, w_out):
    images, t, c = x.shape
    ff = w_in.shape[1]
    outs = [
        (cot.shape, BF16), ((images, t, c), F32), ((images, t, c), BF16), ((images, t, ff), BF16),
        ((images, t, c), BF16), ((images, t, ff), BF16),
    ]
    scratch = [
        ((t, c), F32), ((t, c), F32), ((t, LANES), F32), ((t, c), F32), ((t, c), F32), ((t, c), F32),
        ((16, c), F32), ((16 * SUB, c), F32), ((SUB, ff), F32),
    ]
    return image_call(last_mlp_kernel, "last_mlp", 3, [x, cot, mask], lay, [(hid, 1), w_in, w_out],
                      outs, [((16, c), F32), ((1, ff), F32)], scratch, 8 * images * t * c * ff)


def backward_mlp(g, x, z, r, d, mask, lay, w_in, w_out):
    images, t, c = x.shape
    ff = w_in.shape[1]
    outs = [((images, t, c), F32), ((images, t, c), BF16), ((images, t, ff), BF16)]
    scratch = [((t, c), F32), ((t, c), F32), ((16 * SUB, c), F32), ((SUB, ff), F32)]
    return image_call(mlp_backward_kernel, "mlp_backward", 1, [g, x, z, r, d, mask], lay, [w_in, w_out],
                      outs, [((16, c), F32), ((1, ff), F32)], scratch, 4 * images * t * c * ff)


def backward_channel(g, x, z, r, q, a, mask, lay, watt):
    images, t, c = x.shape
    outs = [((images, t, c), F32), ((images, t, c), BF16), ((images, t, 3 * c), BF16)]
    scratch = [((t, c), F32), ((t, c), F32), ((16 * SUB, c), F32), ((SUB, 3 * c), F32)]
    return image_call(channel_backward_kernel, "channel_backward", 2, [g, x, z, r, q, a, mask], lay, [watt],
                      outs, [((16, c), F32), ((1, 3 * c), F32)], scratch, 10 * images * t * c * c)


def backward_window(g, inputs, z, r, q, p, mask, lay, watt):
    images, t, c = g.shape
    outs = [(inputs.shape, BF16), ((images, t, c), BF16), ((images, t, 3 * c), BF16)]
    scratch = [
        ((t, c), F32), ((t, 3 * c), F32), ((t, c), F32), ((t, 3 * c), F32), ((t, c), F32), ((t, c), F32),
        ((16, c), F32), ((16 * SUB, c), F32), ((SUB, 3 * c), F32),
    ]
    return image_call(window_backward_kernel, "window_backward", 0, [g, inputs, z, r, q, p, mask], lay, [watt],
                      outs, [((16, c), F32), ((1, 3 * c), F32)], scratch, 12 * images * t * c * c)


def grad_pair_kernel(first, left0, right0, left1, right1, out0, out1):
    step = pl.program_id(0)

    @pl.when(step < first)
    def _():
        out0[...] = dot(left0[...], right0[...], DIMS_TN).astype(BF16)

    @pl.when(step >= first)
    def _():
        out1[...] = dot(left1[...], right1[...], DIMS_TN).astype(BF16)


def grad_pair(name, left0, right0, left1, right1):
    flat = [a.reshape(-1, a.shape[-1]) for a in (left0, right0, left1, right1)]
    rows, c = flat[0].shape
    first, second = flat[1].shape[1] // c, flat[3].shape[1] // c

    def at_first(i):
        return (0, jnp.minimum(i, first - 1))

    def at_second(i):
        return (0, jnp.maximum(i - first, 0))

    outs = [((c, flat[1].shape[1]), BF16), ((c, flat[3].shape[1]), BF16)]
    return pl.pallas_call(
        functools.partial(grad_pair_kernel, first),
        grid=(first + second,),
        in_specs=[
            whole((rows, c)), pl.BlockSpec((rows, c), at_first),
            whole((rows, c)), pl.BlockSpec((rows, c), at_second),
        ],
        out_specs=[pl.BlockSpec((c, c), at_first), pl.BlockSpec((c, c), at_second)],
        out_shape=[jax.ShapeDtypeStruct(s, d) for s, d in outs],
        compiler_params=params(),
        cost_estimate=cost(2 * rows * c * c * (first + second), [(a.shape, BF16) for a in flat] + outs),
        name=name,
    )(*flat)


WIDE = 8
NARROW = 4
BOTH = ("narrow", "wide")
AXES = (("wide", 2), ("wide", 4), ("wide", 1), ("narrow", 2), ("narrow", 1))
ORDERS = ((0, 1, 2, 3), (0, 1, 3, 2))
MESH_ID = pl.DeviceIdType.MESH
STAGES = (0, 4, 8, 12, 1, 5, 9, 13, 2, 6, 10, 14, 3, 7, 11, 15)


def flip(value, bit):
    return value + bit - 2 * bit * ((value // bit) % 2)


def place(order, rel):
    at = {"narrow": lax.axis_index("narrow"), "wide": lax.axis_index("wide")}
    for i, axis in enumerate(tuple(ORDERS[order]) + (4,)):
        if rel & (1 << i):
            name, bit = AXES[axis]
            at[name] = flip(at[name], bit)
    return at


def highest(rel):
    return rel.bit_length() - 1


def meet():
    barrier = pltpu.get_barrier_semaphore()
    for axis in range(5):
        order = (axis, axis, axis, axis)
        name, bit = AXES[axis]
        at = {"narrow": lax.axis_index("narrow"), "wide": lax.axis_index("wide")}
        at[name] = flip(at[name], bit)
        pl.semaphore_signal(barrier, inc=1, device_id=at, device_id_type=MESH_ID)
    pl.semaphore_wait(barrier, 5)


class Gather:
    def __init__(self, index, order, own, view, send, recv, keep):
        self.index, self.order, self.own, self.view = index, order, own, view
        self.send, self.recv, self.keep = send, recv, keep

    def ref(self, rel):
        at = place(self.order, rel)
        return self.view(at["narrow"], at["wide"])

    def copy(self, rel, axis, slot):
        target = self.ref(rel)
        return pltpu.make_async_remote_copy(
            src_ref=self.own if rel == 0 else target,
            dst_ref=target,
            send_sem=self.send.at[self.index, slot],
            recv_sem=self.recv.at[self.index, rel | (1 << axis)],
            device_id=place(self.order, 1 << axis),
            device_id_type=MESH_ID,
        )

    def arrival(self, rel):
        target = self.ref(rel)
        return pltpu.make_async_remote_copy(
            src_ref=target, dst_ref=target, send_sem=self.send.at[self.index, 0],
            recv_sem=self.recv.at[self.index, rel], device_id=place(self.order, 1), device_id_type=MESH_ID,
        )

    def sends(self, rel):
        first = highest(rel) + 1
        return [(axis, rel | (1 << axis)) for axis in range(first, 5)][::-1]

    def stage(self, rel):
        if rel == 0:
            pltpu.make_async_copy(self.own, self.ref(0), self.keep.at[self.index]).start()
        else:
            self.arrival(rel).wait_recv()
        for axis, slot in self.sends(rel):
            self.copy(rel, axis, slot).start()

    def finish(self):
        for rel in range(16, 32):
            self.arrival(rel).wait_recv()
        for rel in range(16):
            for axis, slot in self.sends(rel):
                self.copy(rel, axis, slot).wait_send()
        pltpu.make_async_copy(self.own, self.ref(0), self.keep.at[self.index]).wait()


def slot_view(ref, start, size):
    return lambda n, w: ref.at[n * WIDE + w, pl.ds(start, size), :]


def in_view(ref, rows, cols):
    return lambda n, w: ref.at[pl.ds(pl.multiple_of(n * rows, rows), rows), pl.ds(pl.multiple_of(w * cols, cols), cols)]


def out_view(ref, rows, cols):
    return lambda n, w: ref.at[pl.ds(pl.multiple_of(w * rows, rows), rows), pl.ds(pl.multiple_of(n * cols, cols), cols)]


def gather_items(pieces, firsts, seconds, wholes, in_mats, out_mats, send, recv, keep):
    items = []
    for piece, dest in zip(pieces, wholes):
        half = piece.shape[0] // 32 * 16
        rest = piece.shape[0] - half
        items.append((0, piece.at[pl.ds(0, half)], slot_view(dest, 0, half)))
        items.append((1, piece.at[pl.ds(half, rest)], slot_view(dest, half, rest)))
    for own, dest in zip(firsts, in_mats):
        items.append((0, own, in_view(dest, *own.shape)))
    for own, dest in zip(seconds, out_mats):
        items.append((1, own, out_view(dest, *own.shape)))
    return [Gather(i, order, own, view, send, recv, keep) for i, (order, own, view) in enumerate(items)]


def gather_kernel(np_, nm, *refs):
    pieces, refs = refs[:np_], refs[np_:]
    firsts, refs = refs[:nm], refs[nm:]
    seconds, refs = refs[:nm], refs[nm:]
    wholes, refs = refs[:np_], refs[np_:]
    in_mats, refs = refs[:nm], refs[nm:]
    out_mats, refs = refs[:nm], refs[nm:]
    items = gather_items(pieces, firsts, seconds, wholes, in_mats, out_mats, *refs)
    meet()
    for rel in STAGES:
        for item in items:
            item.stage(rel)
    for item in items:
        item.finish()


def gather(name, ident, pieces, firsts, seconds):
    count = 2 * len(pieces) + len(firsts) + len(seconds)
    outs = [jax.ShapeDtypeStruct((WIDE * NARROW,) + p.shape, p.dtype) for p in pieces]
    outs += [jax.ShapeDtypeStruct((NARROW * f.shape[0], WIDE * f.shape[1]), f.dtype) for f in firsts]
    outs += [jax.ShapeDtypeStruct((WIDE * s.shape[0], NARROW * s.shape[1]), s.dtype) for s in seconds]
    args = list(pieces) + list(firsts) + list(seconds)
    arrays = [(o.shape, o.dtype) for o in outs]
    return pl.pallas_call(
        functools.partial(gather_kernel, len(pieces), len(firsts)),
        in_specs=[pl.BlockSpec(memory_space=pl.ANY)] * len(args),
        out_specs=[pl.BlockSpec(memory_space=pl.ANY)] * len(outs),
        out_shape=outs,
        scratch_shapes=[
            pltpu.SemaphoreType.DMA((count, 32)), pltpu.SemaphoreType.DMA((count, 32)),
            pltpu.SemaphoreType.DMA((count,)),
        ],
        compiler_params=pltpu.CompilerParams(collective_id=ident, has_side_effects=True, vmem_limit_bytes=VMEM_LIMIT),
        cost_estimate=cost(0, arrays),
        name=name,
    )(*args)


class Reduce:
    def __init__(self, index, order, view, acc, mate, inbox, out, sems):
        self.index, self.order, self.view = index, order, view
        self.acc, self.mate, self.inbox, self.out = acc, mate, inbox, out
        self.load_sem, self.send_sem, self.mate_sem, self.recv_sem = sems

    def ref(self, rel):
        at = place(self.order, rel)
        return self.view(at["narrow"], at["wide"])

    def load(self, rel):
        return pltpu.make_async_copy(self.ref(rel), self.acc.at[rel], self.load_sem.at[self.index, rel])

    def to_mate(self, rel):
        return pltpu.make_async_remote_copy(
            src_ref=self.ref(rel | 16), dst_ref=self.mate.at[rel], send_sem=self.send_sem.at[self.index, 16 + rel],
            recv_sem=self.mate_sem.at[self.index, rel], device_id=place(self.order, 16), device_id_type=MESH_ID,
        )

    def onward(self, rel):
        return pltpu.make_async_remote_copy(
            src_ref=self.acc.at[rel], dst_ref=self.inbox.at[rel - 1], send_sem=self.send_sem.at[self.index, rel],
            recv_sem=self.recv_sem.at[self.index, rel], device_id=place(self.order, 1 << highest(rel)),
            device_id_type=MESH_ID,
        )

    def begin(self, rel):
        self.to_mate(rel).start()
        self.load(rel).start()

    def stage(self, rel):
        self.load(rel).wait()
        self.to_mate(rel).wait_recv()
        total = self.acc[rel].astype(F32) + self.mate[rel].astype(F32)
        for axis in range(highest(rel) + 1, 4):
            came = rel | (1 << axis)
            self.onward(came).wait_recv()
            total = total + self.inbox[came - 1].astype(F32)
        if rel == 0:
            self.out[...] = total
        else:
            self.acc[rel] = total.astype(BF16)
            self.onward(rel).start()

    def finish(self):
        for rel in range(16):
            self.to_mate(rel).wait_send()
            if rel:
                self.onward(rel).wait_send()


def reduce_kernel(shapes, np_, nm, *refs):
    pieces, refs = refs[:np_], refs[np_:]
    in_mats, refs = refs[:nm], refs[nm:]
    out_mats, refs = refs[:nm], refs[nm:]
    count = len(shapes)
    outs, refs = refs[:count], refs[count:]
    bufs, sems = refs[: 3 * count], refs[3 * count :]
    views = []
    for k, piece in enumerate(pieces):
        half = shapes[2 * k][0]
        views += [(0, slot_view(piece, 0, half)), (1, slot_view(piece, half, shapes[2 * k + 1][0]))]
    for k, mat in enumerate(in_mats):
        views.append((0, in_view(mat, *shapes[2 * np_ + k])))
    for k, mat in enumerate(out_mats):
        views.append((1, out_view(mat, *shapes[2 * np_ + nm + k])))
    items = [
        Reduce(i, order, view, *bufs[3 * i : 3 * i + 3], outs[i], sems) for i, (order, view) in enumerate(views)
    ]
    meet()
    for rel in reversed(STAGES):
        for item in items:
            item.begin(rel)
    for rel in reversed(STAGES):
        for item in items:
            item.stage(rel)
    for item in items:
        item.finish()


def reduce_all(name, ident, pieces, in_mats, out_mats):
    shapes = []
    for p in pieces:
        half = p.shape[1] // 32 * 16
        shapes += [(half, p.shape[2]), (p.shape[1] - half, p.shape[2])]
    shapes += [(m.shape[0] // NARROW, m.shape[1] // WIDE) for m in in_mats]
    shapes += [(m.shape[0] // WIDE, m.shape[1] // NARROW) for m in out_mats]
    count = len(shapes)
    args = list(pieces) + list(in_mats) + list(out_mats)
    scratch = []
    for s in shapes:
        scratch += [pltpu.VMEM((16,) + s, BF16), pltpu.VMEM((16,) + s, BF16), pltpu.VMEM((15,) + s, BF16)]
    scratch += [
        pltpu.SemaphoreType.DMA((count, 16)), pltpu.SemaphoreType.DMA((count, 32)),
        pltpu.SemaphoreType.DMA((count, 16)), pltpu.SemaphoreType.DMA((count, 16)),
    ]
    return pl.pallas_call(
        functools.partial(reduce_kernel, tuple(shapes), len(pieces), len(in_mats)),
        in_specs=[pl.BlockSpec(memory_space=pl.ANY)] * len(args),
        out_specs=[pl.BlockSpec(memory_space=pltpu.VMEM)] * count,
        out_shape=[jax.ShapeDtypeStruct(s, F32) for s in shapes],
        scratch_shapes=scratch,
        compiler_params=pltpu.CompilerParams(collective_id=ident, has_side_effects=True, vmem_limit_bytes=VMEM_LIMIT),
        cost_estimate=cost(0, [(a.shape, a.dtype) for a in args]),
        name=name,
    )(*args)


def copy_attention(src, start, dst):
    cn = dst.shape[0]
    cw = src.shape[2] // 4
    c = WIDE * cw
    for w in range(WIDE):
        dst[:, pl.ds(3 * cw * w, 3 * cw)] = src[w, pl.ds(start, cn), pl.ds(0, 3 * cw)]
        dst[:, pl.ds(3 * c + cw * w, cw)] = src[w, pl.ds(start, cn), pl.ds(3 * cw, cw)]


def unpack_first_kernel(got, watt, lay, sh, hid):
    copy_attention(got, 16, watt)
    cw = got.shape[2] // 4
    for w in range(WIDE):
        lay[0, :, pl.ds(cw * w, cw)] = got[w, pl.ds(0, 16), pl.ds(0, cw)].astype(F32)

    @pl.when(pl.program_id(0) == 0)
    def _():
        for w in range(WIDE):
            part = got[w, pl.ds(0, 16), pl.ds(LANES, cw)].astype(F32)
            sh[:, pl.ds(cw * w, cw)] = part
            for j in range(2):
                for q in range(4):
                    row = 5 + 4 * j + q
                    hid[j, :, pl.ds(4 * cw * w + cw * q, cw)] = part[row : row + 1]


def unpack_first(got):
    rows, lanes = got.shape[1:]
    c = 2 * lanes
    cn = c // NARROW
    outs = [((c, 4 * c), BF16), ((NARROW, 16, c), F32), ((16, c), F32), ((2, 1, 4 * c), F32)]
    return pl.pallas_call(
        unpack_first_kernel,
        grid=(NARROW,),
        in_specs=[pl.BlockSpec((WIDE, rows, lanes), lambda n: (n, 0, 0))],
        out_specs=[
            pl.BlockSpec((cn, 4 * c), lambda n: (n, 0)), pl.BlockSpec((1, 16, c), lambda n: (n, 0, 0)),
            pl.BlockSpec((16, c), lambda n: (0, 0)), pl.BlockSpec((2, 1, 4 * c), lambda n: (0, 0, 0)),
        ],
        out_shape=[jax.ShapeDtypeStruct(s, d) for s, d in outs],
        compiler_params=params(),
        cost_estimate=cost(0, [(got.shape, BF16)] + outs),
        name="unpack_first",
    )(got)


def unpack_rest_kernel(got, watt, w_in, w_out):
    cn = watt.shape[0]
    lanes = got.shape[2]
    cw = lanes // 4
    copy_attention(got, 0, watt)
    for w in range(WIDE):
        w_in[:, pl.ds(lanes * w, lanes)] = got[w, pl.ds(cn, cn), :]
        for h in range(2):
            w_out[pl.ds(cw * w, cw), pl.ds(lanes * h, lanes)] = got[w, pl.ds(2 * cn + cw * h, cw), :]


def rest_specs(rows, lanes):
    c = 2 * lanes
    cn = c // NARROW
    packed = pl.BlockSpec((WIDE, rows, lanes), lambda n: (n, 0, 0))
    flat = pl.BlockSpec((cn, 4 * c), lambda n: (n, 0))
    return packed, [flat, flat, pl.BlockSpec((c, c), lambda n: (0, n))], (c, 4 * c)


def unpack_rest(got):
    packed, mats, shape = rest_specs(*got.shape[1:])
    return pl.pallas_call(
        unpack_rest_kernel,
        grid=(NARROW,),
        in_specs=[packed],
        out_specs=mats,
        out_shape=[jax.ShapeDtypeStruct(shape, BF16)] * 3,
        compiler_params=params(),
        cost_estimate=cost(0, [(got.shape, BF16)] * 2),
        name="unpack_rest",
    )(got)


def gather_attention(gq, gp, start, dst):
    cn = gq.shape[0]
    cw = dst.shape[2] // 4
    for w in range(WIDE):
        dst[w, pl.ds(start, cn), pl.ds(0, 3 * cw)] = gq[:, pl.ds(3 * cw * w, 3 * cw)]
        dst[w, pl.ds(start, cn), pl.ds(3 * cw, cw)] = gp[:, pl.ds(cw * w, cw)]


def pack_rest_kernel(gq, gp, g_in, g_out, out):
    cn = gq.shape[0]
    lanes = out.shape[2]
    cw = lanes // 4
    gather_attention(gq, gp, 0, out)
    for w in range(WIDE):
        out[w, pl.ds(cn, cn), :] = g_in[:, pl.ds(lanes * w, lanes)]
        for h in range(2):
            out[w, pl.ds(2 * cn + cw * h, cw), :] = g_out[pl.ds(cw * w, cw), pl.ds(lanes * h, lanes)]


def pack_rest(gq, gp, g_in, g_out):
    c = gp.shape[0]
    cn, lanes = c // NARROW, c // 2
    rows = 3 * cn
    packed, mats, _ = rest_specs(rows, lanes)
    shape = (WIDE * NARROW, rows, lanes)
    return pl.pallas_call(
        pack_rest_kernel,
        grid=(NARROW,),
        in_specs=[pl.BlockSpec((cn, 3 * c), lambda n: (n, 0)), pl.BlockSpec((cn, c), lambda n: (n, 0)), mats[1], mats[2]],
        out_specs=packed,
        out_shape=jax.ShapeDtypeStruct(shape, BF16),
        compiler_params=params(),
        cost_estimate=cost(0, [(shape, BF16)] * 2),
        name="pack_rest",
    )(gq, gp, g_in, g_out)


def pack_first_kernel(gq, gp, small, sb, cb, hid0, hid1, out, shared):
    gather_attention(gq, gp, 16, out)
    c = gp.shape[1]
    cw = c // WIDE

    @pl.when(pl.program_id(0) == 0)
    def _():
        shared[...] = jnp.zeros_like(shared)
        shared[pl.ds(0, 1), :] = sb[:, pl.ds(0, c)]
        shared[pl.ds(1, 1), :] = sb[:, pl.ds(2 * c, c)]
        for k in range(3):
            shared[pl.ds(2 + k, 1), :] = cb[:, pl.ds(k * c, c)]
        for j, hid in enumerate((hid0, hid1)):
            for w in range(WIDE):
                for q in range(4):
                    shared[pl.ds(5 + 4 * j + q, 1), pl.ds(cw * w, cw)] = hid[:, pl.ds(4 * cw * w + cw * q, cw)]

    out[:, pl.ds(0, 16), :] = jnp.zeros((WIDE, 16, out.shape[2]), BF16)
    for w in range(WIDE):
        out[w, pl.ds(0, 16), pl.ds(0, cw)] = small[0, :, pl.ds(cw * w, cw)].astype(BF16)
        out[w, pl.ds(0, 16), pl.ds(LANES, cw)] = shared[:, pl.ds(cw * w, cw)].astype(BF16)


def pack_first(gq, gp, small, sb, cb, hid0, hid1):
    c = gp.shape[0]
    cn, lanes = c // NARROW, c // 2
    rows = cn + 16
    shape = (WIDE * NARROW, rows, lanes)
    return pl.pallas_call(
        pack_first_kernel,
        grid=(NARROW,),
        in_specs=[
            pl.BlockSpec((cn, 3 * c), lambda n: (n, 0)), pl.BlockSpec((cn, c), lambda n: (n, 0)),
            pl.BlockSpec((1, 16, c), lambda n: (n, 0, 0)),
        ] + [whole(a.shape) for a in (sb, cb, hid0, hid1)],
        out_specs=pl.BlockSpec((WIDE, rows, lanes), lambda n: (n, 0, 0)),
        out_shape=jax.ShapeDtypeStruct(shape, BF16),
        scratch_shapes=[pltpu.VMEM((16, c), F32)],
        compiler_params=params(),
        cost_estimate=cost(0, [(shape, BF16)] * 2),
        name="pack_first",
    )(gq, gp, small, sb, cb, hid0, hid1)


def attention_piece(qkv, proj):
    return jnp.concatenate([qkv.T, proj.T], axis=1)


def halves_piece(second, rows, lanes):
    return second.reshape(second.shape[0], -1, lanes).transpose(1, 0, 2).reshape(rows, lanes)


def pad_to(item, rows, lanes):
    return jnp.pad(item, ((0, rows - item.shape[0]), (0, lanes - item.shape[1])))


def small_rows(conv_weight, conv_bias, norm_gain, norm_bias, out_bias):
    return jnp.concatenate([conv_weight[0], conv_bias, norm_gain, norm_bias, out_bias])


def shared_rows(attn_bias, hidden_bias):
    return jnp.concatenate([attn_bias, hidden_bias.reshape(-1, attn_bias.shape[1])])


class Direct:
    def __init__(self, p):
        lanes = p["spatial_qkv"].shape[0] * 4 // 3
        small = pad_to(small_rows(p["conv_weight"], p["conv_bias"], p["norm_gain"], p["norm_bias"], p["out_bias"]), 16, LANES)
        shared = pad_to(shared_rows(p["attn_bias"], p["hidden_bias"]), 16, LANES)
        head = pad_to(jnp.concatenate([small, shared], axis=1), 16, lanes)
        first = jnp.concatenate([head, attention_piece(p["spatial_qkv"], p["projection"][0])])
        rows = p["spatial_qkv"].shape[1]
        rest = jnp.concatenate([
            attention_piece(p["channel_qkv"], p["projection"][1]), p["mlp_in"][1].T,
            halves_piece(p["mlp_out"][1], rows, lanes),
        ])
        rest = lax.all_gather(rest, BOTH, axis=0, tiled=False)
        got, win0, wout0 = gather("gather_first", 1, [first], [p["mlp_in"][0].T], [p["mlp_out"][0]])
        watt0, self.lay, self.sh, self.hid = unpack_first(got)
        watt1, win1, wout1 = unpack_rest(rest)
        self.watt, self.w_in, self.w_out = (watt0, watt1), (win0, win1), (wout0, wout1)

    def reduce_rest(self, gq, gp, g_in, g_out):
        packed = pack_rest(gq, gp, g_in, g_out)
        packed = packed.reshape(-1, packed.shape[2])
        self.rest = lax.psum_scatter(packed, BOTH, scatter_dimension=0, tiled=True)

    def reduce_first(self, gq, gp, g_in, g_out, smalls, sb, cb, hid0, hid1):
        c = gp.shape[0]
        cn, lanes, cw = c // NARROW, c // 2, c // WIDE
        packed = pack_first(gq, gp, jnp.stack(smalls), sb, cb, hid0, hid1)
        low, high, gi0, go0 = reduce_all("reduce_first", 2, [packed], [g_in], [g_out])
        att0 = jnp.concatenate([low[16:], high])
        rest = self.rest.astype(F32)
        att1, gi1 = rest[:cn], rest[cn : 2 * cn]
        go1 = rest[2 * cn :].reshape(2, cw, lanes).transpose(1, 0, 2).reshape(cw, 2 * lanes)
        small, shared = low[:16, :cw], low[:16, LANES : LANES + cw]
        proj = jnp.stack([att0[:, 3 * cw :].T, att1[:, 3 * cw :].T])
        return (
            small[None, :9], small[9:10], small[10:11], small[11:12], att0[:, : 3 * cw].T, att1[:, : 3 * cw].T,
            proj, jnp.stack([gi0.T, gi1.T]), jnp.stack([go0, go1]), shared[:5], shared[5:13].reshape(2, lanes),
            small[12:13],
        )


class Plain:
    def __init__(self, p):
        self.layers, self.cw = p["conv_bias"].shape
        wide = p["attn_bias"].shape
        self.narrow = 4 // self.layers
        self.cn = p["spatial_qkv"].shape[1]
        self.c = self.cn * self.narrow
        self.wide = self.c // self.cw
        self.fw = p["hidden_bias"].shape[1]
        c, cn, cw, fw, n, w = self.c, self.cn, self.cw, self.fw, self.narrow, self.wide

        def spread(v):
            return lax.all_gather(v, BOTH, axis=0, tiled=False).reshape((n, w) + v.shape)

        def attention(qkv, proj):
            got = spread(attention_piece(qkv, proj)).transpose(0, 2, 1, 3)
            return jnp.concatenate([got[..., : 3 * cw].reshape(c, 3 * c), got[..., 3 * cw :].reshape(c, c)], axis=1)

        self.watt = tuple(attention(p[k], p["projection"][i]) for i, k in enumerate(("spatial_qkv", "channel_qkv")))
        self.w_in = tuple(spread(p["mlp_in"][i].T).transpose(0, 2, 1, 3).reshape(c, -1) for i in range(2))
        self.w_out = tuple(spread(p["mlp_out"][i]).transpose(1, 2, 0, 3).reshape(c, -1) for i in range(2))

        def layer(v):
            return spread(v).transpose(0, 2, 3, 1, 4).reshape(4, -1, c)

        rows = [layer(p["conv_weight"])]
        rows += [layer(p[k][:, None]) for k in ("conv_bias", "norm_gain", "norm_bias", "out_bias")]
        self.lay = jnp.pad(jnp.concatenate(rows, axis=1).astype(F32), ((0, 0), (0, 3), (0, 0)))
        attn = spread(p["attn_bias"])[0].transpose(1, 0, 2).reshape(5, c)
        self.sh = jnp.pad(attn.astype(F32), ((0, 11), (0, 0)))
        self.hid = spread(p["hidden_bias"])[0].transpose(1, 0, 2).reshape(2, 1, -1).astype(F32)

    def matrix(self, grad, rows_wide):
        n, w = self.narrow, self.wide
        a, b = (w, n) if rows_wide else (n, w)
        grad = grad.reshape(a, grad.shape[0] // a, b, grad.shape[1] // b)
        grad = grad.transpose(2, 0, 1, 3) if rows_wide else grad.transpose(0, 2, 1, 3)
        grad = grad.astype(BF16).reshape(n * w * grad.shape[2], grad.shape[3])
        return lax.psum_scatter(grad, BOTH, scatter_dimension=0, tiled=True).astype(F32)

    def reduce_rest(self, gq, gp, g_in, g_out):
        self.rest = (self.matrix(gq, False), self.matrix(gp, False), self.matrix(g_in, False), self.matrix(g_out, True))

    def reduce_first(self, gq, gp, g_in, g_out, smalls, sb, cb, hid0, hid1):
        c, cw, fw, n, w = self.c, self.cw, self.fw, self.narrow, self.wide
        first = (self.matrix(gq, False), self.matrix(gp, False), self.matrix(g_in, False), self.matrix(g_out, True))
        small = jnp.stack(smalls).reshape(n, self.layers * 16, w, cw).transpose(0, 2, 1, 3)
        attn = jnp.concatenate([sb[:, :c], sb[:, 2 * c :], cb.reshape(3, c)]).reshape(5, w, cw).transpose(1, 0, 2)
        hid = jnp.concatenate([hid0, hid1]).reshape(2, w, fw).transpose(1, 0, 2).reshape(w, -1, cw)
        common = jnp.concatenate([attn, hid], axis=1)
        common = jnp.broadcast_to(common[None], (n,) + common.shape)
        flat = jnp.concatenate([small, common], axis=2).astype(BF16).reshape(-1, cw)
        got = lax.psum_scatter(flat, BOTH, scatter_dimension=0, tiled=True).astype(F32)
        small = got[: self.layers * 16].reshape(self.layers, 16, cw)
        shared = got[self.layers * 16 :]
        rest = self.rest
        return (
            small[:, :9], small[:, 9], small[:, 10], small[:, 11], first[0].T, rest[0].T,
            jnp.stack([first[1].T, rest[1].T]), jnp.stack([first[2].T, rest[2].T]), jnp.stack([first[3], rest[3]]),
            shared[:5], shared[5:].reshape(2, fw), small[:, 12],
        )


NAMES = (
    "conv_weight", "conv_bias", "norm_gain", "norm_bias", "spatial_qkv", "channel_qkv", "projection", "mlp_in",
    "mlp_out", "attn_bias", "hidden_bias", "out_bias",
)


def local(plan, inputs, heights, widths, *rest):
    weights = plan(dict(zip(NAMES, rest[:-1])))
    cotangent = rest[-1]
    lay, sh, hid = weights.lay, weights.sh, weights.hid
    mask = token_mask(heights, widths)
    n1, z1, r1, q1, o1, p1, x2 = forward_window(inputs, mask, lay, sh, weights.watt[0])
    n2, z2, r2, u1, d1, x4 = forward_mlp(x2, mask, lay, hid, weights.w_in[0], weights.w_out[0])
    n3, z3, r3, q3, o3, a3, x6 = forward_channel(x4, mask, lay, sh, weights.watt[1])
    out, g6, n4, u2, gy2, gh2, small3, hid1 = last_mlp(
        x6, cotangent, mask, lay, hid, weights.w_in[1], weights.w_out[1])
    gi1, go1 = grad_pair("last_mlp_grads", n4, gh2, gy2, u2)
    g4, ga3, dq3, small2, cb = backward_channel(g6, x4, z3, r3, q3, a3, mask, lay, weights.watt[1])
    gq1, gp1 = grad_pair("channel_grads", n3, dq3, o3, ga3)
    weights.reduce_rest(gq1, gp1, gi1, go1)
    g2, gy1, gh1, small1, hid0 = backward_mlp(g4, x2, z2, r2, d1, mask, lay, weights.w_in[0], weights.w_out[0])
    gi0, go0 = grad_pair("mlp_grads", n2, gh1, gy1, u1)
    input_grad, ga1, dq1, small0, sb = backward_window(g2, inputs, z1, r1, q1, p1, mask, lay, weights.watt[0])
    gq0, gp0 = grad_pair("window_grads", n1, dq1, o1, ga1)
    grads = weights.reduce_first(gq0, gp0, gi0, go0, (small0, small1, small2, small3), sb, cb, hid0, hid1)
    return (out, input_grad) + grads


def solution(mesh):
    matrix = P("wide", "narrow")
    cells = P(("wide", "narrow"), None, None, None)
    stacked = P(None, "wide", "narrow")
    row = P("narrow", "wide")
    shared = P(None, "wide")
    images = P(("wide", "narrow"))
    kernels = P("narrow", None, "wide")
    in_specs = (
        cells, images, images, kernels, row, row, row, matrix, matrix,
        stacked, stacked, stacked, shared, shared, row, cells,
    )
    out_specs = (
        cells, cells, kernels, row, row, row, matrix, matrix, stacked, stacked, stacked, shared, shared, row,
    )
    plan = Direct if (mesh.shape["wide"], mesh.shape["narrow"]) == (WIDE, NARROW) else Plain
    body = functools.partial(local, plan)
    return jax.shard_map(body, mesh=mesh, in_specs=in_specs, out_specs=out_specs, check_vma=False)
```

time: 1270 us -> 676 us (0.53)
  waiting for transfers between devices: 360 us -> 0.05 us
  local copies, waits for them, and re-layouts: 270 us -> 28.9 us
  Pallas kernels: 500 us -> 623 us
  matrix products: 82.9 us -> 0 us
  other arithmetic: 35.7 us -> 6.12 us
    pallas_call x0 -> x10, Pallas kernels: none -> 287 us  [the longest x1 98.7 us: gather(): pl.pallas_call(functools.partial(gather_kernel, len(pieces), len(firsts))...]
    reduce_scatter x4 -> x1, waiting for transfers between devices: 247 us -> 0.01 us  [reduce_rest(): self.rest = lax.psum_scatter(packed, BOTH, scatter_dimension=0, tiled=True)]
    pallas_call x7, Pallas kernels: 500 us -> 335 us  [image_call(): pl.pallas_call(kernel, grid=(images,), in_specs=ins, out_specs=out_specs,...]
    all_gather x4 -> x1, waiting for transfers between devices: 113 us -> 0.01 us  [__init__(): rest = lax.all_gather(rest, BOTH, axis=0, tiled=False)]
    reshape x32 -> x3, local copies, waits for them, and re-layouts: 113 us -> 1.65 us  [the longest x1 0.77 us: shared_rows(): hidden_bias.reshape(-1, attn_bias.shape[1])]
    dot_general x8 -> x0, matrix products: 82.9 us -> none  [dot(): return lax.dot_general(a, b, dims, preferred_element_type=F32)]
    slice x31 -> x7, local copies, waits for them, and re-layouts: 50.4 us -> 7.95 us  [the longest x1 1.66 us: __init__(): p['mlp_out'][1]]
    transpose x13 -> x3, local copies, waits for them, and re-layouts: 38.8 us -> 1.72 us  [the longest x1 1.68 us: __init__(): p['mlp_in'][1]]
  transfers between devices with their start and end apart: 8 -> 2, of which waited for: 5 -> 0; matrix products, arithmetic and copies ran while one was open for 24% -> 3% of each run, Pallas kernels for 18% -> 63%
where the time goes in v2:
time: 676 us; the launch traced here: 673 us
  Pallas kernels  623 us (92%)
  local copies, waits for them, and re-layouts  28.9 us (4%)
  between operations  14.8 us (2%)
    pallas_call x7, Pallas kernels, image_call(): pl.pallas_call(kernel, grid=(images,), in_specs=ins, out_specs=out_specs,...  335 us
    pallas_call x1, Pallas kernels, gather(): pl.pallas_call(functools.partial(gather_kernel, len(pieces), len(firsts))...  98.7 us
    pallas_call x4, Pallas kernels, grad_pair(): pl.pallas_call(functools.partial(grad_pair_kernel, first), grid=(first +...  81.6 us
    pallas_call x1, Pallas kernels, reduce_all(): pl.pallas_call(functools.partial(reduce_kernel, tuple(shapes), len(pieces...  71.8 us
    unnamed x48, local copies, waits for them, and re-layouts  15.3 us
  transfers between devices with their start and end apart: 2, of which 0 were waited for; matrix products, arithmetic and copies ran while one was open for 3% of the time, Pallas kernels for 63%

profile of v2, /device:TPU:0, one launch (start us, length us, event | category | flops | bytes accessed | tf_op | source)
XLA Modules:
  0.0 672.5 jit_solution(6952608618926918800)
XLA Ops:
  7.2 1.0 fusion.18
  8.3 1.1 copy.33
  9.4 1.7 slice_bitcast_fusion.2
  11.1 1.7 fusion.16
  12.8 0.9 pad_maximum_fusion.2
  13.7 0.8 reshape.237
  14.5 0.1 copy.45
  14.6 1.1 copy.30
  15.8 2.1 copy.32.inp
  17.9 2.1 copy.36.cot
  20.1 0.8 fusion.1.refs_0_
  20.8 98.7 %gather_first.1 = (bf16[32,208,384]{2,1,0:T(8,128)(2,1)}, bf16[768,3072]{1,0:T(8,128)(2,1)}, bf16[768,3072]{1,0:T(8,128)(2,1)}) custom-call(bf16[208,384]{1,0:T(8,128)(2,1)} %fusion.1.refs_0_, bf16[192,384]{1,0:T(8,128)(2,1)} %get-tuple-element.159.refs_1_, bf16[96,768]{1,0:T(8,128)(2,1)} %get-tuple-element.161.refs_2_), custom_call_target="tpu_custom_call" | custom-call | bytes 14548992 | tf_op jit(solution)/shard_map/gather_first/pallas_call | solution.py:783
  119.6 6.7 unpack_first.1
  126.4 1.2 broadcast_in_dim.4.mask
  127.6 53.3 %window_forward.1 = (bf16[8,224,768]{2,1,0:T(8,128)(2,1)}, f32[8,224,768]{2,1,0:T(8,128)}, f32[8,224,128]{2,1,0:T(8,128)}, bf16[8,224,2304]{2,1,0:T(8,128)(2,1)}...) custom-call(bf16[8,14,14,768]{3,2,1,0:T(8,128)(2,1)} %copy.32.inp, ...), custom_call_target="tpu_custom_call" | custom-call | flops 10569646080 | bytes 38797312 | tf_op jit(solution)/shard_map/window_forward/pallas_call | solution.py:508
  180.9 36.1 %mlp_forward.1 = (bf16[8,224,768]{2,1,0:T(8,128)(2,1)}, f32[8,224,768]{2,1,0:T(8,128)}, f32[8,224,128]{2,1,0:T(8,128)}, bf16[8,224,3072]{2,1,0:T(8,128)(2,1)}, b...) custom-call(f32[8,224,768]{2,1,0:T(8,128)} %get-tuple-element.83.x_in, f32[8,224,128]{2,1,0:T(8,128)} %broadcast_in_dim.4.mask, ...), custom_call_target="tpu_custom_call" | custom-call | flops 16911433728 | bytes 52781056 | tf_op jit(solution)/shard_map/mlp_forward/pallas_call | solution.py:508
  217.0 10.7 %unpack_rest.1 = (bf16[768,3072]{1,0:T(8,128)(2,1)}, bf16[768,3072]{1,0:T(8,128)(2,1)}, bf16[768,3072]{1,0:T(8,128)(2,1)}) custom-call(bf16[32,576,384]{2,1,0:T(8,128)(2,1)} %bitcast.70), custom_call_target="tpu_custom_call" | custom-call | bytes 28311552 | tf_op jit(solution)/shard_map/unpack_rest/pallas_call | solution.py:973
  227.7 27.1 %channel_forward.1 = (bf16[8,224,768]{2,1,0:T(8,128)(2,1)}, f32[8,224,768]{2,1,0:T(8,128)}, f32[8,224,128]{2,1,0:T(8,128)}, bf16[8,224,2304]{2,1,0:T(8,128)(2,1)...) custom-call(f32[8,224,768]{2,1,0:T(8,128)} %get-tuple-element.87.x_in, ...), custom_call_target="tpu_custom_call" | custom-call | flops 9512681472 | bytes 40222720 | tf_op jit(solution)/shard_map/channel_forward/pallas_call | solution.py:508
  254.8 71.0 %last_mlp.1 = (bf16[8,14,14,768]{3,2,1,0:T(8,128)(2,1)}, f32[8,224,768]{2,1,0:T(8,128)}, bf16[8,224,768]{2,1,0:T(8,128)(2,1)}, bf16[8,224,3072]{2,1,0:T(8,128)(2...) custom-call(f32[8,224,768]{2,1,0:T(8,128)} %get-tuple-element.89.x_in, ...), custom_call_target="tpu_custom_call" | custom-call | flops 33822867456 | bytes 53989376 | tf_op jit(solution)/shard_map/last_mlp/pallas_call | solution.py:508
  325.8 37.6 %channel_backward.1 = (f32[8,224,768]{2,1,0:T(8,128)}, bf16[8,224,768]{2,1,0:T(8,128)(2,1)}, bf16[8,224,2304]{2,1,0:T(8,128)(2,1)}, f32[16,768]{1,0:T(8,128)}, f32[1,2304]{1,0:T(1,128)}) custom-call(f32[8,224,768]{2,1,0:T(8,128)} %get-tuple-element.93.g_in, f32[8,224,768]{2,1,0:T(8,128)} %get-tuple-element.87.x_in, f32[8,224,768]{2,1,0:T(8,128)} %get-tuple-element.94.z_in, ...), custom_call_target="tpu_custom_call" | custom-call | flops 10569646080 | bytes 51241984 | tf_op jit(solution)/shard_map/channel_backward/pallas_call | solution.py:508
  363.4 15.4 %channel_grads.1 = (bf16[768,2304]{1,0:T(8,128)(2,1)}, bf16[768,768]{1,0:T(8,128)(2,1)}) custom-call(bf16[1792,768]{1,0:T(8,128)(2,1)} %bitcast.98, bf16[1792,2304]{1,0:T(8,128)(2,1)} %bitcast.91, bf16[1792,768]{1,0:T(8,128)(2,1)} %bitcast.99, bf16[1792,768]{1,0:T(8,128)(2,1)} %bitcast.101), custom_call_target="tpu_custom_call" | custom-call | flops 8455716864 | bytes 21233664 | tf_op jit(solution)/shard_map/channel_grads/pallas_call | solution.py:634
  378.8 25.0 %last_mlp_grads.1 = (bf16[768,3072]{1,0:T(8,128)(2,1)}, bf16[768,3072]{1,0:T(8,128)(2,1)}) custom-call(bf16[1792,768]{1,0:T(8,128)(2,1)} %bitcast.96, bf16[1792,3072]{1,0:T(8,128)(2,1)} %bitcast.89, bf16[1792,768]{1,0:T(8,128)(2,1)} %bitcast.97, bf16[1792,3072]{1,0:T(8,128)(2,1)} %bitcast.88), custom_call_target="tpu_custom_call" | custom-call | flops 16911433728 | bytes 36962304 | tf_op jit(solution)/shard_map/last_mlp_grads/pallas_call | solution.py:634
  403.8 11.0 %pack_rest.1 = bf16[32,576,384]{2,1,0:T(8,128)(2,1)} custom-call(bf16[768,2304]{1,0:T(8,128)(2,1)} %get-tuple-element.134.gq, bf16[768,768]{1,0:T(8,128)(2,1)} %get-tuple-element.135.gp, bf16[768,3072]{1,0:T(8,128)(2,1)} %get-tuple-element.140.g_in, bf16[768,3072]{1,0:T(8,128)(2,1)} %get-tuple-element.141.g_out), custom_call_target="tpu_custom_call" | custom-call | bytes 28311552 | tf_op jit(solution)/shard_map/pack_rest/pallas_call | solution.py:1010
  414.8 38.6 %mlp_backward.1 = (f32[8,224,768]{2,1,0:T(8,128)}, bf16[8,224,768]{2,1,0:T(8,128)(2,1)}, bf16[8,224,3072]{2,1,0:T(8,128)(2,1)}, f32[16,768]{1,0:T(8,128)}, f32[1,3072]{1,0:T(1,128)}) custom-call(f32[8,224,768]{2,1,0:T(8,128)} %get-tuple-element.98.g_in, f32[8,224,768]{2,1,0:T(8,128)} %get-tuple-element.83.x_in, f32[8,224,768]{2,1,0:T(8,128)} %get-tuple-element.99.z_in, ...), custom_call_target="tpu_custom_call" | custom-call | flops 16911433728 | bytes 58322944 | tf_op jit(solution)/shard_map/mlp_backward/pallas_call | solution.py:508
  453.4 71.7 %window_backward.1 = (bf16[8,14,14,768]{3,2,1,0:T(8,128)(2,1)}, bf16[8,224,768]{2,1,0:T(8,128)(2,1)}, bf16[8,224,2304]{2,1,0:T(8,128)(2,1)}, f32[16,768]{1,0:T(8,128)}, f32[1,2304]{1,0:T(1,128)}) custom-call(f32[8,224,768]{2,1,0:T(8,128)} %get-tuple-element.102.g_in, bf16[8,14,14,768]{3,2,1,0:T(8,128)(2,1)} %copy.32.inp, ...), custom_call_target="tpu_custom_call" | custom-call | flops 12683575296 | bytes 46720000 | tf_op jit(solution)/shard_map/window_backward/pallas_call | solution.py:508
  525.2 1.5 pad_maximum_fusion.3.small
  526.7 16.0 %window_grads.1 = (bf16[768,2304]{1,0:T(8,128)(2,1)}, bf16[768,768]{1,0:T(8,128)(2,1)}) custom-call(bf16[1792,768]{1,0:T(8,128)(2,1)} %bitcast.93, bf16[1792,2304]{1,0:T(8,128)(2,1)} %bitcast.90, bf16[1792,768]{1,0:T(8,128)(2,1)} %bitcast.94, bf16[1792,768]{1,0:T(8,128)(2,1)} %bitcast.100), custom_call_target="tpu_custom_call" | custom-call | flops 8455716864 | bytes 21233664 | tf_op jit(solution)/shard_map/window_grads/pallas_call | solution.py:634
  542.6 6.6 pack_first.1.refs_0_
  549.2 25.3 %mlp_grads.1 = (bf16[768,3072]{1,0:T(8,128)(2,1)}, bf16[768,3072]{1,0:T(8,128)(2,1)}) custom-call(bf16[1792,768]{1,0:T(8,128)(2,1)} %bitcast.92, bf16[1792,3072]{1,0:T(8,128)(2,1)} %bitcast.87, bf16[1792,768]{1,0:T(8,128)(2,1)} %bitcast.95, bf16[1792,3072]{1,0:T(8,128)(2,1)} %bitcast.86), custom_call_target="tpu_custom_call" | custom-call | flops 16911433728 | bytes 36962304 | tf_op jit(solution)/shard_map/mlp_grads/pallas_call | solution.py:634
  574.5 71.8 %reduce_first.1 = (f32[96,384]{1,0:T(8,128)}, f32[112,384]{1,0:T(8,128)}, f32[192,384]{1,0:T(8,128)}, f32[96,768]{1,0:T(8,128)}) custom-call(bf16[32,208,384]{2,1,0:T(8,128)(2,1)} %pack_first.1.refs_0_, bf16[768,3072]{1,0:T(8,128)(2,1)} %get-tuple-element.126.refs_1_, bf16[768,3072]{1,0:T(8,128)(2,1)} %get-tuple-element.127.refs_2_), custom_call_target="tpu_custom_call" | custom-call | bytes 14548992 | tf_op jit(solution)/shard_map/reduce_first/pallas_call | solution.py:894
  646.4 0.9 slice.90
  647.2 1.3 slice.89
  648.5 0.9 slice.82
  649.4 2.7 copy.39
  652.2 2.7 copy.40
  654.9 0.7 reshape.257
  655.6 0.7 slice_bitcast_fusion.6
  656.3 0.6 copy.41
  656.9 0.9 copy.42
  657.9 1.4 fusion.17
  659.2 1.1 convert_element_type.16
  660.4 0.9 slice.97
  661.4 0.2 copy.48
  661.6 0.2 stack_reshape.3
  661.9 0.8 copy.44
  662.7 0.9 copy.43
  663.5 0.9 pad_maximum_fusion.1
  664.4 0.9 pad_maximum_fusion
  (57 shorter events, 0.8 us)
Async XLA Ops:
  7.2 8.5 %copy-start.2 = (bf16[8,14,14,768]{3,0,2,1:T(8,128)(2,1)S(1)}, bf16[8,14,14,768]{3,0,2,1:T(8,128)(2,1)}, u32[]{:S(2)}) copy-start(bf16[8,14,14,768]{3,0,2,1:T(8,128)(2,1)} %param.16) | copy-start | bytes 7225348
  7.2 209.8 %all-gather.3.cloned.1.call-start = ((), (), s32[]{:S(2)}) async-start(), calls=%async_computation.2 | async-start | bytes 14598144 | tf_op jit(solution)/shard_map/all_gather | solution.py:1098
  13.7 645.5 %reduce-scatter.2.cloned.1.call-start = ((), (), s32[]{:S(2)}) async-start(), calls=%async_computation.1 | async-start | bytes 14598144 | tf_op jit(solution)/shard_map/reduce_scatter | solution.py:1107
  15.7 2.2 copy-start.3
  15.7 4.3 copy-start.10
  15.7 4.3 copy-start.12
  15.7 4.3 copy-start.13
  15.7 4.3 copy-start.14
  15.7 4.3 copy-start.15
  15.7 4.3 copy-start.11
  17.9 108.4 %copy-start.16 = (s32[8]{0:T(128)S(1)}, s32[8]{0:T(128)}, u32[]{:S(2)}) copy-start(s32[8]{0:T(128)} %param.18) | copy-start | bytes 100
  17.9 108.4 %copy-start.17 = (s32[8]{0:T(128)S(1)}, s32[8]{0:T(128)}, u32[]{:S(2)}) copy-start(s32[8]{0:T(128)} %param.17) | copy-start | bytes 100
  453.4 71.8 %copy-start.7 = (f32[16,768]{1,0:T(8,128)S(1)}, f32[16,768]{1,0:T(8,128)}, u32[]{:S(2)}) copy-start(f32[16,768]{1,0:T(8,128)} %get-tuple-element.117) | copy-start | bytes 147460
  453.4 71.8 %copy-start.8 = (f32[16,768]{1,0:T(8,128)S(1)}, f32[16,768]{1,0:T(8,128)}, u32[]{:S(2)}) copy-start(f32[16,768]{1,0:T(8,128)} %get-tuple-element.116) | copy-start | bytes 147460
  453.4 71.8 %copy-start.9 = (f32[16,768]{1,0:T(8,128)S(1)}, f32[16,768]{1,0:T(8,128)}, u32[]{:S(2)}) copy-start(f32[16,768]{1,0:T(8,128)} %get-tuple-element.115) | copy-start | bytes 147460
  574.5 74.9 %copy-start = (bf16[8,14,14,768]{3,2,1,0:T(8,128)(2,1)S(1)}, bf16[8,14,14,768]{3,2,1,0:T(8,128)(2,1)}, u32[]{:S(2)}) copy-start(bf16[8,14,14,768]{3,2,1,0:T(8,128)(2,1)} %get-tuple-element.144) | copy-start | bytes 7225348
  646.4 5.8 copy-start.1
  649.4 7.5 %copy-start.4 = (f32[112,384]{1,0:T(8,128)S(1)}, f32[112,384]{1,0:T(8,128)}, u32[]{:S(2)}) copy-start(f32[112,384]{1,0:T(8,128)} %get-tuple-element.129) | copy-start | bytes 516100
  654.9 8.6 %copy-start.6 = (f32[96,768]{1,0:T(8,128)S(1)}, f32[96,768]{1,0:T(8,128)}, u32[]{:S(2)}) copy-start(f32[96,768]{1,0:T(8,128)} %get-tuple-element.143) | copy-start | bytes 884740
  654.9 9.5 %copy-start.5 = (f32[192,384]{1,0:T(8,128)S(1)}, f32[192,384]{1,0:T(8,128)}, u32[]{:S(2)}) copy-start(f32[192,384]{1,0:T(8,128)} %get-tuple-element.142) | copy-start | bytes 884740
Sparse Core Ops, SparseCore 0:
  13.8 137.0 all-gather.2
  414.9 161.9 reduce-scatter.1

commit v3 on v2

--- a/solution.py
+++ b/solution.py
@@ -491,7 +491,19 @@
     return pltpu.CompilerParams(dimension_semantics=("arbitrary",), vmem_limit_bytes=VMEM_LIMIT)
 
 
-def image_call(kernel, name, layer, batched, lay, shared, outs, sums, scratch, flops):
+def carrier(kernel, carry, ins, outs, scratch, refs):
+    extra_in, extra_out = len(carry.args), len(carry.outs)
+    base_in, refs = refs[:ins], refs[ins:]
+    carry_in, refs = refs[:extra_in], refs[extra_in:]
+    base_out, refs = refs[:outs], refs[outs:]
+    carry_out, refs = refs[:extra_out], refs[extra_out:]
+    base_scratch, carry_scratch = refs[:scratch], refs[scratch:]
+    carry.run(carry_in, carry_out, carry_scratch)
+    kernel(*base_in, *base_out, *base_scratch)
+    carry.end(carry_in, carry_out, carry_scratch)
+
+
+def image_call(kernel, name, layer, batched, lay, shared, outs, sums, scratch, flops, carry=None):
     images = batched[0].shape[0]
     ins = [per_image(a.shape) for a in batched] + [one_layer(lay.shape, layer)]
     args = list(batched) + [lay]
@@ -504,15 +516,34 @@
             args.append(item)
     out_specs = [per_image(s) for s, _ in outs]
     out_specs += [pl.BlockSpec(tuple(s), lambda i: (0, 0)) for s, _ in sums]
-    arrays = [(a.shape, a.dtype) for a in args] + outs + sums
+    results = outs + sums
+    buffers = [pltpu.VMEM(s, d) for s, d in scratch]
+    options = params()
+    body = kernel
+    if carry is not None:
+        counts = (len(args), len(results), len(scratch))
+
+        def body(*refs):
+            carrier(kernel, carry, *counts, refs)
+
+        args = args + carry.args
+        ins = ins + [pl.BlockSpec(memory_space=pl.ANY)] * len(carry.args)
+        out_specs += [carry.out_spec or pl.BlockSpec(tuple(s), lambda i: (0, 0)) for s, _ in carry.outs]
+        results = results + carry.outs
+        buffers += carry.scratch
+        options = pltpu.CompilerParams(
+            dimension_semantics=("arbitrary",), vmem_limit_bytes=VMEM_LIMIT, collective_id=carry.ident,
+            has_side_effects=True,
+        )
+    arrays = [(a.shape, a.dtype) for a in args] + results
     return pl.pallas_call(
-        kernel,
+        body,
         grid=(images,),
         in_specs=ins,
         out_specs=out_specs,
-        out_shape=[jax.ShapeDtypeStruct(s, d) for s, d in outs + sums],
-        scratch_shapes=[pltpu.VMEM(s, d) for s, d in scratch],
-        compiler_params=params(),
+        out_shape=[jax.ShapeDtypeStruct(s, d) for s, d in results],
+        scratch_shapes=buffers,
+        compiler_params=options,
         cost_estimate=cost(flops, arrays),
         name=name,
     )(*args)
@@ -528,7 +559,7 @@
     return jnp.broadcast_to(valid.astype(F32)[..., None], valid.shape + (LANES,))
 
 
-def forward_window(inputs, mask, lay, sh, watt):
+def forward_window(inputs, mask, lay, sh, watt, carry=None):
     images, _, _, c = inputs.shape
     t = 4 * WTOK
     outs = [
@@ -538,7 +569,7 @@
     ]
     scratch = [((t, c), F32), ((t, c), F32), ((t, 3 * c), F32), ((t, c), F32)]
     return image_call(window_forward_kernel, "window_forward", 0, [inputs, mask], lay, [sh, watt],
-                      outs, [], scratch, 10 * images * t * c * c)
+                      outs, [], scratch, 10 * images * t * c * c, carry)
 
 
 def forward_mlp(x, mask, lay, hid, w_in, w_out):
@@ -596,7 +627,7 @@
                       outs, [((16, c), F32), ((1, 3 * c), F32)], scratch, 10 * images * t * c * c)
 
 
-def backward_window(g, inputs, z, r, q, p, mask, lay, watt):
+def backward_window(g, inputs, z, r, q, p, mask, lay, watt, carry=None):
     images, t, c = g.shape
     outs = [(inputs.shape, BF16), ((images, t, c), BF16), ((images, t, 3 * c), BF16)]
     scratch = [
@@ -604,7 +635,7 @@
         ((16, c), F32), ((16 * SUB, c), F32), ((SUB, 3 * c), F32),
     ]
     return image_call(window_backward_kernel, "window_backward", 0, [g, inputs, z, r, q, p, mask], lay, [watt],
-                      outs, [((16, c), F32), ((1, 3 * c), F32)], scratch, 12 * images * t * c * c)
+                      outs, [((16, c), F32), ((1, 3 * c), F32)], scratch, 12 * images * t * c * c, carry)
 
 
 def grad_pair_kernel(first, left0, right0, left1, right1, out0, out1):
@@ -771,6 +802,90 @@
             item.stage(rel)
     for item in items:
         item.finish()
+
+
+GATHER_STEPS = ((0,), (1, 2, 4, 8), (5, 12, 9), (3, 6, 10), (13, 7), (14, 11), (15,))
+REDUCE_STEPS = ((), (15, 11), (7, 14, 10), (3, 6, 13), (2, 9), (5, 12), (1, 8, 4), (0,))
+
+
+class Beside:
+    def __init__(self, ident, first, second):
+        self.ident = ident
+        self.args = [first, second]
+        self.outs = [
+            ((NARROW * first.shape[0], WIDE * first.shape[1]), BF16),
+            ((WIDE * second.shape[0], NARROW * second.shape[1]), BF16),
+        ]
+        self.out_spec = pl.BlockSpec(memory_space=pl.ANY)
+        self.scratch = [
+            pltpu.SemaphoreType.DMA((2, 32)), pltpu.SemaphoreType.DMA((2, 32)), pltpu.SemaphoreType.DMA((2,)),
+        ]
+
+    def run(self, ins, outs, scratch):
+        items = gather_items([], ins[:1], ins[1:], [], outs[:1], outs[1:], *scratch)
+        for s, rels in enumerate(GATHER_STEPS):
+
+            @pl.when(pl.program_id(0) == s)
+            def _(s=s, rels=rels):
+                if s == 0:
+                    meet()
+                for rel in rels:
+                    for item in items:
+                        item.stage(rel)
+
+    def end(self, ins, outs, scratch):
+        items = gather_items([], ins[:1], ins[1:], [], outs[:1], outs[1:], *scratch)
+
+        @pl.when(last_step())
+        def _():
+            for item in items:
+                item.finish()
+
+
+class Behind:
+    def __init__(self, ident, g_in, g_out):
+        self.ident = ident
+        self.args = [g_in, g_out]
+        self.shapes = [
+            (g_in.shape[0] // NARROW, g_in.shape[1] // WIDE), (g_out.shape[0] // WIDE, g_out.shape[1] // NARROW),
+        ]
+        self.outs = [(s, F32) for s in self.shapes]
+        self.out_spec = None
+        self.scratch = []
+        for s in self.shapes:
+            self.scratch += [pltpu.VMEM((16,) + s, BF16), pltpu.VMEM((16,) + s, BF16), pltpu.VMEM((15,) + s, BF16)]
+        self.scratch += [
+            pltpu.SemaphoreType.DMA((2, 16)), pltpu.SemaphoreType.DMA((2, 32)),
+            pltpu.SemaphoreType.DMA((2, 16)), pltpu.SemaphoreType.DMA((2, 16)),
+        ]
+
+    def items(self, ins, outs, scratch):
+        views = [(0, in_view(ins[0], *self.shapes[0])), (1, out_view(ins[1], *self.shapes[1]))]
+        return [
+            Reduce(i, order, view, *scratch[3 * i : 3 * i + 3], outs[i], scratch[6:])
+            for i, (order, view) in enumerate(views)
+        ]
+
+    def run(self, ins, outs, scratch):
+        items = self.items(ins, outs, scratch)
+        for s, rels in enumerate(REDUCE_STEPS):
+
+            @pl.when(pl.program_id(0) == s)
+            def _(s=s, rels=rels):
+                if s == 0:
+                    meet()
+                    for rel in reversed(STAGES):
+                        for item in items:
+                            item.begin(rel)
+                for rel in rels:
+                    for item in items:
+                        item.stage(rel)
+
+    def end(self, ins, outs, scratch):
+        @pl.when(last_step())
+        def _():
+            for item in self.items(ins, outs, scratch):
+                item.finish()
 
 
 def gather(name, ident, pieces, firsts, seconds):
@@ -1096,21 +1211,31 @@
             halves_piece(p["mlp_out"][1], rows, lanes),
         ])
         rest = lax.all_gather(rest, BOTH, axis=0, tiled=False)
-        got, win0, wout0 = gather("gather_first", 1, [first], [p["mlp_in"][0].T], [p["mlp_out"][0]])
+        (got,) = gather("gather_first", 1, [first], [], [])
         watt0, self.lay, self.sh, self.hid = unpack_first(got)
         watt1, win1, wout1 = unpack_rest(rest)
-        self.watt, self.w_in, self.w_out = (watt0, watt1), (win0, win1), (wout0, wout1)
+        self.watt, self.w_in, self.w_out = (watt0, watt1), [None, win1], [None, wout1]
+        self.own = (p["mlp_in"][0].T, p["mlp_out"][0])
+
+    def forward_window(self, *args):
+        *outs, self.w_in[0], self.w_out[0] = forward_window(*args, carry=Beside(3, *self.own))
+        return outs
+
+    def backward_window(self, g_in, g_out, *args):
+        *outs, self.gi0, self.go0 = backward_window(*args, carry=Behind(4, g_in, g_out))
+        return outs
 
     def reduce_rest(self, gq, gp, g_in, g_out):
         packed = pack_rest(gq, gp, g_in, g_out)
         packed = packed.reshape(-1, packed.shape[2])
         self.rest = lax.psum_scatter(packed, BOTH, scatter_dimension=0, tiled=True)
 
-    def reduce_first(self, gq, gp, g_in, g_out, smalls, sb, cb, hid0, hid1):
+    def reduce_first(self, gq, gp, smalls, sb, cb, hid0, hid1):
         c = gp.shape[0]
         cn, lanes, cw = c // NARROW, c // 2, c // WIDE
         packed = pack_first(gq, gp, jnp.stack(smalls), sb, cb, hid0, hid1)
-        low, high, gi0, go0 = reduce_all("reduce_first", 2, [packed], [g_in], [g_out])
+        low, high = reduce_all("reduce_first", 2, [packed], [], [])
+        gi0, go0 = self.gi0, self.go0
         att0 = jnp.concatenate([low[16:], high])
         rest = self.rest.astype(F32)
         att1, gi1 = rest[:cn], rest[cn : 2 * cn]
@@ -1156,6 +1281,13 @@
         self.sh = jnp.pad(attn.astype(F32), ((0, 11), (0, 0)))
         self.hid = spread(p["hidden_bias"])[0].transpose(1, 0, 2).reshape(2, 1, -1).astype(F32)
 
+    def forward_window(self, *args):
+        return forward_window(*args)
+
+    def backward_window(self, g_in, g_out, *args):
+        self.pair = (self.matrix(g_in, False), self.matrix(g_out, True))
+        return backward_window(*args)
+
     def matrix(self, grad, rows_wide):
         n, w = self.narrow, self.wide
         a, b = (w, n) if rows_wide else (n, w)
@@ -1167,9 +1299,9 @@
     def reduce_rest(self, gq, gp, g_in, g_out):
         self.rest = (self.matrix(gq, False), self.matrix(gp, False), self.matrix(g_in, False), self.matrix(g_out, True))
 
-    def reduce_first(self, gq, gp, g_in, g_out, smalls, sb, cb, hid0, hid1):
+    def reduce_first(self, gq, gp, smalls, sb, cb, hid0, hid1):
         c, cw, fw, n, w = self.c, self.cw, self.fw, self.narrow, self.wide
-        first = (self.matrix(gq, False), self.matrix(gp, False), self.matrix(g_in, False), self.matrix(g_out, True))
+        first = (self.matrix(gq, False), self.matrix(gp, False)) + self.pair
         small = jnp.stack(smalls).reshape(n, self.layers * 16, w, cw).transpose(0, 2, 1, 3)
         attn = jnp.concatenate([sb[:, :c], sb[:, 2 * c :], cb.reshape(3, c)]).reshape(5, w, cw).transpose(1, 0, 2)
         hid = jnp.concatenate([hid0, hid1]).reshape(2, w, fw).transpose(1, 0, 2).reshape(w, -1, cw)
@@ -1194,11 +1326,13 @@
 
 
 def local(plan, inputs, heights, widths, *rest):
+    if inputs.shape[0] != len(REDUCE_STEPS):
+        plan = Plain
     weights = plan(dict(zip(NAMES, rest[:-1])))
     cotangent = rest[-1]
     lay, sh, hid = weights.lay, weights.sh, weights.hid
     mask = token_mask(heights, widths)
-    n1, z1, r1, q1, o1, p1, x2 = forward_window(inputs, mask, lay, sh, weights.watt[0])
+    n1, z1, r1, q1, o1, p1, x2 = weights.forward_window(inputs, mask, lay, sh, weights.watt[0])
     n2, z2, r2, u1, d1, x4 = forward_mlp(x2, mask, lay, hid, weights.w_in[0], weights.w_out[0])
     n3, z3, r3, q3, o3, a3, x6 = forward_channel(x4, mask, lay, sh, weights.watt[1])
     out, g6, n4, u2, gy2, gh2, small3, hid1 = last_mlp(
@@ -1209,9 +1343,10 @@
     weights.reduce_rest(gq1, gp1, gi1, go1)
     g2, gy1, gh1, small1, hid0 = backward_mlp(g4, x2, z2, r2, d1, mask, lay, weights.w_in[0], weights.w_out[0])
     gi0, go0 = grad_pair("mlp_grads", n2, gh1, gy1, u1)
-    input_grad, ga1, dq1, small0, sb = backward_window(g2, inputs, z1, r1, q1, p1, mask, lay, weights.watt[0])
+    input_grad, ga1, dq1, small0, sb = weights.backward_window(
+        gi0, go0, g2, inputs, z1, r1, q1, p1, mask, lay, weights.watt[0])
     gq0, gp0 = grad_pair("window_grads", n1, dq1, o1, ga1)
-    grads = weights.reduce_first(gq0, gp0, gi0, go0, (small0, small1, small2, small3), sb, cb, hid0, hid1)
+    grads = weights.reduce_first(gq0, gp0, (small0, small1, small2, small3), sb, cb, hid0, hid1)
     return (out, input_grad) + grads
 
 

time: 676 us -> 662 us (0.979)
  Pallas kernels: 623 us -> 609 us
    pallas_call x7, Pallas kernels: 335 us -> 401 us  [image_call(): pl.pallas_call(body, grid=(images,), in_specs=ins, out_specs=out_specs, o...]
    pallas_call x1, Pallas kernels: 98.7 us -> 54.7 us  [gather(): pl.pallas_call(functools.partial(gather_kernel, len(pieces), len(firsts))...]
    pallas_call x1, Pallas kernels: 71.8 us -> 36.5 us  [reduce_all(): pl.pallas_call(functools.partial(reduce_kernel, tuple(shapes), len(pieces...]
  transfers between devices with their start and end apart: 2 -> 2, of which waited for: 0 -> 0; matrix products, arithmetic and copies ran while one was open for 3% -> 3% of each run, Pallas kernels for 63% -> 62%
where the time goes in v3:
time: 662 us; the launch traced here: 659 us
  Pallas kernels  609 us (92%)
  local copies, waits for them, and re-layouts  28.9 us (4%)
  between operations  14.7 us (2%)
    pallas_call x7, Pallas kernels, image_call(): pl.pallas_call(body, grid=(images,), in_specs=ins, out_specs=out_specs, o...  401 us
    pallas_call x4, Pallas kernels, grad_pair(): pl.pallas_call(functools.partial(grad_pair_kernel, first), grid=(first +...  81.7 us
    pallas_call x1, Pallas kernels, gather(): pl.pallas_call(functools.partial(gather_kernel, len(pieces), len(firsts))...  54.7 us
    pallas_call x1, Pallas kernels, reduce_all(): pl.pallas_call(functools.partial(reduce_kernel, tuple(shapes), len(pieces...  36.5 us
    unnamed x48, local copies, waits for them, and re-layouts  15.2 us
  transfers between devices with their start and end apart: 2, of which 0 were waited for; matrix products, arithmetic and copies ran while one was open for 3% of the time, Pallas kernels for 62%

profile of v3, /device:TPU:0, one launch (start us, length us, event | category | flops | bytes accessed | tf_op | source)
XLA Modules:
  0.0 658.9 jit_solution(12724324773163057096)
XLA Ops:
  7.2 1.0 fusion.18
  8.3 1.1 copy.33
  9.4 1.7 slice_bitcast_fusion.2
  11.1 1.7 fusion.16
  12.8 0.9 pad_maximum_fusion.2
  13.7 0.8 reshape.237
  14.5 0.1 copy.45
  14.6 1.1 copy.30
  15.8 2.1 copy.32.refs_0_.refs_1_
  17.9 2.1 copy.36.cot
  20.0 0.8 fusion.1.refs_0_
  20.8 54.7 %gather_first.1.got = bf16[32,208,384]{2,1,0:T(8,128)(2,1)} custom-call(bf16[208,384]{1,0:T(8,128)(2,1)} %fusion.1.refs_0_), custom_call_target="tpu_custom_call" | custom-call | bytes 5111808 | tf_op jit(solution)/shard_map/gather_first/pallas_call | solution.py:898
  75.5 6.8 %unpack_first.1 = (bf16[768,3072]{1,0:T(8,128)(2,1)}, f32[4,16,768]{2,1,0:T(8,128)}, f32[16,768]{1,0:T(8,128)}, f32[2,1,3072]{2,1,0:T(1,128)}) custom-call(bf16[32,208,384]{2,1,0:T(8,128)(2,1)} %gather_first.1.got), custom_call_target="tpu_custom_call" | custom-call | bytes 10100736 | tf_op jit(solution)/shard_map/unpack_first/pallas_call | solution.py:1052
  82.5 1.2 broadcast_in_dim.4.refs_1_.mask.refs_6_
  83.7 97.7 %window_forward.1 = (bf16[8,224,768]{2,1,0:T(8,128)(2,1)}, f32[8,224,768]{2,1,0:T(8,128)}, f32[8,224,128]{2,1,0:T(8,128)}, bf16[8,224,2304]{2,1,0:T(8,128)(2,1)}...) custom-call(bf16[8,14,14,768]{3,2,1,0:T(8,128)(2,1)} %copy.32.refs_0, ...), custom_call_target="tpu_custom_call" | custom-call | flops 10569646080 | bytes 48529408 | tf_op jit(solution)/shard_map/window_forward/pallas_call | solution.py:539
  181.4 36.0 %mlp_forward.1 = (bf16[8,224,768]{2,1,0:T(8,128)(2,1)}, f32[8,224,768]{2,1,0:T(8,128)}, f32[8,224,128]{2,1,0:T(8,128)}, bf16[8,224,3072]{2,1,0:T(8,128)(2,1)}, b...) custom-call(f32[8,224,768]{2,1,0:T(8,128)} %get-tuple-element.81.x_in, ...), custom_call_target="tpu_custom_call" | custom-call | flops 16911433728 | bytes 52781056 | tf_op jit(solution)/shard_map/mlp_forward/pallas_call | solution.py:539
  217.5 10.7 %unpack_rest.1 = (bf16[768,3072]{1,0:T(8,128)(2,1)}, bf16[768,3072]{1,0:T(8,128)(2,1)}, bf16[768,3072]{1,0:T(8,128)(2,1)}) custom-call(bf16[32,576,384]{2,1,0:T(8,128)(2,1)} %bitcast.69), custom_call_target="tpu_custom_call" | custom-call | bytes 28311552 | tf_op jit(solution)/shard_map/unpack_rest/pallas_call | solution.py:1088
  228.2 27.1 %channel_forward.1 = (bf16[8,224,768]{2,1,0:T(8,128)(2,1)}, f32[8,224,768]{2,1,0:T(8,128)}, f32[8,224,128]{2,1,0:T(8,128)}, bf16[8,224,2304]{2,1,0:T(8,128)(2,1)...) custom-call(f32[8,224,768]{2,1,0:T(8,128)} %get-tuple-element.85.x_in, ...), custom_call_target="tpu_custom_call" | custom-call | flops 9512681472 | bytes 40222720 | tf_op jit(solution)/shard_map/channel_forward/pallas_call | solution.py:539
  255.3 71.0 %last_mlp.1 = (bf16[8,14,14,768]{3,2,1,0:T(8,128)(2,1)}, f32[8,224,768]{2,1,0:T(8,128)}, bf16[8,224,768]{2,1,0:T(8,128)(2,1)}, bf16[8,224,3072]{2,1,0:T(8,128)(2...) custom-call(f32[8,224,768]{2,1,0:T(8,128)} %get-tuple-element.87.x_in, ...), custom_call_target="tpu_custom_call" | custom-call | flops 33822867456 | bytes 53989376 | tf_op jit(solution)/shard_map/last_mlp/pallas_call | solution.py:539
  326.3 37.6 %channel_backward.1 = (f32[8,224,768]{2,1,0:T(8,128)}, bf16[8,224,768]{2,1,0:T(8,128)(2,1)}, bf16[8,224,2304]{2,1,0:T(8,128)(2,1)}, f32[16,768]{1,0:T(8,128)}, f32[1,2304]{1,0:T(1,128)}) custom-call(f32[8,224,768]{2,1,0:T(8,128)} %get-tuple-element.91.g_in, f32[8,224,768]{2,1,0:T(8,128)} %get-tuple-element.85.x_in, f32[8,224,768]{2,1,0:T(8,128)} %get-tuple-element.92.z_in, ...), custom_call_target="tpu_custom_call" | custom-call | flops 10569646080 | bytes 51241984 | tf_op jit(solution)/shard_map/channel_backward/pallas_call | solution.py:539
  363.9 15.4 %channel_grads.1 = (bf16[768,2304]{1,0:T(8,128)(2,1)}, bf16[768,768]{1,0:T(8,128)(2,1)}) custom-call(bf16[1792,768]{1,0:T(8,128)(2,1)} %bitcast.95, bf16[1792,2304]{1,0:T(8,128)(2,1)} %bitcast.89, bf16[1792,768]{1,0:T(8,128)(2,1)} %bitcast.96, bf16[1792,768]{1,0:T(8,128)(2,1)} %bitcast.98), custom_call_target="tpu_custom_call" | custom-call | flops 8455716864 | bytes 21233664 | tf_op jit(solution)/shard_map/channel_grads/pallas_call | solution.py:665
  379.3 24.9 %last_mlp_grads.1 = (bf16[768,3072]{1,0:T(8,128)(2,1)}, bf16[768,3072]{1,0:T(8,128)(2,1)}) custom-call(bf16[1792,768]{1,0:T(8,128)(2,1)} %bitcast.93, bf16[1792,3072]{1,0:T(8,128)(2,1)} %bitcast.86, bf16[1792,768]{1,0:T(8,128)(2,1)} %bitcast.94, bf16[1792,3072]{1,0:T(8,128)(2,1)} %bitcast.85), custom_call_target="tpu_custom_call" | custom-call | flops 16911433728 | bytes 36962304 | tf_op jit(solution)/shard_map/last_mlp_grads/pallas_call | solution.py:665
  404.2 10.9 %pack_rest.1 = bf16[32,576,384]{2,1,0:T(8,128)(2,1)} custom-call(bf16[768,2304]{1,0:T(8,128)(2,1)} %get-tuple-element.132.gq, bf16[768,768]{1,0:T(8,128)(2,1)} %get-tuple-element.133.gp, bf16[768,3072]{1,0:T(8,128)(2,1)} %get-tuple-element.138.g_in, bf16[768,3072]{1,0:T(8,128)(2,1)} %get-tuple-element.139.g_out), custom_call_target="tpu_custom_call" | custom-call | bytes 28311552 | tf_op jit(solution)/shard_map/pack_rest/pallas_call | solution.py:1125
  415.1 38.6 %mlp_backward.1 = (f32[8,224,768]{2,1,0:T(8,128)}, bf16[8,224,768]{2,1,0:T(8,128)(2,1)}, bf16[8,224,3072]{2,1,0:T(8,128)(2,1)}, f32[16,768]{1,0:T(8,128)}, f32[1,3072]{1,0:T(1,128)}) custom-call(f32[8,224,768]{2,1,0:T(8,128)} %get-tuple-element.96.g_in, f32[8,224,768]{2,1,0:T(8,128)} %get-tuple-element.81.x_in, f32[8,224,768]{2,1,0:T(8,128)} %get-tuple-element.97.z_in, ...), custom_call_target="tpu_custom_call" | custom-call | flops 16911433728 | bytes 58322944 | tf_op jit(solution)/shard_map/mlp_backward/pallas_call | solution.py:539
  453.7 25.9 %mlp_grads.1 = (bf16[768,3072]{1,0:T(8,128)(2,1)}, bf16[768,3072]{1,0:T(8,128)(2,1)}) custom-call(bf16[1792,768]{1,0:T(8,128)(2,1)} %bitcast.92, bf16[1792,3072]{1,0:T(8,128)(2,1)} %bitcast.87, bf16[1792,768]{1,0:T(8,128)(2,1)} %bitcast.99, bf16[1792,3072]{1,0:T(8,128)(2,1)} %bitcast.84), custom_call_target="tpu_custom_call" | custom-call | flops 16911433728 | bytes 36962304 | tf_op jit(solution)/shard_map/mlp_grads/pallas_call | solution.py:665
  479.6 93.2 %window_backward.1 = (bf16[8,14,14,768]{3,2,1,0:T(8,128)(2,1)}, bf16[8,224,768]{2,1,0:T(8,128)(2,1)}, bf16[8,224,2304]{2,1,0:T(8,128)(2,1)}, f32[16,768]{1,0:T(8...) custom-call(f32[8,224,768]{2,1,0:T(8,128)} %get-tuple-element.100.refs_0_, ...), custom_call_target="tpu_custom_call" | custom-call | flops 12683575296 | bytes 56747008 | tf_op jit(solution)/shard_map/window_backward/pallas_call | solution.py:539
  572.8 1.5 pad_maximum_fusion.3.small
  574.3 15.5 %window_grads.1 = (bf16[768,2304]{1,0:T(8,128)(2,1)}, bf16[768,768]{1,0:T(8,128)(2,1)}) custom-call(bf16[1792,768]{1,0:T(8,128)(2,1)} %bitcast.90, bf16[1792,2304]{1,0:T(8,128)(2,1)} %bitcast.88, bf16[1792,768]{1,0:T(8,128)(2,1)} %bitcast.91, bf16[1792,768]{1,0:T(8,128)(2,1)} %bitcast.97), custom_call_target="tpu_custom_call" | custom-call | flops 8455716864 | bytes 21233664 | tf_op jit(solution)/shard_map/window_grads/pallas_call | solution.py:665
  589.8 6.6 pack_first.1.refs_0_
  596.3 36.5 %reduce_first.1 = (f32[96,384]{1,0:T(8,128)}, f32[112,384]{1,0:T(8,128)}) custom-call(bf16[32,208,384]{2,1,0:T(8,128)(2,1)} %pack_first.1.refs_0_), custom_call_target="tpu_custom_call" | custom-call | bytes 5111808 | tf_op jit(solution)/shard_map/reduce_first/pallas_call | solution.py:1009
  632.9 0.9 slice.90
  633.7 1.3 slice.89
  635.0 0.9 slice.82
  635.9 2.7 copy.39
  638.7 2.7 copy.40
  641.4 0.7 reshape.257
  642.1 0.7 slice_bitcast_fusion.6
  642.8 0.6 copy.41
  643.4 0.9 copy.42
  644.3 1.4 fusion.17
  645.7 1.1 convert_element_type.16
  646.9 0.9 slice.97
  647.9 0.2 copy.38
  648.1 0.2 stack_reshape.3
  648.4 0.8 copy.44
  649.2 0.9 copy.43
  650.0 0.9 pad_maximum_fusion.1
  650.9 0.9 pad_maximum_fusion
  (57 shorter events, 0.8 us)
Async XLA Ops:
  7.2 8.5 %copy-start.2 = (bf16[8,14,14,768]{3,0,2,1:T(8,128)(2,1)S(1)}, bf16[8,14,14,768]{3,0,2,1:T(8,128)(2,1)}, u32[]{:S(2)}) copy-start(bf16[8,14,14,768]{3,0,2,1:T(8,128)(2,1)} %param.16) | copy-start | bytes 7225348
  7.2 210.3 %all-gather.3.cloned.1.call-start = ((), (), s32[]{:S(2)}) async-start(), calls=%async_computation.2 | async-start | bytes 14598144 | tf_op jit(solution)/shard_map/all_gather | solution.py:1213
  13.7 632.0 %reduce-scatter.2.cloned.1.call-start = ((), (), s32[]{:S(2)}) async-start(), calls=%async_computation.1 | async-start | bytes 14598144 | tf_op jit(solution)/shard_map/reduce_scatter | solution.py:1231
  15.7 2.2 copy-start.3
  15.7 4.3 copy-start.10
  15.7 4.2 copy-start.12
  15.7 4.2 copy-start.13
  15.7 4.2 copy-start.14
  15.7 4.2 copy-start.15
  15.7 4.3 copy-start.11
  20.8 61.6 %copy-start.16 = (s32[8]{0:T(128)S(1)}, s32[8]{0:T(128)}, u32[]{:S(2)}) copy-start(s32[8]{0:T(128)} %param.18) | copy-start | bytes 100
  20.8 61.6 %copy-start.17 = (s32[8]{0:T(128)S(1)}, s32[8]{0:T(128)}, u32[]{:S(2)}) copy-start(s32[8]{0:T(128)} %param.17) | copy-start | bytes 100
  479.6 93.2 %copy-start.7 = (f32[16,768]{1,0:T(8,128)S(1)}, f32[16,768]{1,0:T(8,128)}, u32[]{:S(2)}) copy-start(f32[16,768]{1,0:T(8,128)} %get-tuple-element.121) | copy-start | bytes 147460
  479.6 93.2 %copy-start.8 = (f32[16,768]{1,0:T(8,128)S(1)}, f32[16,768]{1,0:T(8,128)}, u32[]{:S(2)}) copy-start(f32[16,768]{1,0:T(8,128)} %get-tuple-element.120) | copy-start | bytes 147460
  479.6 93.2 %copy-start.9 = (f32[16,768]{1,0:T(8,128)S(1)}, f32[16,768]{1,0:T(8,128)}, u32[]{:S(2)}) copy-start(f32[16,768]{1,0:T(8,128)} %get-tuple-element.119) | copy-start | bytes 147460
  596.3 39.6 %copy-start = (bf16[8,14,14,768]{3,2,1,0:T(8,128)(2,1)S(1)}, bf16[8,14,14,768]{3,2,1,0:T(8,128)(2,1)}, u32[]{:S(2)}) copy-start(bf16[8,14,14,768]{3,2,1,0:T(8,128)(2,1)} %get-tuple-element.142) | copy-start | bytes 7225348
  632.9 5.8 copy-start.1
  635.9 7.5 %copy-start.4 = (f32[112,384]{1,0:T(8,128)S(1)}, f32[112,384]{1,0:T(8,128)}, u32[]{:S(2)}) copy-start(f32[112,384]{1,0:T(8,128)} %get-tuple-element.127) | copy-start | bytes 516100
  641.4 8.6 %copy-start.6 = (f32[96,768]{1,0:T(8,128)S(1)}, f32[96,768]{1,0:T(8,128)}, u32[]{:S(2)}) copy-start(f32[96,768]{1,0:T(8,128)} %get-tuple-element.141) | copy-start | bytes 884740
  641.4 9.5 %copy-start.5 = (f32[192,384]{1,0:T(8,128)S(1)}, f32[192,384]{1,0:T(8,128)}, u32[]{:S(2)}) copy-start(f32[192,384]{1,0:T(8,128)} %get-tuple-element.140) | copy-start | bytes 884740
Sparse Core Ops, SparseCore 0:
  13.8 141.4 all-gather.2
  415.2 180.9 reduce-scatter.1

commit v4 on v3

--- a/solution.py
+++ b/solution.py
@@ -572,7 +572,7 @@
                       outs, [], scratch, 10 * images * t * c * c, carry)
 
 
-def forward_mlp(x, mask, lay, hid, w_in, w_out):
+def forward_mlp(x, mask, lay, hid, w_in, w_out, carry=None):
     images, t, c = x.shape
     ff = w_in.shape[1]
     outs = [
@@ -581,10 +581,10 @@
     ]
     scratch = [((t, c), F32), ((t, c), F32)]
     return image_call(mlp_forward_kernel, "mlp_forward", 1, [x, mask], lay, [(hid, 0), w_in, w_out],
-                      outs, [], scratch, 4 * images * t * c * ff)
-
-
-def forward_channel(x, mask, lay, sh, watt):
+                      outs, [], scratch, 4 * images * t * c * ff, carry)
+
+
+def forward_channel(x, mask, lay, sh, watt, carry=None):
     images, t, c = x.shape
     outs = [
         ((images, t, c), BF16), ((images, t, c), F32), ((images, t, LANES), F32),
@@ -592,7 +592,7 @@
         ((images, c // GROUP, GROUP, GROUP), BF16), ((images, t, c), F32),
     ]
     return image_call(channel_forward_kernel, "channel_forward", 2, [x, mask], lay, [sh, watt],
-                      outs, [], [((t, c), F32)], 9 * images * t * c * c)
+                      outs, [], [((t, c), F32)], 9 * images * t * c * c, carry)
 
 
 def last_mlp(x, cot, mask, lay, hid, w_in, w_out):
@@ -610,21 +610,21 @@
                       outs, [((16, c), F32), ((1, ff), F32)], scratch, 8 * images * t * c * ff)
 
 
-def backward_mlp(g, x, z, r, d, mask, lay, w_in, w_out):
+def backward_mlp(g, x, z, r, d, mask, lay, w_in, w_out, carry=None):
     images, t, c = x.shape
     ff = w_in.shape[1]
     outs = [((images, t, c), F32), ((images, t, c), BF16), ((images, t, ff), BF16)]
     scratch = [((t, c), F32), ((t, c), F32), ((16 * SUB, c), F32), ((SUB, ff), F32)]
     return image_call(mlp_backward_kernel, "mlp_backward", 1, [g, x, z, r, d, mask], lay, [w_in, w_out],
-                      outs, [((16, c), F32), ((1, ff), F32)], scratch, 4 * images * t * c * ff)
-
-
-def backward_channel(g, x, z, r, q, a, mask, lay, watt):
+                      outs, [((16, c), F32), ((1, ff), F32)], scratch, 4 * images * t * c * ff, carry)
+
+
+def backward_channel(g, x, z, r, q, a, mask, lay, watt, carry=None):
     images, t, c = x.shape
     outs = [((images, t, c), F32), ((images, t, c), BF16), ((images, t, 3 * c), BF16)]
     scratch = [((t, c), F32), ((t, c), F32), ((16 * SUB, c), F32), ((SUB, 3 * c), F32)]
     return image_call(channel_backward_kernel, "channel_backward", 2, [g, x, z, r, q, a, mask], lay, [watt],
-                      outs, [((16, c), F32), ((1, 3 * c), F32)], scratch, 10 * images * t * c * c)
+                      outs, [((16, c), F32), ((1, 3 * c), F32)], scratch, 10 * images * t * c * c, carry)
 
 
 def backward_window(g, inputs, z, r, q, p, mask, lay, watt, carry=None):
@@ -684,6 +684,8 @@
 ORDERS = ((0, 1, 2, 3), (0, 1, 3, 2))
 MESH_ID = pl.DeviceIdType.MESH
 STAGES = (0, 4, 8, 12, 1, 5, 9, 13, 2, 6, 10, 14, 3, 7, 11, 15)
+GATHER_STEPS = ((0,), (1, 2, 4, 8), (5, 12, 9), (3, 6, 10), (13, 7), (14, 11), (15,))
+REDUCE_STEPS = ((), (15, 11), (7, 14, 10), (3, 6, 13), (2, 9), (5, 12), (1, 8, 4), (0,))
 
 
 def flip(value, bit):
@@ -705,124 +707,108 @@
 
 def meet():
     barrier = pltpu.get_barrier_semaphore()
-    for axis in range(5):
-        order = (axis, axis, axis, axis)
-        name, bit = AXES[axis]
+    for name, bit in AXES:
         at = {"narrow": lax.axis_index("narrow"), "wide": lax.axis_index("wide")}
         at[name] = flip(at[name], bit)
         pl.semaphore_signal(barrier, inc=1, device_id=at, device_id_type=MESH_ID)
     pl.semaphore_wait(barrier, 5)
 
 
+class Part:
+    def __init__(self, operand, kind, shape, start, size, order):
+        self.operand, self.kind, self.shape, self.start, self.size, self.order = operand, kind, shape, start, size, order
+
+    def whole(self):
+        rows, cols = self.shape
+        return {
+            "slot": (WIDE * NARROW, rows, cols), "in": (NARROW * rows, WIDE * cols), "out": (WIDE * rows, NARROW * cols),
+        }[self.kind]
+
+    def view(self, ref, n, w):
+        rows, cols = self.shape
+        if self.kind == "slot":
+            return ref.at[n * WIDE + w, pl.ds(self.start, self.size), :]
+        a, b = (n, w) if self.kind == "in" else (w, n)
+        step = 16
+        while step < 128 and rows % (2 * step) == 0 and self.start % (2 * step) == 0:
+            step *= 2
+        at = pl.multiple_of(a * rows + self.start, step)
+        return ref.at[pl.ds(at, self.size), pl.ds(pl.multiple_of(b * cols, cols), cols)]
+
+    def of(self, ref, rel):
+        at = place(self.order, rel)
+        return self.view(ref, at["narrow"], at["wide"])
+
+
+def halves(operand, kind, shape):
+    low = shape[0] // 32 * 16
+    return [Part(operand, kind, shape, 0, low, 0), Part(operand, kind, shape, low, shape[0] - low, 1)]
+
+
+def pair(first, second, shape_in, shape_out):
+    return [Part(first, "in", shape_in, 0, shape_in[0], 0), Part(second, "out", shape_out, 0, shape_out[0], 1)]
+
+
 class Gather:
-    def __init__(self, index, order, own, view, send, recv, keep):
-        self.index, self.order, self.own, self.view = index, order, own, view
-        self.send, self.recv, self.keep = send, recv, keep
-
-    def ref(self, rel):
-        at = place(self.order, rel)
-        return self.view(at["narrow"], at["wide"])
-
-    def copy(self, rel, axis, slot):
-        target = self.ref(rel)
+    def __init__(self, index, part, own, dest, sems):
+        self.index, self.part, self.dest = index, part, dest
+        self.own = own.at[pl.ds(part.start, part.size), :]
+        self.send, self.recv, self.keep = sems
+
+    def copy(self, rel, axis):
+        target = self.part.of(self.dest, rel)
+        slot = rel | (1 << axis)
         return pltpu.make_async_remote_copy(
-            src_ref=self.own if rel == 0 else target,
-            dst_ref=target,
-            send_sem=self.send.at[self.index, slot],
-            recv_sem=self.recv.at[self.index, rel | (1 << axis)],
-            device_id=place(self.order, 1 << axis),
-            device_id_type=MESH_ID,
+            src_ref=self.own if rel == 0 else target, dst_ref=target, send_sem=self.send.at[self.index, slot],
+            recv_sem=self.recv.at[self.index, slot], device_id=place(self.part.order, 1 << axis), device_id_type=MESH_ID,
         )
 
     def arrival(self, rel):
-        target = self.ref(rel)
+        target = self.part.of(self.dest, rel)
         return pltpu.make_async_remote_copy(
             src_ref=target, dst_ref=target, send_sem=self.send.at[self.index, 0],
-            recv_sem=self.recv.at[self.index, rel], device_id=place(self.order, 1), device_id_type=MESH_ID,
+            recv_sem=self.recv.at[self.index, rel], device_id=place(self.part.order, 1), device_id_type=MESH_ID,
         )
 
-    def sends(self, rel):
-        first = highest(rel) + 1
-        return [(axis, rel | (1 << axis)) for axis in range(first, 5)][::-1]
+    def stay(self):
+        return pltpu.make_async_copy(self.own, self.part.of(self.dest, 0), self.keep.at[self.index])
 
     def stage(self, rel):
         if rel == 0:
-            pltpu.make_async_copy(self.own, self.ref(0), self.keep.at[self.index]).start()
+            self.stay().start()
         else:
             self.arrival(rel).wait_recv()
-        for axis, slot in self.sends(rel):
-            self.copy(rel, axis, slot).start()
+        for axis in reversed(range(highest(rel) + 1, 5)):
+            self.copy(rel, axis).start()
 
     def finish(self):
         for rel in range(16, 32):
             self.arrival(rel).wait_recv()
         for rel in range(16):
-            for axis, slot in self.sends(rel):
-                self.copy(rel, axis, slot).wait_send()
-        pltpu.make_async_copy(self.own, self.ref(0), self.keep.at[self.index]).wait()
-
-
-def slot_view(ref, start, size):
-    return lambda n, w: ref.at[n * WIDE + w, pl.ds(start, size), :]
-
-
-def in_view(ref, rows, cols):
-    return lambda n, w: ref.at[pl.ds(pl.multiple_of(n * rows, rows), rows), pl.ds(pl.multiple_of(w * cols, cols), cols)]
-
-
-def out_view(ref, rows, cols):
-    return lambda n, w: ref.at[pl.ds(pl.multiple_of(w * rows, rows), rows), pl.ds(pl.multiple_of(n * cols, cols), cols)]
-
-
-def gather_items(pieces, firsts, seconds, wholes, in_mats, out_mats, send, recv, keep):
-    items = []
-    for piece, dest in zip(pieces, wholes):
-        half = piece.shape[0] // 32 * 16
-        rest = piece.shape[0] - half
-        items.append((0, piece.at[pl.ds(0, half)], slot_view(dest, 0, half)))
-        items.append((1, piece.at[pl.ds(half, rest)], slot_view(dest, half, rest)))
-    for own, dest in zip(firsts, in_mats):
-        items.append((0, own, in_view(dest, *own.shape)))
-    for own, dest in zip(seconds, out_mats):
-        items.append((1, own, out_view(dest, *own.shape)))
-    return [Gather(i, order, own, view, send, recv, keep) for i, (order, own, view) in enumerate(items)]
-
-
-def gather_kernel(np_, nm, *refs):
-    pieces, refs = refs[:np_], refs[np_:]
-    firsts, refs = refs[:nm], refs[nm:]
-    seconds, refs = refs[:nm], refs[nm:]
-    wholes, refs = refs[:np_], refs[np_:]
-    in_mats, refs = refs[:nm], refs[nm:]
-    out_mats, refs = refs[:nm], refs[nm:]
-    items = gather_items(pieces, firsts, seconds, wholes, in_mats, out_mats, *refs)
-    meet()
-    for rel in STAGES:
-        for item in items:
-            item.stage(rel)
-    for item in items:
-        item.finish()
-
-
-GATHER_STEPS = ((0,), (1, 2, 4, 8), (5, 12, 9), (3, 6, 10), (13, 7), (14, 11), (15,))
-REDUCE_STEPS = ((), (15, 11), (7, 14, 10), (3, 6, 13), (2, 9), (5, 12), (1, 8, 4), (0,))
+            for axis in range(highest(rel) + 1, 5):
+                self.copy(rel, axis).wait_send()
+        self.stay().wait()
+
+
+def gather_sems(count):
+    return [pltpu.SemaphoreType.DMA((count, 32)), pltpu.SemaphoreType.DMA((count, 32)), pltpu.SemaphoreType.DMA((count,))]
 
 
 class Beside:
-    def __init__(self, ident, first, second):
-        self.ident = ident
-        self.args = [first, second]
-        self.outs = [
-            ((NARROW * first.shape[0], WIDE * first.shape[1]), BF16),
-            ((WIDE * second.shape[0], NARROW * second.shape[1]), BF16),
-        ]
+    def __init__(self, ident, args, parts, pick=None):
+        self.ident, self.args, self.parts = ident, list(args), parts
+        self.pick = pick or {}
+        shapes = {p.operand: p.whole() for p in parts}
+        self.outs = [(shapes[k], BF16) for k in range(len(self.args))]
         self.out_spec = pl.BlockSpec(memory_space=pl.ANY)
-        self.scratch = [
-            pltpu.SemaphoreType.DMA((2, 32)), pltpu.SemaphoreType.DMA((2, 32)), pltpu.SemaphoreType.DMA((2,)),
-        ]
+        self.scratch = gather_sems(len(parts))
+
+    def items(self, ins, outs, scratch):
+        ins = [ref.at[self.pick[k]] if k in self.pick else ref for k, ref in enumerate(ins)]
+        return [Gather(i, p, ins[p.operand], outs[p.operand], scratch) for i, p in enumerate(self.parts)]
 
     def run(self, ins, outs, scratch):
-        items = gather_items([], ins[:1], ins[1:], [], outs[:1], outs[1:], *scratch)
+        items = self.items(ins, outs, scratch)
         for s, rels in enumerate(GATHER_STEPS):
 
             @pl.when(pl.program_id(0) == s)
@@ -834,36 +820,81 @@
                         item.stage(rel)
 
     def end(self, ins, outs, scratch):
-        items = gather_items([], ins[:1], ins[1:], [], outs[:1], outs[1:], *scratch)
-
         @pl.when(last_step())
         def _():
-            for item in items:
+            for item in self.items(ins, outs, scratch):
                 item.finish()
 
 
+class Reduce:
+    def __init__(self, index, part, src, out, bufs, sems):
+        self.index, self.part, self.src, self.out = index, part, src, out
+        self.acc, self.mate, self.inbox = bufs
+        self.load_sem, self.send_sem, self.mate_sem, self.recv_sem = sems
+
+    def load(self, rel):
+        return pltpu.make_async_copy(self.part.of(self.src, rel), self.acc.at[rel], self.load_sem.at[self.index, rel])
+
+    def to_mate(self, rel):
+        return pltpu.make_async_remote_copy(
+            src_ref=self.part.of(self.src, rel | 16), dst_ref=self.mate.at[rel],
+            send_sem=self.send_sem.at[self.index, 16 + rel], recv_sem=self.mate_sem.at[self.index, rel],
+            device_id=place(self.part.order, 16), device_id_type=MESH_ID,
+        )
+
+    def onward(self, rel):
+        return pltpu.make_async_remote_copy(
+            src_ref=self.acc.at[rel], dst_ref=self.inbox.at[rel - 1], send_sem=self.send_sem.at[self.index, rel],
+            recv_sem=self.recv_sem.at[self.index, rel], device_id=place(self.part.order, 1 << highest(rel)),
+            device_id_type=MESH_ID,
+        )
+
+    def begin(self, rel):
+        self.to_mate(rel).start()
+        self.load(rel).start()
+
+    def stage(self, rel):
+        self.load(rel).wait()
+        self.to_mate(rel).wait_recv()
+        total = self.acc[rel].astype(F32) + self.mate[rel].astype(F32)
+        for axis in range(highest(rel) + 1, 4):
+            came = rel | (1 << axis)
+            self.onward(came).wait_recv()
+            total = total + self.inbox[came - 1].astype(F32)
+        if rel == 0:
+            self.out[pl.ds(self.part.start, self.part.size), :] = total
+        else:
+            self.acc[rel] = total.astype(BF16)
+            self.onward(rel).start()
+
+    def finish(self):
+        for rel in range(16):
+            self.to_mate(rel).wait_send()
+            if rel:
+                self.onward(rel).wait_send()
+
+
 class Behind:
-    def __init__(self, ident, g_in, g_out):
-        self.ident = ident
-        self.args = [g_in, g_out]
-        self.shapes = [
-            (g_in.shape[0] // NARROW, g_in.shape[1] // WIDE), (g_out.shape[0] // WIDE, g_out.shape[1] // NARROW),
-        ]
-        self.outs = [(s, F32) for s in self.shapes]
+    def __init__(self, ident, args, parts):
+        self.ident, self.args, self.parts = ident, list(args), parts
+        shapes = {p.operand: p.shape for p in parts}
+        self.outs = [(shapes[k], F32) for k in range(len(self.args))]
         self.out_spec = None
         self.scratch = []
-        for s in self.shapes:
-            self.scratch += [pltpu.VMEM((16,) + s, BF16), pltpu.VMEM((16,) + s, BF16), pltpu.VMEM((15,) + s, BF16)]
+        for p in parts:
+            block = (p.size, p.shape[1])
+            self.scratch += [pltpu.VMEM((16,) + block, BF16), pltpu.VMEM((16,) + block, BF16), pltpu.VMEM((15,) + block, BF16)]
+        count = len(parts)
         self.scratch += [
-            pltpu.SemaphoreType.DMA((2, 16)), pltpu.SemaphoreType.DMA((2, 32)),
-            pltpu.SemaphoreType.DMA((2, 16)), pltpu.SemaphoreType.DMA((2, 16)),
+            pltpu.SemaphoreType.DMA((count, 16)), pltpu.SemaphoreType.DMA((count, 32)),
+            pltpu.SemaphoreType.DMA((count, 16)), pltpu.SemaphoreType.DMA((count, 16)),
         ]
 
     def items(self, ins, outs, scratch):
-        views = [(0, in_view(ins[0], *self.shapes[0])), (1, out_view(ins[1], *self.shapes[1]))]
+        bufs, sems = scratch[: 3 * len(self.parts)], scratch[3 * len(self.parts) :]
         return [
-            Reduce(i, order, view, *scratch[3 * i : 3 * i + 3], outs[i], scratch[6:])
-            for i, (order, view) in enumerate(views)
+            Reduce(i, p, ins[p.operand], outs[p.operand], bufs[3 * i : 3 * i + 3], sems)
+            for i, p in enumerate(self.parts)
         ]
 
     def run(self, ins, outs, scratch):
@@ -888,97 +919,10 @@
                 item.finish()
 
 
-def gather(name, ident, pieces, firsts, seconds):
-    count = 2 * len(pieces) + len(firsts) + len(seconds)
-    outs = [jax.ShapeDtypeStruct((WIDE * NARROW,) + p.shape, p.dtype) for p in pieces]
-    outs += [jax.ShapeDtypeStruct((NARROW * f.shape[0], WIDE * f.shape[1]), f.dtype) for f in firsts]
-    outs += [jax.ShapeDtypeStruct((WIDE * s.shape[0], NARROW * s.shape[1]), s.dtype) for s in seconds]
-    args = list(pieces) + list(firsts) + list(seconds)
-    arrays = [(o.shape, o.dtype) for o in outs]
-    return pl.pallas_call(
-        functools.partial(gather_kernel, len(pieces), len(firsts)),
-        in_specs=[pl.BlockSpec(memory_space=pl.ANY)] * len(args),
-        out_specs=[pl.BlockSpec(memory_space=pl.ANY)] * len(outs),
-        out_shape=outs,
-        scratch_shapes=[
-            pltpu.SemaphoreType.DMA((count, 32)), pltpu.SemaphoreType.DMA((count, 32)),
-            pltpu.SemaphoreType.DMA((count,)),
-        ],
-        compiler_params=pltpu.CompilerParams(collective_id=ident, has_side_effects=True, vmem_limit_bytes=VMEM_LIMIT),
-        cost_estimate=cost(0, arrays),
-        name=name,
-    )(*args)
-
-
-class Reduce:
-    def __init__(self, index, order, view, acc, mate, inbox, out, sems):
-        self.index, self.order, self.view = index, order, view
-        self.acc, self.mate, self.inbox, self.out = acc, mate, inbox, out
-        self.load_sem, self.send_sem, self.mate_sem, self.recv_sem = sems
-
-    def ref(self, rel):
-        at = place(self.order, rel)
-        return self.view(at["narrow"], at["wide"])
-
-    def load(self, rel):
-        return pltpu.make_async_copy(self.ref(rel), self.acc.at[rel], self.load_sem.at[self.index, rel])
-
-    def to_mate(self, rel):
-        return pltpu.make_async_remote_copy(
-            src_ref=self.ref(rel | 16), dst_ref=self.mate.at[rel], send_sem=self.send_sem.at[self.index, 16 + rel],
-            recv_sem=self.mate_sem.at[self.index, rel], device_id=place(self.order, 16), device_id_type=MESH_ID,
-        )
-
-    def onward(self, rel):
-        return pltpu.make_async_remote_copy(
-            src_ref=self.acc.at[rel], dst_ref=self.inbox.at[rel - 1], send_sem=self.send_sem.at[self.index, rel],
-            recv_sem=self.recv_sem.at[self.index, rel], device_id=place(self.order, 1 << highest(rel)),
-            device_id_type=MESH_ID,
-        )
-
-    def begin(self, rel):
-        self.to_mate(rel).start()
-        self.load(rel).start()
-
-    def stage(self, rel):
-        self.load(rel).wait()
-        self.to_mate(rel).wait_recv()
-        total = self.acc[rel].astype(F32) + self.mate[rel].astype(F32)
-        for axis in range(highest(rel) + 1, 4):
-            came = rel | (1 << axis)
-            self.onward(came).wait_recv()
-            total = total + self.inbox[came - 1].astype(F32)
-        if rel == 0:
-            self.out[...] = total
-        else:
-            self.acc[rel] = total.astype(BF16)
-            self.onward(rel).start()
-
-    def finish(self):
-        for rel in range(16):
-            self.to_mate(rel).wait_send()
-            if rel:
-                self.onward(rel).wait_send()
-
-
-def reduce_kernel(shapes, np_, nm, *refs):
-    pieces, refs = refs[:np_], refs[np_:]
-    in_mats, refs = refs[:nm], refs[nm:]
-    out_mats, refs = refs[:nm], refs[nm:]
-    count = len(shapes)
-    outs, refs = refs[:count], refs[count:]
-    bufs, sems = refs[: 3 * count], refs[3 * count :]
-    views = []
-    for k, piece in enumerate(pieces):
-        half = shapes[2 * k][0]
-        views += [(0, slot_view(piece, 0, half)), (1, slot_view(piece, half, shapes[2 * k + 1][0]))]
-    for k, mat in enumerate(in_mats):
-        views.append((0, in_view(mat, *shapes[2 * np_ + k])))
-    for k, mat in enumerate(out_mats):
-        views.append((1, out_view(mat, *shapes[2 * np_ + nm + k])))
-    items = [
-        Reduce(i, order, view, *bufs[3 * i : 3 * i + 3], outs[i], sems) for i, (order, view) in enumerate(views)
-    ]
+def reduce_kernel(plan, *refs):
+    ins, refs = refs[: len(plan.args)], refs[len(plan.args) :]
+    outs, scratch = refs[: len(plan.outs)], refs[len(plan.outs) :]
+    items = plan.items(ins, outs, scratch)
     meet()
     for rel in reversed(STAGES):
         for item in items:
@@ -990,32 +934,19 @@
         item.finish()
 
 
-def reduce_all(name, ident, pieces, in_mats, out_mats):
-    shapes = []
-    for p in pieces:
-        half = p.shape[1] // 32 * 16
-        shapes += [(half, p.shape[2]), (p.shape[1] - half, p.shape[2])]
-    shapes += [(m.shape[0] // NARROW, m.shape[1] // WIDE) for m in in_mats]
-    shapes += [(m.shape[0] // WIDE, m.shape[1] // NARROW) for m in out_mats]
-    count = len(shapes)
-    args = list(pieces) + list(in_mats) + list(out_mats)
-    scratch = []
-    for s in shapes:
-        scratch += [pltpu.VMEM((16,) + s, BF16), pltpu.VMEM((16,) + s, BF16), pltpu.VMEM((15,) + s, BF16)]
-    scratch += [
-        pltpu.SemaphoreType.DMA((count, 16)), pltpu.SemaphoreType.DMA((count, 32)),
-        pltpu.SemaphoreType.DMA((count, 16)), pltpu.SemaphoreType.DMA((count, 16)),
-    ]
+def reduce_now(name, plan):
     return pl.pallas_call(
-        functools.partial(reduce_kernel, tuple(shapes), len(pieces), len(in_mats)),
-        in_specs=[pl.BlockSpec(memory_space=pl.ANY)] * len(args),
-        out_specs=[pl.BlockSpec(memory_space=pltpu.VMEM)] * count,
-        out_shape=[jax.ShapeDtypeStruct(s, F32) for s in shapes],
-        scratch_shapes=scratch,
-        compiler_params=pltpu.CompilerParams(collective_id=ident, has_side_effects=True, vmem_limit_bytes=VMEM_LIMIT),
-        cost_estimate=cost(0, [(a.shape, a.dtype) for a in args]),
+        functools.partial(reduce_kernel, plan),
+        in_specs=[pl.BlockSpec(memory_space=pl.ANY)] * len(plan.args),
+        out_specs=[pl.BlockSpec(memory_space=pltpu.VMEM)] * len(plan.outs),
+        out_shape=[jax.ShapeDtypeStruct(s, d) for s, d in plan.outs],
+        scratch_shapes=plan.scratch,
+        compiler_params=pltpu.CompilerParams(
+            collective_id=plan.ident, has_side_effects=True, vmem_limit_bytes=VMEM_LIMIT
+        ),
+        cost_estimate=cost(0, [(a.shape, a.dtype) for a in plan.args]),
         name=name,
-    )(*args)
+    )(*plan.args)
 
 
 def copy_attention(src, start, dst):
@@ -1064,36 +995,23 @@
     )(got)
 
 
-def unpack_rest_kernel(got, watt, w_in, w_out):
-    cn = watt.shape[0]
-    lanes = got.shape[2]
-    cw = lanes // 4
+def unpack_attention_kernel(got, watt):
     copy_attention(got, 0, watt)
-    for w in range(WIDE):
-        w_in[:, pl.ds(lanes * w, lanes)] = got[w, pl.ds(cn, cn), :]
-        for h in range(2):
-            w_out[pl.ds(cw * w, cw), pl.ds(lanes * h, lanes)] = got[w, pl.ds(2 * cn + cw * h, cw), :]
-
-
-def rest_specs(rows, lanes):
+
+
+def unpack_attention(got):
+    rows, lanes = got.shape[1:]
     c = 2 * lanes
-    cn = c // NARROW
-    packed = pl.BlockSpec((WIDE, rows, lanes), lambda n: (n, 0, 0))
-    flat = pl.BlockSpec((cn, 4 * c), lambda n: (n, 0))
-    return packed, [flat, flat, pl.BlockSpec((c, c), lambda n: (0, n))], (c, 4 * c)
-
-
-def unpack_rest(got):
-    packed, mats, shape = rest_specs(*got.shape[1:])
+    shape = (c, 4 * c)
     return pl.pallas_call(
-        unpack_rest_kernel,
+        unpack_attention_kernel,
         grid=(NARROW,),
-        in_specs=[packed],
-        out_specs=mats,
-        out_shape=[jax.ShapeDtypeStruct(shape, BF16)] * 3,
+        in_specs=[pl.BlockSpec((WIDE, rows, lanes), lambda n: (n, 0, 0))],
+        out_specs=pl.BlockSpec((c // NARROW, 4 * c), lambda n: (n, 0)),
+        out_shape=jax.ShapeDtypeStruct(shape, BF16),
         compiler_params=params(),
-        cost_estimate=cost(0, [(got.shape, BF16)] * 2),
-        name="unpack_rest",
+        cost_estimate=cost(0, [(shape, BF16)] * 2),
+        name="unpack_attention",
     )(got)
 
 
@@ -1105,33 +1023,24 @@
         dst[w, pl.ds(start, cn), pl.ds(3 * cw, cw)] = gp[:, pl.ds(cw * w, cw)]
 
 
-def pack_rest_kernel(gq, gp, g_in, g_out, out):
-    cn = gq.shape[0]
-    lanes = out.shape[2]
-    cw = lanes // 4
+def pack_attention_kernel(gq, gp, out):
     gather_attention(gq, gp, 0, out)
-    for w in range(WIDE):
-        out[w, pl.ds(cn, cn), :] = g_in[:, pl.ds(lanes * w, lanes)]
-        for h in range(2):
-            out[w, pl.ds(2 * cn + cw * h, cw), :] = g_out[pl.ds(cw * w, cw), pl.ds(lanes * h, lanes)]
-
-
-def pack_rest(gq, gp, g_in, g_out):
+
+
+def pack_attention(gq, gp):
     c = gp.shape[0]
     cn, lanes = c // NARROW, c // 2
-    rows = 3 * cn
-    packed, mats, _ = rest_specs(rows, lanes)
-    shape = (WIDE * NARROW, rows, lanes)
+    shape = (WIDE * NARROW, cn, lanes)
     return pl.pallas_call(
-        pack_rest_kernel,
+        pack_attention_kernel,
         grid=(NARROW,),
-        in_specs=[pl.BlockSpec((cn, 3 * c), lambda n: (n, 0)), pl.BlockSpec((cn, c), lambda n: (n, 0)), mats[1], mats[2]],
-        out_specs=packed,
+        in_specs=[pl.BlockSpec((cn, 3 * c), lambda n: (n, 0)), pl.BlockSpec((cn, c), lambda n: (n, 0))],
+        out_specs=pl.BlockSpec((WIDE, cn, lanes), lambda n: (n, 0, 0)),
         out_shape=jax.ShapeDtypeStruct(shape, BF16),
         compiler_params=params(),
         cost_estimate=cost(0, [(shape, BF16)] * 2),
-        name="pack_rest",
-    )(gq, gp, g_in, g_out)
+        name="pack_attention",
+    )(gq, gp)
 
 
 def pack_first_kernel(gq, gp, small, sb, cb, hid0, hid1, out, shared):
@@ -1182,71 +1091,152 @@
     return jnp.concatenate([qkv.T, proj.T], axis=1)
 
 
-def halves_piece(second, rows, lanes):
-    return second.reshape(second.shape[0], -1, lanes).transpose(1, 0, 2).reshape(rows, lanes)
-
-
-def pad_to(item, rows, lanes):
-    return jnp.pad(item, ((0, rows - item.shape[0]), (0, lanes - item.shape[1])))
-
-
-def small_rows(conv_weight, conv_bias, norm_gain, norm_bias, out_bias):
-    return jnp.concatenate([conv_weight[0], conv_bias, norm_gain, norm_bias, out_bias])
-
-
-def shared_rows(attn_bias, hidden_bias):
-    return jnp.concatenate([attn_bias, hidden_bias.reshape(-1, attn_bias.shape[1])])
+def turned(value):
+    return value.astype(F32).T.astype(BF16)
+
+
+def gather_first_kernel(
+    plan, conv_weight, conv_bias, norm_gain, norm_bias, qkv0, qkv1, proj, mlp_in, attn_bias, hidden_bias, out_bias,
+    got, chan, in0, in1, piece, *sems,
+):
+    cw = conv_bias.shape[1]
+    cn = qkv0.shape[1]
+    piece[pl.ds(0, 16), :] = jnp.zeros((16, piece.shape[1]), BF16)
+    taps_now = conv_weight[0].astype(F32)
+    rows = [taps_now] + [r[...].astype(F32) for r in (conv_bias, norm_gain, norm_bias, out_bias)]
+    rows.append(jnp.zeros((3, cw), F32))
+    piece[pl.ds(0, 16), pl.ds(0, cw)] = jnp.concatenate(rows, axis=0).astype(BF16)
+    hidden = hidden_bias[...].astype(F32)
+    rows = [attn_bias[...].astype(F32)]
+    rows += [hidden[j : j + 1, cw * q : cw * (q + 1)] for j in range(2) for q in range(4)]
+    rows.append(jnp.zeros((3, cw), F32))
+    piece[pl.ds(0, 16), pl.ds(LANES, cw)] = jnp.concatenate(rows, axis=0).astype(BF16)
+    piece[pl.ds(16, cn), pl.ds(0, 3 * cw)] = turned(qkv0[...])
+    piece[pl.ds(16, cn), pl.ds(3 * cw, cw)] = turned(proj[0])
+    items = plan.items([piece], [got], sems)
+    meet()
+    for item in items:
+        item.stage(0)
+    in0[...] = turned(mlp_in[0])
+    in1[...] = turned(mlp_in[1])
+    chan[:, pl.ds(0, 3 * cw)] = turned(qkv1[...])
+    chan[:, pl.ds(3 * cw, cw)] = turned(proj[1])
+    for rel in STAGES[1:]:
+        for item in items:
+            item.stage(rel)
+    for item in items:
+        item.finish()
+
+
+def gather_first(p):
+    rows, cn = p["spatial_qkv"].shape
+    lanes = rows * 4 // 3
+    shape = (16 + cn, lanes)
+    plan = Beside(1, [None], halves(0, "slot", shape))
+    outs = plan.outs + [((cn, lanes), BF16)] * 3
+    args = [p[k] for k in NAMES if k != "mlp_out"]
+    vmem = pl.BlockSpec(memory_space=pltpu.VMEM)
+    return pl.pallas_call(
+        functools.partial(gather_first_kernel, plan),
+        in_specs=[vmem] * len(args),
+        out_specs=[plan.out_spec] + [vmem] * 3,
+        out_shape=[jax.ShapeDtypeStruct(s, d) for s, d in outs],
+        scratch_shapes=[pltpu.VMEM(shape, BF16)] + plan.scratch,
+        compiler_params=pltpu.CompilerParams(collective_id=1, has_side_effects=True, vmem_limit_bytes=VMEM_LIMIT),
+        cost_estimate=cost(0, outs),
+        name="gather_first",
+    )(*args)
+
+
+def finish_kernel(
+    att0, att1, in0, in1, out0, out1,
+    conv_weight, conv_bias, norm_gain, norm_bias, qkv0, qkv1, proj, mlp_in, mlp_out, attn_bias, hidden_bias, out_bias,
+):
+    cw = conv_bias.shape[1]
+    cn = qkv0.shape[1]
+    conv_weight[0] = att0[pl.ds(0, 9), pl.ds(0, cw)]
+    for k, row in enumerate((conv_bias, norm_gain, norm_bias, out_bias)):
+        row[...] = att0[pl.ds(9 + k, 1), pl.ds(0, cw)]
+    attn_bias[...] = att0[pl.ds(0, 5), pl.ds(LANES, cw)]
+    for j in range(2):
+        for q in range(4):
+            hidden_bias[pl.ds(j, 1), pl.ds(cw * q, cw)] = att0[pl.ds(5 + 4 * j + q, 1), pl.ds(LANES, cw)]
+    qkv0[...] = att0[pl.ds(16, cn), pl.ds(0, 3 * cw)].T
+    proj[0] = att0[pl.ds(16, cn), pl.ds(3 * cw, cw)].T
+    qkv1[...] = att1[:, pl.ds(0, 3 * cw)].T
+    proj[1] = att1[:, pl.ds(3 * cw, cw)].T
+    mlp_in[0] = in0[...].T
+    mlp_in[1] = in1[...].T
+    mlp_out[0] = out0[...]
+    mlp_out[1] = out1[...]
+
+
+def finish(*reduced):
+    att0 = reduced[0]
+    cn, lanes = att0.shape[0] - 16, att0.shape[1]
+    cw = lanes // 4
+    row = (1, cw)
+    shapes = [
+        (1, 9, cw), row, row, row, (3 * cw, cn), (3 * cw, cn), (2, cw, cn), (2, lanes, cn), (2, cw, 2 * lanes),
+        (5, cw), (2, lanes), row,
+    ]
+    vmem = pl.BlockSpec(memory_space=pltpu.VMEM)
+    return pl.pallas_call(
+        finish_kernel,
+        in_specs=[vmem] * 6,
+        out_specs=[vmem] * len(shapes),
+        out_shape=[jax.ShapeDtypeStruct(s, F32) for s in shapes],
+        compiler_params=pltpu.CompilerParams(vmem_limit_bytes=VMEM_LIMIT),
+        cost_estimate=cost(0, [(s, F32) for s in shapes]),
+        name="finish",
+    )(*reduced)
 
 
 class Direct:
     def __init__(self, p):
-        lanes = p["spatial_qkv"].shape[0] * 4 // 3
-        small = pad_to(small_rows(p["conv_weight"], p["conv_bias"], p["norm_gain"], p["norm_bias"], p["out_bias"]), 16, LANES)
-        shared = pad_to(shared_rows(p["attn_bias"], p["hidden_bias"]), 16, LANES)
-        head = pad_to(jnp.concatenate([small, shared], axis=1), 16, lanes)
-        first = jnp.concatenate([head, attention_piece(p["spatial_qkv"], p["projection"][0])])
-        rows = p["spatial_qkv"].shape[1]
-        rest = jnp.concatenate([
-            attention_piece(p["channel_qkv"], p["projection"][1]), p["mlp_in"][1].T,
-            halves_piece(p["mlp_out"][1], rows, lanes),
-        ])
-        rest = lax.all_gather(rest, BOTH, axis=0, tiled=False)
-        (got,) = gather("gather_first", 1, [first], [], [])
+        got, self.chan, self.in0, self.in1 = gather_first(p)
+        self.second = p["mlp_out"]
         watt0, self.lay, self.sh, self.hid = unpack_first(got)
-        watt1, win1, wout1 = unpack_rest(rest)
-        self.watt, self.w_in, self.w_out = (watt0, watt1), [None, win1], [None, wout1]
-        self.own = (p["mlp_in"][0].T, p["mlp_out"][0])
+        self.watt, self.w_in, self.w_out = [watt0, None], [None, None], [None, None]
 
     def forward_window(self, *args):
-        *outs, self.w_in[0], self.w_out[0] = forward_window(*args, carry=Beside(3, *self.own))
+        parts = pair(0, 1, self.in0.shape, self.second.shape[1:])
+        carry = Beside(3, [self.in0, self.second], parts, {1: 0})
+        *outs, self.w_in[0], self.w_out[0] = forward_window(*args, carry=carry)
         return outs
 
-    def backward_window(self, g_in, g_out, *args):
-        *outs, self.gi0, self.go0 = backward_window(*args, carry=Behind(4, g_in, g_out))
+    def forward_mlp(self, *args):
+        parts = halves(0, "slot", self.chan.shape) + halves(1, "in", self.in1.shape)
+        *outs, chan, self.w_in[1] = forward_mlp(*args, carry=Beside(4, [self.chan, self.in1], parts))
+        self.watt[1] = unpack_attention(chan)
         return outs
 
-    def reduce_rest(self, gq, gp, g_in, g_out):
-        packed = pack_rest(gq, gp, g_in, g_out)
-        packed = packed.reshape(-1, packed.shape[2])
-        self.rest = lax.psum_scatter(packed, BOTH, scatter_dimension=0, tiled=True)
-
-    def reduce_first(self, gq, gp, smalls, sb, cb, hid0, hid1):
-        c = gp.shape[0]
-        cn, lanes, cw = c // NARROW, c // 2, c // WIDE
-        packed = pack_first(gq, gp, jnp.stack(smalls), sb, cb, hid0, hid1)
-        low, high = reduce_all("reduce_first", 2, [packed], [], [])
-        gi0, go0 = self.gi0, self.go0
-        att0 = jnp.concatenate([low[16:], high])
-        rest = self.rest.astype(F32)
-        att1, gi1 = rest[:cn], rest[cn : 2 * cn]
-        go1 = rest[2 * cn :].reshape(2, cw, lanes).transpose(1, 0, 2).reshape(cw, 2 * lanes)
-        small, shared = low[:16, :cw], low[:16, LANES : LANES + cw]
-        proj = jnp.stack([att0[:, 3 * cw :].T, att1[:, 3 * cw :].T])
-        return (
-            small[None, :9], small[9:10], small[10:11], small[11:12], att0[:, : 3 * cw].T, att1[:, : 3 * cw].T,
-            proj, jnp.stack([gi0.T, gi1.T]), jnp.stack([go0, go1]), shared[:5], shared[5:13].reshape(2, lanes),
-            small[12:13],
-        )
+    def forward_channel(self, *args):
+        parts = halves(0, "out", self.second.shape[1:])
+        *outs, self.w_out[1] = forward_channel(*args, carry=Beside(5, [self.second], parts, {0: 1}))
+        return outs
+
+    def backward_channel(self, grads, *args):
+        self.go1 = grads[1]
+        parts = halves(0, "in", self.in1.shape)
+        *outs, self.gi1 = backward_channel(*args, carry=Behind(6, grads[:1], parts))
+        return outs
+
+    def backward_mlp(self, grads, *args):
+        self.att1 = pack_attention(*grads)
+        parts = halves(0, "out", self.second.shape[1:])
+        *outs, self.go1 = backward_mlp(*args, carry=Behind(7, [self.go1], parts))
+        return outs
+
+    def backward_window(self, grads, *args):
+        parts = pair(0, 1, self.in0.shape, self.second.shape[1:]) + halves(2, "slot", self.chan.shape)
+        *outs, self.gi0, self.go0, self.att1 = backward_window(*args, carry=Behind(8, list(grads) + [self.att1], parts))
+        return outs
+
+    def reduce_last(self, grads, smalls, sb, cb, hid0, hid1):
+        packed = pack_first(*grads, jnp.stack(smalls), sb, cb, hid0, hid1)
+        (att0,) = reduce_now("reduce_last", Behind(2, [packed], halves(0, "slot", packed.shape[1:])))
+        return tuple(finish(att0, self.att1, self.gi0, self.gi1, self.go0, self.go1))
 
 
 class Plain:
@@ -1284,8 +1274,22 @@
     def forward_window(self, *args):
         return forward_window(*args)
 
-    def backward_window(self, g_in, g_out, *args):
-        self.pair = (self.matrix(g_in, False), self.matrix(g_out, True))
+    def forward_mlp(self, *args):
+        return forward_mlp(*args)
+
+    def forward_channel(self, *args):
+        return forward_channel(*args)
+
+    def backward_channel(self, grads, *args):
+        self.mlp1 = (self.matrix(grads[0], False), self.matrix(grads[1], True))
+        return backward_channel(*args)
+
+    def backward_mlp(self, grads, *args):
+        self.att1 = (self.matrix(grads[0], False), self.matrix(grads[1], False))
+        return backward_mlp(*args)
+
+    def backward_window(self, grads, *args):
+        self.mlp0 = (self.matrix(grads[0], False), self.matrix(grads[1], True))
         return backward_window(*args)
 
     def matrix(self, grad, rows_wide):
@@ -1296,12 +1300,10 @@
         grad = grad.astype(BF16).reshape(n * w * grad.shape[2], grad.shape[3])
         return lax.psum_scatter(grad, BOTH, scatter_dimension=0, tiled=True).astype(F32)
 
-    def reduce_rest(self, gq, gp, g_in, g_out):
-        self.rest = (self.matrix(gq, False), self.matrix(gp, False), self.matrix(g_in, False), self.matrix(g_out, True))
-
-    def reduce_first(self, gq, gp, smalls, sb, cb, hid0, hid1):
+    def reduce_last(self, grads, smalls, sb, cb, hid0, hid1):
         c, cw, fw, n, w = self.c, self.cw, self.fw, self.narrow, self.wide
-        first = (self.matrix(gq, False), self.matrix(gp, False)) + self.pair
+        first = (self.matrix(grads[0], False), self.matrix(grads[1], False)) + self.mlp0
+        rest = self.att1 + self.mlp1
         small = jnp.stack(smalls).reshape(n, self.layers * 16, w, cw).transpose(0, 2, 1, 3)
         attn = jnp.concatenate([sb[:, :c], sb[:, 2 * c :], cb.reshape(3, c)]).reshape(5, w, cw).transpose(1, 0, 2)
         hid = jnp.concatenate([hid0, hid1]).reshape(2, w, fw).transpose(1, 0, 2).reshape(w, -1, cw)
@@ -1311,7 +1313,6 @@
         got = lax.psum_scatter(flat, BOTH, scatter_dimension=0, tiled=True).astype(F32)
         small = got[: self.layers * 16].reshape(self.layers, 16, cw)
         shared = got[self.layers * 16 :]
-        rest = self.rest
         return (
             small[:, :9], small[:, 9], small[:, 10], small[:, 11], first[0].T, rest[0].T,
             jnp.stack([first[1].T, rest[1].T]), jnp.stack([first[2].T, rest[2].T]), jnp.stack([first[3], rest[3]]),
@@ -1333,21 +1334,22 @@
     lay, sh, hid = weights.lay, weights.sh, weights.hid
     mask = token_mask(heights, widths)
     n1, z1, r1, q1, o1, p1, x2 = weights.forward_window(inputs, mask, lay, sh, weights.watt[0])
-    n2, z2, r2, u1, d1, x4 = forward_mlp(x2, mask, lay, hid, weights.w_in[0], weights.w_out[0])
-    n3, z3, r3, q3, o3, a3, x6 = forward_channel(x4, mask, lay, sh, weights.watt[1])
+    n2, z2, r2, u1, d1, x4 = weights.forward_mlp(x2, mask, lay, hid, weights.w_in[0], weights.w_out[0])
+    n3, z3, r3, q3, o3, a3, x6 = weights.forward_channel(x4, mask, lay, sh, weights.watt[1])
     out, g6, n4, u2, gy2, gh2, small3, hid1 = last_mlp(
         x6, cotangent, mask, lay, hid, weights.w_in[1], weights.w_out[1])
-    gi1, go1 = grad_pair("last_mlp_grads", n4, gh2, gy2, u2)
-    g4, ga3, dq3, small2, cb = backward_channel(g6, x4, z3, r3, q3, a3, mask, lay, weights.watt[1])
-    gq1, gp1 = grad_pair("channel_grads", n3, dq3, o3, ga3)
-    weights.reduce_rest(gq1, gp1, gi1, go1)
-    g2, gy1, gh1, small1, hid0 = backward_mlp(g4, x2, z2, r2, d1, mask, lay, weights.w_in[0], weights.w_out[0])
-    gi0, go0 = grad_pair("mlp_grads", n2, gh1, gy1, u1)
+    grads = grad_pair("last_mlp_grads", n4, gh2, gy2, u2)
+    g4, ga3, dq3, small2, cb = weights.backward_channel(
+        grads, g6, x4, z3, r3, q3, a3, mask, lay, weights.watt[1])
+    grads = grad_pair("channel_grads", n3, dq3, o3, ga3)
+    g2, gy1, gh1, small1, hid0 = weights.backward_mlp(
+        grads, g4, x2, z2, r2, d1, mask, lay, weights.w_in[0], weights.w_out[0])
+    grads = grad_pair("mlp_grads", n2, gh1, gy1, u1)
     input_grad, ga1, dq1, small0, sb = weights.backward_window(
-        gi0, go0, g2, inputs, z1, r1, q1, p1, mask, lay, weights.watt[0])
-    gq0, gp0 = grad_pair("window_grads", n1, dq1, o1, ga1)
-    grads = weights.reduce_first(gq0, gp0, (small0, small1, small2, small3), sb, cb, hid0, hid1)
-    return (out, input_grad) + grads
+        grads, g2, inputs, z1, r1, q1, p1, mask, lay, weights.watt[0])
+    grads = grad_pair("window_grads", n1, dq1, o1, ga1)
+    last = weights.reduce_last(grads, (small0, small1, small2, small3), sb, cb, hid0, hid1)
+    return (out, input_grad) + tuple(last)
 
 
 def solution(mesh):

time: 662 us -> 663 us (level)
  Pallas kernels: 609 us -> 636 us
  between operations: 14.7 us -> 1.03 us
  local copies, waits for them, and re-layouts: 28.9 us -> 21.5 us
    pallas_call x7, Pallas kernels: 401 us -> 444 us  [image_call(): pl.pallas_call(body, grid=(images,), in_specs=ins, out_specs=out_specs, o...]
    pallas_call x4 -> x5, Pallas kernels: 113 us -> 98 us  [the longest x1 46.3 us: gather_first(): pl.pallas_call(functools.partial(gather_first_kernel, plan), in_specs=[vm...]
    slice x7 -> x0, local copies, waits for them, and re-layouts: 7.97 us -> none  [the longest x1 1.66 us: __init__(): p['mlp_out'][1]]
    unnamed x48 -> x17, local copies, waits for them, and re-layouts: 15.2 us -> 20.2 us
  transfers between devices with their start and end apart: 2 -> 0, of which waited for: 0 -> 0; matrix products, arithmetic and copies ran while one was open for 3% -> 0% of each run, Pallas kernels for 62% -> 0%
where the time goes in v4:
time: 663 us; the launch traced here: 660 us
  Pallas kernels  636 us (96%)
  local copies, waits for them, and re-layouts  21.5 us (3%)
    pallas_call x7, Pallas kernels, image_call(): pl.pallas_call(body, grid=(images,), in_specs=ins, out_specs=out_specs, o...  444 us
    pallas_call x4, Pallas kernels, grad_pair(): pl.pallas_call(functools.partial(grad_pair_kernel, first), grid=(first +...  81.2 us
    pallas_call x1, Pallas kernels, gather_first(): pl.pallas_call(functools.partial(gather_first_kernel, plan), in_specs=[vm...  46.3 us
    pallas_call x1, Pallas kernels, reduce_now(): pl.pallas_call(functools.partial(reduce_kernel, plan), in_specs=[pl.Block...  36.4 us
    unnamed x17, local copies, waits for them, and re-layouts  20.2 us

profile of v4, /device:TPU:0, one launch (start us, length us, event | category | flops | bytes accessed | tf_op | source)
XLA Modules:
  0.0 659.9 jit_solution(13975101016292053220)
XLA Ops:
  0.6 0.0 copy-start
  0.7 0.9 and_convert_fusion
  1.6 1.9 copy.30.mlp_in
  3.5 1.3 broadcast_in_dim.2.refs_1_.mask.refs_6_.refs_5_
  4.8 3.7 copy.31.refs_0_.refs_1_
  8.5 0.0 copy-done
  8.5 2.0 copy.32.cot
  10.5 46.3 %gather_first.1 = (bf16[32,208,384]{2,1,0:T(8,128)(2,1)}, bf16[192,384]{1,0:T(8,128)(2,1)}, bf16[192,384]{1,0:T(8,128)(2,1)}, bf16[192,384]{1,0:T(8,128)(2,1)}) custom-call(bf16[1,9,96]{2,1,0:T(8,128)(2,1)} %conv_weight.1, bf16[1,96]{1,0:T(2,128)(2,1)} %conv_bias.1, bf16[1,96]{1,0:T(2,128)(2,1)} %norm_gain.1, bf16[1,96]{1,0:T(2,128)(2,1)} %norm_bias.1, ...), custom_call_target="tpu_custom_call" | custom-call | bytes 5554176 | tf_op jit(solution)/shard_map/gather_first/pallas_call | solution.py:1139
  56.8 6.6 %unpack_first.1 = (bf16[768,3072]{1,0:T(8,128)(2,1)}, f32[4,16,768]{2,1,0:T(8,128)}, f32[16,768]{1,0:T(8,128)}, f32[2,1,3072]{2,1,0:T(1,128)}) custom-call(bf16[32,208,384]{2,1,0:T(8,128)(2,1)} %get-tuple-element.95.got), custom_call_target="tpu_custom_call" | custom-call | bytes 10100736 | tf_op jit(solution)/shard_map/unpack_first/pallas_call | solution.py:983
  63.4 75.8 %window_forward.1 = (bf16[8,224,768]{2,1,0:T(8,128)(2,1)}, f32[8,224,768]{2,1,0:T(8,128)}, f32[8,224,128]{2,1,0:T(8,128)}, bf16[8,224,2304]{2,1,0:T(8,128)(2,1)}...) custom-call(bf16[8,14,14,768]{3,2,1,0:T(8,128)(2,1)} %copy.31.refs_0, ...), custom_call_target="tpu_custom_call" | custom-call | flops 10569646080 | bytes 48676864 | tf_op jit(solution)/shard_map/window_forward/pallas_call | solution.py:539
  139.2 69.3 %mlp_forward.1 = (bf16[8,224,768]{2,1,0:T(8,128)(2,1)}, f32[8,224,768]{2,1,0:T(8,128)}, f32[8,224,128]{2,1,0:T(8,128)}, bf16[8,224,3072]{2,1,0:T(8,128)(2,1)}, b...) custom-call(f32[8,224,768]{2,1,0:T(8,128)} %get-tuple-element.100.re, ...), custom_call_target="tpu_custom_call" | custom-call | flops 16911433728 | bytes 62513152 | tf_op jit(solution)/shard_map/mlp_forward/pallas_call | solution.py:539
  208.5 6.1 unpack_attention.1.refs_4_.refs_8_
  214.6 43.3 %channel_forward.1 = (bf16[8,224,768]{2,1,0:T(8,128)(2,1)}, f32[8,224,768]{2,1,0:T(8,128)}, f32[8,224,128]{2,1,0:T(8,128)}, bf16[8,224,2304]{2,1,0:T(8,128)(2,1)...) custom-call(f32[8,224,768]{2,1,0:T(8,128)} %get-tuple-element.106.re, ...), custom_call_target="tpu_custom_call" | custom-call | flops 9512681472 | bytes 45236224 | tf_op jit(solution)/shard_map/channel_forward/pallas_call | solution.py:539
  257.9 70.5 %last_mlp.1 = (bf16[8,14,14,768]{3,2,1,0:T(8,128)(2,1)}, f32[8,224,768]{2,1,0:T(8,128)}, bf16[8,224,768]{2,1,0:T(8,128)(2,1)}, bf16[8,224,3072]{2,1,0:T(8,128)(2...) custom-call(f32[8,224,768]{2,1,0:T(8,128)} %get-tuple-element.108.x_i, ...), custom_call_target="tpu_custom_call" | custom-call | flops 33822867456 | bytes 53989376 | tf_op jit(solution)/shard_map/last_mlp/pallas_call | solution.py:539
  328.4 4.5 copy.34
  332.9 25.4 %last_mlp_grads.1 = (bf16[768,3072]{1,0:T(8,128)(2,1)}, bf16[768,3072]{1,0:T(8,128)(2,1)}) custom-call(bf16[1792,768]{1,0:T(8,128)(2,1)} %bitcast.38, bf16[1792,3072]{1,0:T(8,128)(2,1)} %bitcast.31, bf16[1792,768]{1,0:T(8,128)(2,1)} %bitcast.39, bf16[1792,3072]{1,0:T(8,128)(2,1)} %bitcast.30), custom_call_target="tpu_custom_call" | custom-call | flops 16911433728 | bytes 36962304 | tf_op jit(solution)/shard_map/last_mlp_grads/pallas_call | solution.py:665
  358.3 46.6 %channel_backward.1 = (f32[8,224,768]{2,1,0:T(8,128)}, bf16[8,224,768]{2,1,0:T(8,128)(2,1)}, bf16[8,224,2304]{2,1,0:T(8,128)(2,1)}, f32[16,768]{1,0:T(8,128)}, f32[1,2304]{1,0:T(1,128)}, /*index=5*/f32[192,384]{1,0:T(8,128)}) custom-call(f32[8,224,768]{2,1,0:T(8,128)} %get-tuple-element.112.refs_0_, f32[8,224,768]{2,1,0:T(8,128)} %get-tuple-element.106.refs_0_.refs_1_, ...), custom_call_target="tpu_custom_call" | custom-call | flops 10569646080 | bytes 56255488 | tf_op jit(solution)/shard_map/channel_backward/pallas_call | solution.py:539
  404.8 44.8 %mlp_backward.1 = (f32[8,224,768]{2,1,0:T(8,128)}, bf16[8,224,768]{2,1,0:T(8,128)(2,1)}, bf16[8,224,3072]{2,1,0:T(8,128)(2,1)}, f32[16,768]{1,0:T(8,128)}, f32[1,3072]{1,0:T(1,128)}, /*index=5*/f32[96,768]{1,0:T(8,128)}) custom-call(f32[8,224,768]{2,1,0:T(8,128)} %get-tuple-element.122.refs_0_, f32[8,224,768]{2,1,0:T(8,128)} %get-tuple-element.100.refs_0_.refs_1_, ...), custom_call_target="tpu_custom_call" | custom-call | flops 16911433728 | bytes 63336448 | tf_op jit(solution)/shard_map/mlp_backward/pallas_call | solution.py:539
  449.6 25.1 %mlp_grads.1 = (bf16[768,3072]{1,0:T(8,128)(2,1)}, bf16[768,3072]{1,0:T(8,128)(2,1)}) custom-call(bf16[1792,768]{1,0:T(8,128)(2,1)} %bitcast.34, bf16[1792,3072]{1,0:T(8,128)(2,1)} %bitcast.29, bf16[1792,768]{1,0:T(8,128)(2,1)} %bitcast.37, bf16[1792,3072]{1,0:T(8,128)(2,1)} %bitcast.28), custom_call_target="tpu_custom_call" | custom-call | flops 16911433728 | bytes 36962304 | tf_op jit(solution)/shard_map/mlp_grads/pallas_call | solution.py:665
  474.7 15.4 %channel_grads.1 = (bf16[768,2304]{1,0:T(8,128)(2,1)}, bf16[768,768]{1,0:T(8,128)(2,1)}) custom-call(bf16[1792,768]{1,0:T(8,128)(2,1)} %bitcast.35, bf16[1792,2304]{1,0:T(8,128)(2,1)} %bitcast.24, bf16[1792,768]{1,0:T(8,128)(2,1)} %bitcast.36, bf16[1792,768]{1,0:T(8,128)(2,1)} %bitcast.26), custom_call_target="tpu_custom_call" | custom-call | flops 8455716864 | bytes 21233664 | tf_op jit(solution)/shard_map/channel_grads/pallas_call | solution.py:665
  490.1 6.0 pack_attention.1.refs_11_
  496.1 93.3 %window_backward.1 = (bf16[8,14,14,768]{3,2,1,0:T(8,128)(2,1)}, bf16[8,224,768]{2,1,0:T(8,128)(2,1)}, bf16[8,224,2304]{2,1,0:T(8,128)(2,1)}, f32[16,768]{1,0:T(8...) custom-call(f32[8,224,768]{2,1,0:T(8,128)} %get-tuple-element.127.refs_0_, ...), custom_call_target="tpu_custom_call" | custom-call | flops 12683575296 | bytes 61760512 | tf_op jit(solution)/shard_map/window_backward/pallas_call | solution.py:539
  589.5 4.5 copy.35
  594.0 0.0 copy-start.1
  594.0 0.0 copy-start.2
  594.0 0.0 copy-start.3
  594.0 0.0 copy-start.4
  594.0 15.3 %window_grads.1 = (bf16[768,2304]{1,0:T(8,128)(2,1)}, bf16[768,768]{1,0:T(8,128)(2,1)}) custom-call(bf16[1792,768]{1,0:T(8,128)(2,1)} %bitcast.32, bf16[1792,2304]{1,0:T(8,128)(2,1)} %bitcast.25, bf16[1792,768]{1,0:T(8,128)(2,1)} %bitcast.33, bf16[1792,768]{1,0:T(8,128)(2,1)} %bitcast.27), custom_call_target="tpu_custom_call" | custom-call | flops 8455716864 | bytes 21233664 | tf_op jit(solution)/shard_map/window_grads/pallas_call | solution.py:665
  609.3 0.0 copy-done.1
  609.3 0.0 copy-done.2
  609.3 0.0 copy-done.3
  609.3 0.0 copy-done.4
  609.3 0.7 pad_maximum_fusion.small
  610.0 6.5 pack_first.1.refs_0_
  616.5 36.4 %reduce_last.1.att0 = f32[208,384]{1,0:T(8,128)} custom-call(bf16[32,208,384]{2,1,0:T(8,128)(2,1)} %pack_first.1.refs_0_), custom_call_target="tpu_custom_call" | custom-call | bytes 5111808 | tf_op jit(solution)/shard_map/reduce_last/pallas_call | solution.py:938
  652.9 3.3 finish.1
  656.2 1.3 copy.36
  657.5 2.2 copy.37
  (2 shorter events, 0.0 us)
Async XLA Ops:
  0.6 7.9 %copy-start = (bf16[8,14,14,768]{3,0,2,1:T(8,128)(2,1)S(1)}, bf16[8,14,14,768]{3,0,2,1:T(8,128)(2,1)}, u32[]{:S(2)}) copy-start(bf16[8,14,14,768]{3,0,2,1:T(8,128)(2,1)} %param.31) | copy-start | bytes 7225348
  594.0 15.3 %copy-start.1 = (f32[16,768]{1,0:T(8,128)S(1)}, f32[16,768]{1,0:T(8,128)}, u32[]{:S(2)}) copy-start(f32[16,768]{1,0:T(8,128)} %get-tuple-element.154) | copy-start | bytes 147460
  594.0 15.3 %copy-start.2 = (f32[16,768]{1,0:T(8,128)S(1)}, f32[16,768]{1,0:T(8,128)}, u32[]{:S(2)}) copy-start(f32[16,768]{1,0:T(8,128)} %get-tuple-element.153) | copy-start | bytes 147460
  594.0 15.3 %copy-start.3 = (f32[16,768]{1,0:T(8,128)S(1)}, f32[16,768]{1,0:T(8,128)}, u32[]{:S(2)}) copy-start(f32[16,768]{1,0:T(8,128)} %get-tuple-element.152) | copy-start | bytes 147460
  594.0 15.3 %copy-start.4 = (f32[16,768]{1,0:T(8,128)S(1)}, f32[16,768]{1,0:T(8,128)}, u32[]{:S(2)}) copy-start(f32[16,768]{1,0:T(8,128)} %get-tuple-element.151) | copy-start | bytes 147460

commit v5 on v4

--- a/solution.py
+++ b/solution.py
@@ -680,38 +680,71 @@
 WIDE = 8
 NARROW = 4
 BOTH = ("narrow", "wide")
-AXES = (("wide", 2), ("wide", 4), ("wide", 1), ("narrow", 2), ("narrow", 1))
-ORDERS = ((0, 1, 2, 3), (0, 1, 3, 2))
 MESH_ID = pl.DeviceIdType.MESH
+RING = (0, 1, -1, 2, -2, 3, -3, 4)
+AFAR = RING[::-1]
+GATHER_STEPS = (((0,), ()), ((1, -1), (0,)), ((2, -2), (1, -1)), ((3, -3), (2, -2)), ((4,), (3, -3)), ((), (4,)))
+REDUCE_STEPS = ((), (15, 11), (7, 14, 10), (3, 6, 13), (2, 9), (5, 12), (1, 8, 4), (0,))
 STAGES = (0, 4, 8, 12, 1, 5, 9, 13, 2, 6, 10, 14, 3, 7, 11, 15)
-GATHER_STEPS = ((0,), (1, 2, 4, 8), (5, 12, 9), (3, 6, 10), (13, 7), (14, 11), (15,))
-REDUCE_STEPS = ((), (15, 11), (7, 14, 10), (3, 6, 13), (2, 9), (5, 12), (1, 8, 4), (0,))
-
-
-def flip(value, bit):
-    return value + bit - 2 * bit * ((value // bit) % 2)
-
-
-def place(order, rel):
-    at = {"narrow": lax.axis_index("narrow"), "wide": lax.axis_index("wide")}
-    for i, axis in enumerate(tuple(ORDERS[order]) + (4,)):
-        if rel & (1 << i):
-            name, bit = AXES[axis]
-            at[name] = flip(at[name], bit)
-    return at
+CARRY_STEPS = 8
+
+
+def whole_part(condition):
+    return jnp.where(condition, jnp.int32(1), jnp.int32(0))
+
+
+def place(order, ring, cross=0, core=0):
+    n, w = lax.axis_index("narrow"), lax.axis_index("wide")
+    z = whole_part(w >= 2) + whole_part(w >= 4) + whole_part(w >= 6)
+    y = whole_part(n >= 2)
+    x, c = w - 2 * z, n - 2 * y
+    a, b = (x, y) if order == 0 else (y, x)
+    if ring:
+        at = z + a * (7 - 2 * z) + ring
+        at = at - 8 * whole_part(at >= 8) if ring > 0 else at + 8 * whole_part(at < 0)
+        a = whole_part(at >= 4)
+        z = at + a * (7 - 2 * at)
+    if cross:
+        b = 1 - b
+    if core:
+        c = 1 - c
+    x, y = (a, b) if order == 0 else (b, a)
+    return {"narrow": 2 * y + c, "wide": 2 * z + x}
+
+
+def chip(order, rel):
+    n, w = lax.axis_index("narrow"), lax.axis_index("wide")
+    z1 = whole_part(w >= 4)
+    z0 = whole_part(w - 4 * z1 >= 2)
+    y = whole_part(n >= 2)
+    x, c = w - 4 * z1 - 2 * z0, n - 2 * y
+    first, second = (4, 8) if order == 0 else (8, 4)
+    bits = (1, 2, first, second, 16)
+    z0, z1, x, y, c = (1 - v if rel & bit else v for v, bit in zip((z0, z1, x, y, c), bits))
+    return {"narrow": 2 * y + c, "wide": 4 * z1 + 2 * z0 + x}
 
 
 def highest(rel):
     return rel.bit_length() - 1
 
 
-def meet():
+def number(ring, cross=0, core=0):
+    return ring % 8 + 8 * cross + 16 * core
+
+
+def ring_peers():
+    return [place(0, 1), place(0, -1), place(1, 1), place(1, -1), place(0, 0, 1), place(1, 0, 1), place(0, 0, 0, 1)]
+
+
+def chip_peers():
+    return [chip(0, 1 << k) for k in range(5)]
+
+
+def meet(peers):
     barrier = pltpu.get_barrier_semaphore()
-    for name, bit in AXES:
-        at = {"narrow": lax.axis_index("narrow"), "wide": lax.axis_index("wide")}
-        at[name] = flip(at[name], bit)
+    for at in peers:
         pl.semaphore_signal(barrier, inc=1, device_id=at, device_id_type=MESH_ID)
-    pl.semaphore_wait(barrier, 5)
+    pl.semaphore_wait(barrier, len(peers))
 
 
 class Part:
@@ -735,8 +768,13 @@
         at = pl.multiple_of(a * rows + self.start, step)
         return ref.at[pl.ds(at, self.size), pl.ds(pl.multiple_of(b * cols, cols), cols)]
 
-    def of(self, ref, rel):
-        at = place(self.order, rel)
+    def of(self, ref, *where):
+        at = place(self.order, *where)
+        return self.view(ref, at["narrow"], at["wide"])
+
+
+    def of_chip(self, ref, rel):
+        at = chip(self.order, rel)
         return self.view(ref, at["narrow"], at["wide"])
 
 
@@ -755,39 +793,69 @@
         self.own = own.at[pl.ds(part.start, part.size), :]
         self.send, self.recv, self.keep = sems
 
-    def copy(self, rel, axis):
-        target = self.part.of(self.dest, rel)
-        slot = rel | (1 << axis)
+    def copy(self, ring, cross, step):
+        target = self.part.of(self.dest, ring, cross)
+        if step is None:
+            to, slot = place(self.part.order, 0, 0, 1), number(ring, cross, 1)
+        elif step == 0:
+            to, slot = place(self.part.order, 0, 1), number(ring, 1)
+        else:
+            to, slot = place(self.part.order, step), number(ring - step)
         return pltpu.make_async_remote_copy(
-            src_ref=self.own if rel == 0 else target, dst_ref=target, send_sem=self.send.at[self.index, slot],
-            recv_sem=self.recv.at[self.index, slot], device_id=place(self.part.order, 1 << axis), device_id_type=MESH_ID,
+            src_ref=self.own if ring == 0 and cross == 0 else target, dst_ref=target,
+            send_sem=self.send.at[self.index, slot], recv_sem=self.recv.at[self.index, slot],
+            device_id=to, device_id_type=MESH_ID,
         )
 
-    def arrival(self, rel):
-        target = self.part.of(self.dest, rel)
+    def arrival(self, ring, cross=0, core=0):
+        target = self.part.of(self.dest, ring, cross, core)
         return pltpu.make_async_remote_copy(
             src_ref=target, dst_ref=target, send_sem=self.send.at[self.index, 0],
-            recv_sem=self.recv.at[self.index, rel], device_id=place(self.part.order, 1), device_id_type=MESH_ID,
+            recv_sem=self.recv.at[self.index, number(ring, cross, core)], device_id=place(self.part.order, 1),
+            device_id_type=MESH_ID,
         )
 
     def stay(self):
         return pltpu.make_async_copy(self.own, self.part.of(self.dest, 0), self.keep.at[self.index])
 
-    def stage(self, rel):
-        if rel == 0:
+    def sends(self, ring):
+        steps = []
+        if 0 <= ring < 4:
+            steps.append(-1)
+        if -3 < ring <= 0:
+            steps.append(1)
+        return steps + [0, None]
+
+    def stage(self, ring):
+        if ring == 0:
             self.stay().start()
         else:
-            self.arrival(rel).wait_recv()
-        for axis in reversed(range(highest(rel) + 1, 5)):
-            self.copy(rel, axis).start()
+            self.arrival(ring).wait_recv()
+        for step in self.sends(ring):
+            self.copy(ring, 0, step).start()
+
+    def crossed(self, ring):
+        self.arrival(ring, 1).wait_recv()
+        self.copy(ring, 1, None).start()
 
     def finish(self):
-        for rel in range(16, 32):
-            self.arrival(rel).wait_recv()
-        for rel in range(16):
-            for axis in range(highest(rel) + 1, 5):
-                self.copy(rel, axis).wait_send()
+        for ring in RING:
+            self.arrival(ring, 0, 1).wait_recv()
+            self.arrival(ring, 1, 1).wait_recv()
+        for ring in RING:
+            for step in self.sends(ring):
+                self.copy(ring, 0, step).wait_send()
+            self.copy(ring, 1, None).wait_send()
         self.stay().wait()
+
+
+def gather_step(items, rings, crosses):
+    for ring in rings:
+        for item in items:
+            item.stage(ring)
+    for ring in crosses:
+        for item in items:
+            item.crossed(ring)
 
 
 def gather_sems(count):
@@ -809,15 +877,13 @@
 
     def run(self, ins, outs, scratch):
         items = self.items(ins, outs, scratch)
-        for s, rels in enumerate(GATHER_STEPS):
+        for s, (rings, crosses) in enumerate(GATHER_STEPS):
 
             @pl.when(pl.program_id(0) == s)
-            def _(s=s, rels=rels):
+            def _(s=s, rings=rings, crosses=crosses):
                 if s == 0:
-                    meet()
-                for rel in rels:
-                    for item in items:
-                        item.stage(rel)
+                    meet(ring_peers())
+                gather_step(items, rings, crosses)
 
     def end(self, ins, outs, scratch):
         @pl.when(last_step())
@@ -833,19 +899,19 @@
         self.load_sem, self.send_sem, self.mate_sem, self.recv_sem = sems
 
     def load(self, rel):
-        return pltpu.make_async_copy(self.part.of(self.src, rel), self.acc.at[rel], self.load_sem.at[self.index, rel])
+        return pltpu.make_async_copy(self.part.of_chip(self.src, rel), self.acc.at[rel], self.load_sem.at[self.index, rel])
 
     def to_mate(self, rel):
         return pltpu.make_async_remote_copy(
-            src_ref=self.part.of(self.src, rel | 16), dst_ref=self.mate.at[rel],
+            src_ref=self.part.of_chip(self.src, rel | 16), dst_ref=self.mate.at[rel],
             send_sem=self.send_sem.at[self.index, 16 + rel], recv_sem=self.mate_sem.at[self.index, rel],
-            device_id=place(self.part.order, 16), device_id_type=MESH_ID,
+            device_id=chip(self.part.order, 16), device_id_type=MESH_ID,
         )
 
     def onward(self, rel):
         return pltpu.make_async_remote_copy(
             src_ref=self.acc.at[rel], dst_ref=self.inbox.at[rel - 1], send_sem=self.send_sem.at[self.index, rel],
-            recv_sem=self.recv_sem.at[self.index, rel], device_id=place(self.part.order, 1 << highest(rel)),
+            recv_sem=self.recv_sem.at[self.index, rel], device_id=chip(self.part.order, 1 << highest(rel)),
             device_id_type=MESH_ID,
         )
 
@@ -904,7 +970,7 @@
             @pl.when(pl.program_id(0) == s)
             def _(s=s, rels=rels):
                 if s == 0:
-                    meet()
+                    meet(chip_peers())
                     for rel in reversed(STAGES):
                         for item in items:
                             item.begin(rel)
@@ -923,7 +989,7 @@
     ins, refs = refs[: len(plan.args)], refs[len(plan.args) :]
     outs, scratch = refs[: len(plan.outs)], refs[len(plan.outs) :]
     items = plan.items(ins, outs, scratch)
-    meet()
+    meet(chip_peers())
     for rel in reversed(STAGES):
         for item in items:
             item.begin(rel)
@@ -1114,16 +1180,14 @@
     piece[pl.ds(16, cn), pl.ds(0, 3 * cw)] = turned(qkv0[...])
     piece[pl.ds(16, cn), pl.ds(3 * cw, cw)] = turned(proj[0])
     items = plan.items([piece], [got], sems)
-    meet()
-    for item in items:
-        item.stage(0)
+    meet(ring_peers())
+    gather_step(items, (0,), ())
     in0[...] = turned(mlp_in[0])
     in1[...] = turned(mlp_in[1])
     chan[:, pl.ds(0, 3 * cw)] = turned(qkv1[...])
     chan[:, pl.ds(3 * cw, cw)] = turned(proj[1])
-    for rel in STAGES[1:]:
-        for item in items:
-            item.stage(rel)
+    for rings, crosses in GATHER_STEPS[1:]:
+        gather_step(items, rings, crosses)
     for item in items:
         item.finish()
 
@@ -1327,7 +1391,7 @@
 
 
 def local(plan, inputs, heights, widths, *rest):
-    if inputs.shape[0] != len(REDUCE_STEPS):
+    if inputs.shape[0] != CARRY_STEPS:
         plan = Plain
     weights = plan(dict(zip(NAMES, rest[:-1])))
     cotangent = rest[-1]

time: 663 us -> 634 us (0.956)
  Pallas kernels: 636 us -> 606 us
    pallas_call x1, Pallas kernels: 46.3 us -> 31 us  [gather_first(): pl.pallas_call(functools.partial(gather_first_kernel, plan), in_specs=[vm...]
    pallas_call x7, Pallas kernels: 444 us -> 429 us  [image_call(): pl.pallas_call(body, grid=(images,), in_specs=ins, out_specs=out_specs, o...]
where the time goes in v5:
time: 634 us; the launch traced here: 630 us
  Pallas kernels  606 us (96%)
  local copies, waits for them, and re-layouts  21.5 us (3%)
    pallas_call x7, Pallas kernels, image_call(): pl.pallas_call(body, grid=(images,), in_specs=ins, out_specs=out_specs, o...  429 us
    pallas_call x4, Pallas kernels, grad_pair(): pl.pallas_call(functools.partial(grad_pair_kernel, first), grid=(first +...  81.2 us
    pallas_call x1, Pallas kernels, reduce_now(): pl.pallas_call(functools.partial(reduce_kernel, plan), in_specs=[pl.Block...  36.1 us
    pallas_call x1, Pallas kernels, gather_first(): pl.pallas_call(functools.partial(gather_first_kernel, plan), in_specs=[vm...  31 us
    unnamed x17, local copies, waits for them, and re-layouts  20.2 us

profile of v5, /device:TPU:0, one launch (start us, length us, event | category | flops | bytes accessed | tf_op | source)
XLA Modules:
  0.0 630.2 jit_solution(17245439927021196246)
XLA Ops:
  0.6 0.0 copy-start
  0.7 0.9 and_convert_fusion
  1.6 1.9 copy.30.mlp_in
  3.5 1.3 broadcast_in_dim.2.refs_1_.mask.refs_6_.refs_5_
  4.8 3.7 copy.31.refs_0_.refs_1_
  8.5 0.0 copy-done
  8.5 2.0 copy.32.cot
  10.5 31.0 %gather_first.1 = (bf16[32,208,384]{2,1,0:T(8,128)(2,1)}, bf16[192,384]{1,0:T(8,128)(2,1)}, bf16[192,384]{1,0:T(8,128)(2,1)}, bf16[192,384]{1,0:T(8,128)(2,1)}) custom-call(bf16[1,9,96]{2,1,0:T(8,128)(2,1)} %conv_weight.1, bf16[1,96]{1,0:T(2,128)(2,1)} %conv_bias.1, bf16[1,96]{1,0:T(2,128)(2,1)} %norm_gain.1, bf16[1,96]{1,0:T(2,128)(2,1)} %norm_bias.1, ...), custom_call_target="tpu_custom_call" | custom-call | bytes 5554176 | tf_op jit(solution)/shard_map/gather_first/pallas_call | solution.py:1203
  41.6 6.6 %unpack_first.1 = (bf16[768,3072]{1,0:T(8,128)(2,1)}, f32[4,16,768]{2,1,0:T(8,128)}, f32[16,768]{1,0:T(8,128)}, f32[2,1,3072]{2,1,0:T(1,128)}) custom-call(bf16[32,208,384]{2,1,0:T(8,128)(2,1)} %get-tuple-element.95.got), custom_call_target="tpu_custom_call" | custom-call | bytes 10100736 | tf_op jit(solution)/shard_map/unpack_first/pallas_call | solution.py:1049
  48.2 70.4 %window_forward.1 = (bf16[8,224,768]{2,1,0:T(8,128)(2,1)}, f32[8,224,768]{2,1,0:T(8,128)}, f32[8,224,128]{2,1,0:T(8,128)}, bf16[8,224,2304]{2,1,0:T(8,128)(2,1)}...) custom-call(bf16[8,14,14,768]{3,2,1,0:T(8,128)(2,1)} %copy.31.refs_0, ...), custom_call_target="tpu_custom_call" | custom-call | flops 10569646080 | bytes 48676864 | tf_op jit(solution)/shard_map/window_forward/pallas_call | solution.py:539
  118.6 60.5 %mlp_forward.1 = (bf16[8,224,768]{2,1,0:T(8,128)(2,1)}, f32[8,224,768]{2,1,0:T(8,128)}, f32[8,224,128]{2,1,0:T(8,128)}, bf16[8,224,3072]{2,1,0:T(8,128)(2,1)}, b...) custom-call(f32[8,224,768]{2,1,0:T(8,128)} %get-tuple-element.100.re, ...), custom_call_target="tpu_custom_call" | custom-call | flops 16911433728 | bytes 62513152 | tf_op jit(solution)/shard_map/mlp_forward/pallas_call | solution.py:539
  179.1 6.1 unpack_attention.1.refs_4_.refs_8_
  185.2 42.9 %channel_forward.1 = (bf16[8,224,768]{2,1,0:T(8,128)(2,1)}, f32[8,224,768]{2,1,0:T(8,128)}, f32[8,224,128]{2,1,0:T(8,128)}, bf16[8,224,2304]{2,1,0:T(8,128)(2,1)...) custom-call(f32[8,224,768]{2,1,0:T(8,128)} %get-tuple-element.106.re, ...), custom_call_target="tpu_custom_call" | custom-call | flops 9512681472 | bytes 45236224 | tf_op jit(solution)/shard_map/channel_forward/pallas_call | solution.py:539
  228.1 70.5 %last_mlp.1 = (bf16[8,14,14,768]{3,2,1,0:T(8,128)(2,1)}, f32[8,224,768]{2,1,0:T(8,128)}, bf16[8,224,768]{2,1,0:T(8,128)(2,1)}, bf16[8,224,3072]{2,1,0:T(8,128)(2...) custom-call(f32[8,224,768]{2,1,0:T(8,128)} %get-tuple-element.108.x_i, ...), custom_call_target="tpu_custom_call" | custom-call | flops 33822867456 | bytes 53989376 | tf_op jit(solution)/shard_map/last_mlp/pallas_call | solution.py:539
  298.6 4.5 copy.34
  303.1 25.4 %last_mlp_grads.1 = (bf16[768,3072]{1,0:T(8,128)(2,1)}, bf16[768,3072]{1,0:T(8,128)(2,1)}) custom-call(bf16[1792,768]{1,0:T(8,128)(2,1)} %bitcast.38, bf16[1792,3072]{1,0:T(8,128)(2,1)} %bitcast.31, bf16[1792,768]{1,0:T(8,128)(2,1)} %bitcast.39, bf16[1792,3072]{1,0:T(8,128)(2,1)} %bitcast.30), custom_call_target="tpu_custom_call" | custom-call | flops 16911433728 | bytes 36962304 | tf_op jit(solution)/shard_map/last_mlp_grads/pallas_call | solution.py:665
  328.5 46.4 %channel_backward.1 = (f32[8,224,768]{2,1,0:T(8,128)}, bf16[8,224,768]{2,1,0:T(8,128)(2,1)}, bf16[8,224,2304]{2,1,0:T(8,128)(2,1)}, f32[16,768]{1,0:T(8,128)}, f32[1,2304]{1,0:T(1,128)}, /*index=5*/f32[192,384]{1,0:T(8,128)}) custom-call(f32[8,224,768]{2,1,0:T(8,128)} %get-tuple-element.112.refs_0_, f32[8,224,768]{2,1,0:T(8,128)} %get-tuple-element.106.refs_0_.refs_1_, ...), custom_call_target="tpu_custom_call" | custom-call | flops 10569646080 | bytes 56255488 | tf_op jit(solution)/shard_map/channel_backward/pallas_call | solution.py:539
  374.9 44.8 %mlp_backward.1 = (f32[8,224,768]{2,1,0:T(8,128)}, bf16[8,224,768]{2,1,0:T(8,128)(2,1)}, bf16[8,224,3072]{2,1,0:T(8,128)(2,1)}, f32[16,768]{1,0:T(8,128)}, f32[1,3072]{1,0:T(1,128)}, /*index=5*/f32[96,768]{1,0:T(8,128)}) custom-call(f32[8,224,768]{2,1,0:T(8,128)} %get-tuple-element.122.refs_0_, f32[8,224,768]{2,1,0:T(8,128)} %get-tuple-element.100.refs_0_.refs_1_, ...), custom_call_target="tpu_custom_call" | custom-call | flops 16911433728 | bytes 63336448 | tf_op jit(solution)/shard_map/mlp_backward/pallas_call | solution.py:539
  419.7 25.1 %mlp_grads.1 = (bf16[768,3072]{1,0:T(8,128)(2,1)}, bf16[768,3072]{1,0:T(8,128)(2,1)}) custom-call(bf16[1792,768]{1,0:T(8,128)(2,1)} %bitcast.34, bf16[1792,3072]{1,0:T(8,128)(2,1)} %bitcast.29, bf16[1792,768]{1,0:T(8,128)(2,1)} %bitcast.37, bf16[1792,3072]{1,0:T(8,128)(2,1)} %bitcast.28), custom_call_target="tpu_custom_call" | custom-call | flops 16911433728 | bytes 36962304 | tf_op jit(solution)/shard_map/mlp_grads/pallas_call | solution.py:665
  444.8 15.4 %channel_grads.1 = (bf16[768,2304]{1,0:T(8,128)(2,1)}, bf16[768,768]{1,0:T(8,128)(2,1)}) custom-call(bf16[1792,768]{1,0:T(8,128)(2,1)} %bitcast.35, bf16[1792,2304]{1,0:T(8,128)(2,1)} %bitcast.24, bf16[1792,768]{1,0:T(8,128)(2,1)} %bitcast.36, bf16[1792,768]{1,0:T(8,128)(2,1)} %bitcast.26), custom_call_target="tpu_custom_call" | custom-call | flops 8455716864 | bytes 21233664 | tf_op jit(solution)/shard_map/channel_grads/pallas_call | solution.py:665
  460.2 6.0 pack_attention.1.refs_11_
  466.2 93.8 %window_backward.1 = (bf16[8,14,14,768]{3,2,1,0:T(8,128)(2,1)}, bf16[8,224,768]{2,1,0:T(8,128)(2,1)}, bf16[8,224,2304]{2,1,0:T(8,128)(2,1)}, f32[16,768]{1,0:T(8...) custom-call(f32[8,224,768]{2,1,0:T(8,128)} %get-tuple-element.127.refs_0_, ...), custom_call_target="tpu_custom_call" | custom-call | flops 12683575296 | bytes 61760512 | tf_op jit(solution)/shard_map/window_backward/pallas_call | solution.py:539
  560.0 4.5 copy.35
  564.6 0.0 copy-start.1
  564.6 0.0 copy-start.2
  564.6 0.0 copy-start.3
  564.6 0.0 copy-start.4
  564.6 15.3 %window_grads.1 = (bf16[768,2304]{1,0:T(8,128)(2,1)}, bf16[768,768]{1,0:T(8,128)(2,1)}) custom-call(bf16[1792,768]{1,0:T(8,128)(2,1)} %bitcast.32, bf16[1792,2304]{1,0:T(8,128)(2,1)} %bitcast.25, bf16[1792,768]{1,0:T(8,128)(2,1)} %bitcast.33, bf16[1792,768]{1,0:T(8,128)(2,1)} %bitcast.27), custom_call_target="tpu_custom_call" | custom-call | flops 8455716864 | bytes 21233664 | tf_op jit(solution)/shard_map/window_grads/pallas_call | solution.py:665
  579.9 0.0 copy-done.1
  579.9 0.0 copy-done.2
  579.9 0.0 copy-done.3
  579.9 0.0 copy-done.4
  579.9 0.7 pad_maximum_fusion.small
  580.6 6.5 %pack_first.1.refs_0_ = bf16[32,208,384]{2,1,0:T(8,128)(2,1)} custom-call(bf16[768,2304]{1,0:T(8,128)(2,1)} %get-tuple-element.149.gq, bf16[768,768]{1,0:T(8,128)(2,1)} %get-tuple-element.150.gp, f32[4,16,768]{2,1,0:T(8,128)} %pad_maximum_fusion.small, f32[1,2304]{1,0:T(1,128)} %get-tuple-element.155.sb, f32[1,2304]{1,0:T(1,128)} %get-tuple-element.156.cb, ...), custom_call_target="tpu_custom_call" | custom-call | bytes 10223616 | tf_op jit(solution)/shard_map/pack_first/pallas_call | solution.py:1140
  587.1 36.1 %reduce_last.1.att0 = f32[208,384]{1,0:T(8,128)} custom-call(bf16[32,208,384]{2,1,0:T(8,128)(2,1)} %pack_first.1.refs_0_), custom_call_target="tpu_custom_call" | custom-call | bytes 5111808 | tf_op jit(solution)/shard_map/reduce_last/pallas_call | solution.py:1004
  623.1 3.3 finish.1
  626.4 1.3 copy.36
  627.7 2.2 copy.37
  (2 shorter events, 0.0 us)
Async XLA Ops:
  0.6 7.9 %copy-start = (bf16[8,14,14,768]{3,0,2,1:T(8,128)(2,1)S(1)}, bf16[8,14,14,768]{3,0,2,1:T(8,128)(2,1)}, u32[]{:S(2)}) copy-start(bf16[8,14,14,768]{3,0,2,1:T(8,128)(2,1)} %param.31) | copy-start | bytes 7225348
  564.6 15.3 %copy-start.1 = (f32[16,768]{1,0:T(8,128)S(1)}, f32[16,768]{1,0:T(8,128)}, u32[]{:S(2)}) copy-start(f32[16,768]{1,0:T(8,128)} %get-tuple-element.154) | copy-start | bytes 147460
  564.6 15.3 %copy-start.2 = (f32[16,768]{1,0:T(8,128)S(1)}, f32[16,768]{1,0:T(8,128)}, u32[]{:S(2)}) copy-start(f32[16,768]{1,0:T(8,128)} %get-tuple-element.153) | copy-start | bytes 147460
  564.6 15.3 %copy-start.3 = (f32[16,768]{1,0:T(8,128)S(1)}, f32[16,768]{1,0:T(8,128)}, u32[]{:S(2)}) copy-start(f32[16,768]{1,0:T(8,128)} %get-tuple-element.152) | copy-start | bytes 147460
  564.6 15.3 %copy-start.4 = (f32[16,768]{1,0:T(8,128)S(1)}, f32[16,768]{1,0:T(8,128)}, u32[]{:S(2)}) copy-start(f32[16,768]{1,0:T(8,128)} %get-tuple-element.151) | copy-start | bytes 147460

commit v6 on v5

--- a/solution.py
+++ b/solution.py
@@ -34,18 +34,44 @@
     return ((r // WIN) * 2 + half) * WTOK + (r % WIN) * SUB
 
 
-def load_cells(src, dst):
+def fill_cells(src, cells):
+    for j in range(cells.shape[0]):
+        cells[j] = src[:, pl.ds(j * LANES, LANES)].astype(F32)
+
+
+def drain_cells(cells, dst):
+    for j in range(cells.shape[0]):
+        dst[:, pl.ds(j * LANES, LANES)] = cells[j].astype(BF16)
+
+
+def cell_rows(cells, r, half):
+    images = cells.shape[1] // (4 * WIN * WIN)
+    start = (r * 2 * WIN + WIN * half) * images
+    if images == 1:
+        return pl.ds(start, WIN)
+    return pl.ds(start + pl.program_id(0), WIN, stride=images)
+
+
+def load_cells(cells, dst):
     for r in range(2 * WIN):
-        row = src[0, r].astype(F32)
-        dst[pl.ds(tok(r, 0), WIN), :] = row[:WIN]
-        dst[pl.ds(tok(r, 1), WIN), :] = row[WIN:]
-
-
-def store_cells(value_at, dst, stage):
+        for half in range(2):
+            for j in range(cells.shape[0]):
+                dst[pl.ds(tok(r, half), WIN), pl.ds(j * LANES, LANES)] = cells.at[j][cell_rows(cells, r, half), :]
+
+
+def store_cells(src, cells):
     for r in range(2 * WIN):
-        stage[pl.ds(0, SUB), :] = value_at(tok(r, 0))
-        stage[pl.ds(WIN, SUB), :] = value_at(tok(r, 1))
-        dst[0, r] = stage[pl.ds(0, 2 * WIN), :].astype(BF16)
+        for half in range(2):
+            for j in range(cells.shape[0]):
+                cells.at[j][cell_rows(cells, r, half), :] = src[pl.ds(tok(r, half), WIN), pl.ds(j * LANES, LANES)]
+
+
+def cells_first(images):
+    return images.transpose(1, 2, 0, 3).reshape(-1, images.shape[3])
+
+
+def images_first(cells):
+    return cells.reshape(2 * WIN, 2 * WIN, -1, cells.shape[1]).transpose(2, 0, 1, 3)
 
 
 def neighbours(left, right):
@@ -216,15 +242,16 @@
 def window_forward_kernel(
     inp, mask, lay, sh, watt,
     n_out, z_out, r_out, q_out, o_out, p_out, x_out,
-    x0, x1, qf, of,
+    cells, x0, x1, qf, of,
 ):
     features = x0.shape[1]
 
     @pl.when(first_step())
     def _():
         x0[...] = jnp.zeros_like(x0)
-
-    load_cells(inp, x0)
+        fill_cells(inp, cells)
+
+    load_cells(cells, x0)
     conv_forward(x0, mask, lay, x1)
     norm_forward(x1, lay, z_out.at[0], r_out.at[0], n_out.at[0])
     chunk = features
@@ -312,16 +339,17 @@
 def last_mlp_kernel(
     x_in, cot, mask, lay, hb, w_in, w_out,
     out, g_out, n_out, u_out, gy_out, gh_out, small_out, hidden_out,
-    x1, z, r, acc, dn, g8, stage, sums, hsums,
+    cells, x1, z, r, acc, dn, g8, sums, hsums,
 ):
     @pl.when(first_step())
     def _():
         g8[...] = jnp.zeros_like(g8)
         sums[...] = jnp.zeros_like(sums)
         hsums[...] = jnp.zeros_like(hsums)
+        fill_cells(cot, cells)
 
     x6 = x_in.at[0]
-    load_cells(cot, g8)
+    load_cells(cells, g8)
     conv_forward(x6, mask, lay, x1)
     norm_forward(x1, lay, z, r, n_out.at[0])
     g8[...] = g8[...] * mask[0, :, 0:1]
@@ -342,12 +370,13 @@
         acc[...] = y if c == 0 else acc[...] + y
         dn[...] = dx if c == 0 else dn[...] + dx
     acc[...] = (x1[...] + (acc[...] + lay_row(lay, 12))) * mask[0, :, 0:1]
-    store_cells(lambda at: acc[pl.ds(at, SUB), :], out, stage)
+    store_cells(acc, cells)
     norm_backward(dn, z, r, lay, g8, sums, 10 * SUB, x1)
     conv_backward(x6, x1, mask, lay, sums, g_out.at[0])
 
     @pl.when(last_step())
     def _():
+        drain_cells(cells, out)
         finish_sums(sums, small_out)
         finish_sums(hsums, hidden_out)
 
@@ -421,7 +450,7 @@
 def window_backward_kernel(
     g_in, inp, z_in, r_in, q_in, p_in, mask, lay, watt,
     g_out, ga_out, dq_out, small_out, bias_out,
-    x0, qf, gof, dqf, dn, g1, stage, sums, bsums,
+    cells, x0, qf, gof, dqf, dn, g1, sums, bsums,
 ):
     features = dn.shape[1]
 
@@ -430,8 +459,9 @@
         x0[...] = jnp.zeros_like(x0)
         sums[...] = jnp.zeros_like(sums)
         bsums[...] = jnp.zeros_like(bsums)
-
-    load_cells(inp, x0)
+        fill_cells(inp, cells)
+
+    load_cells(cells, x0)
     ga_out[0] = g_in[0].astype(BF16)
     sums[pl.ds(12 * SUB, SUB), :] = sums[pl.ds(12 * SUB, SUB), :] + fold_rows(ga_out[0].astype(F32))
     gof[...] = rounded(dot(ga_out[0], watt[:, pl.ds(3 * features, features)], DIMS_NT))
@@ -460,15 +490,18 @@
     dn[...] = dot(dq_out[0], watt[:, pl.ds(0, 3 * features)], DIMS_NT)
     norm_backward(dn, z_in.at[0], r_in.at[0], lay, g_in.at[0], sums, 10 * SUB, g1)
     conv_backward(x0, g1, mask, lay, sums, dn)
-    store_cells(lambda at: dn[pl.ds(at, SUB), :], g_out, stage)
+    store_cells(dn, cells)
 
     @pl.when(last_step())
     def _():
+        drain_cells(cells, g_out)
         finish_sums(sums, small_out)
         finish_sums(bsums, bias_out)
 
 
 def per_image(shape):
+    if len(shape) == 2:
+        return whole(shape)
     rest = (0,) * (len(shape) - 1)
     return pl.BlockSpec((1,) + tuple(shape[1:]), lambda i: (i,) + rest)
 
@@ -504,7 +537,7 @@
 
 
 def image_call(kernel, name, layer, batched, lay, shared, outs, sums, scratch, flops, carry=None):
-    images = batched[0].shape[0]
+    images = next(a.shape[0] for a in batched if a.ndim > 2)
     ins = [per_image(a.shape) for a in batched] + [one_layer(lay.shape, layer)]
     args = list(batched) + [lay]
     for item in shared:
@@ -560,14 +593,13 @@
 
 
 def forward_window(inputs, mask, lay, sh, watt, carry=None):
-    images, _, _, c = inputs.shape
-    t = 4 * WTOK
+    (rows, c), images, t = inputs.shape, mask.shape[0], mask.shape[1]
     outs = [
         ((images, t, c), BF16), ((images, t, c), F32), ((images, t, LANES), F32),
         ((images, t, 3 * c), BF16), ((images, t, c), BF16),
         ((images, 4, c // GROUP, WTOK, WTOK * GROUP // HD), BF16), ((images, t, c), F32),
     ]
-    scratch = [((t, c), F32), ((t, c), F32), ((t, 3 * c), F32), ((t, c), F32)]
+    scratch = [((c // LANES, rows, LANES), F32), ((t, c), F32), ((t, c), F32), ((t, 3 * c), F32), ((t, c), F32)]
     return image_call(window_forward_kernel, "window_forward", 0, [inputs, mask], lay, [sh, watt],
                       outs, [], scratch, 10 * images * t * c * c, carry)
 
@@ -603,8 +635,8 @@
         ((images, t, c), BF16), ((images, t, ff), BF16),
     ]
     scratch = [
-        ((t, c), F32), ((t, c), F32), ((t, LANES), F32), ((t, c), F32), ((t, c), F32), ((t, c), F32),
-        ((16, c), F32), ((16 * SUB, c), F32), ((SUB, ff), F32),
+        ((c // LANES, cot.shape[0], LANES), F32), ((t, c), F32), ((t, c), F32), ((t, LANES), F32), ((t, c), F32),
+        ((t, c), F32), ((t, c), F32), ((16 * SUB, c), F32), ((SUB, ff), F32),
     ]
     return image_call(last_mlp_kernel, "last_mlp", 3, [x, cot, mask], lay, [(hid, 1), w_in, w_out],
                       outs, [((16, c), F32), ((1, ff), F32)], scratch, 8 * images * t * c * ff)
@@ -631,8 +663,8 @@
     images, t, c = g.shape
     outs = [(inputs.shape, BF16), ((images, t, c), BF16), ((images, t, 3 * c), BF16)]
     scratch = [
-        ((t, c), F32), ((t, 3 * c), F32), ((t, c), F32), ((t, 3 * c), F32), ((t, c), F32), ((t, c), F32),
-        ((16, c), F32), ((16 * SUB, c), F32), ((SUB, 3 * c), F32),
+        ((c // LANES, inputs.shape[0], LANES), F32), ((t, c), F32), ((t, 3 * c), F32), ((t, c), F32),
+        ((t, 3 * c), F32), ((t, c), F32), ((t, c), F32), ((16 * SUB, c), F32), ((SUB, 3 * c), F32),
     ]
     return image_call(window_backward_kernel, "window_backward", 0, [g, inputs, z, r, q, p, mask], lay, [watt],
                       outs, [((16, c), F32), ((1, 3 * c), F32)], scratch, 12 * images * t * c * c, carry)
@@ -1081,76 +1113,76 @@
     )(got)
 
 
-def gather_attention(gq, gp, start, dst):
-    cn = gq.shape[0]
-    cw = dst.shape[2] // 4
+def grad_attention_kernel(start, left0, right0, left1, right1, *refs):
+    *head, out, result = refs[:-1] if len(refs) > 2 else refs
+    step = pl.program_id(0)
+    c = right0.shape[1]
+    cn, cw = c // NARROW, c // WIDE
+
+    def spread(s, w, low, high):
+        for n in range(NARROW):
+            at = pl.ds(low - 3 * cw * w, high - low)
+            out[n * WIDE + w, pl.ds(start, cn), at] = result[pl.ds(cn * n, cn), pl.ds(low - c * s, high - low)]
+
+    for s in range(4):
+
+        @pl.when(step == s)
+        def _(s=s):
+            if s < 3:
+                result[...] = dot(left0[...], right0[...], DIMS_TN).astype(BF16)
+                for w in range(WIDE):
+                    low, high = max(3 * cw * w, c * s), min(3 * cw * (w + 1), c * (s + 1))
+                    if low < high:
+                        spread(s, w, low, high)
+            else:
+                result[...] = dot(left1[...], right1[...], DIMS_TN).astype(BF16)
+                for w in range(WIDE):
+                    for n in range(NARROW):
+                        at = pl.ds(3 * cw, cw)
+                        out[n * WIDE + w, pl.ds(start, cn), at] = result[pl.ds(cn * n, cn), pl.ds(cw * w, cw)]
+                if head:
+                    pack_small(*head, out, refs[-1])
+
+
+def pack_small(small, sb, cb, hid0, hid1, out, shared):
+    c = small.shape[2]
+    cw = c // WIDE
+    shared[...] = jnp.zeros_like(shared)
+    shared[pl.ds(0, 1), :] = sb[:, pl.ds(0, c)]
+    shared[pl.ds(1, 1), :] = sb[:, pl.ds(2 * c, c)]
+    for k in range(3):
+        shared[pl.ds(2 + k, 1), :] = cb[:, pl.ds(k * c, c)]
+    for j, hid in enumerate((hid0, hid1)):
+        for w in range(WIDE):
+            for q in range(4):
+                shared[pl.ds(5 + 4 * j + q, 1), pl.ds(cw * w, cw)] = hid[:, pl.ds(4 * cw * w + cw * q, cw)]
+    out[:, pl.ds(0, 16), :] = jnp.zeros((WIDE * NARROW, 16, out.shape[2]), BF16)
     for w in range(WIDE):
-        dst[w, pl.ds(start, cn), pl.ds(0, 3 * cw)] = gq[:, pl.ds(3 * cw * w, 3 * cw)]
-        dst[w, pl.ds(start, cn), pl.ds(3 * cw, cw)] = gp[:, pl.ds(cw * w, cw)]
-
-
-def pack_attention_kernel(gq, gp, out):
-    gather_attention(gq, gp, 0, out)
-
-
-def pack_attention(gq, gp):
-    c = gp.shape[0]
-    cn, lanes = c // NARROW, c // 2
-    shape = (WIDE * NARROW, cn, lanes)
+        for n in range(NARROW):
+            out[n * WIDE + w, pl.ds(0, 16), pl.ds(0, cw)] = small[n, :, pl.ds(cw * w, cw)].astype(BF16)
+            out[n * WIDE + w, pl.ds(0, 16), pl.ds(LANES, cw)] = shared[:, pl.ds(cw * w, cw)].astype(BF16)
+
+
+def grad_attention(name, left0, right0, left1, right1, head=()):
+    flat = [a.reshape(-1, a.shape[-1]) for a in (left0, right0, left1, right1)]
+    rows, c = flat[0].shape
+    cn = c // NARROW
+    start = 16 if head else 0
+    shape = (WIDE * NARROW, start + cn, c // 2)
+    scratch = [pltpu.VMEM((c, c), BF16)] + ([pltpu.VMEM((16, c), F32)] if head else [])
     return pl.pallas_call(
-        pack_attention_kernel,
-        grid=(NARROW,),
-        in_specs=[pl.BlockSpec((cn, 3 * c), lambda n: (n, 0)), pl.BlockSpec((cn, c), lambda n: (n, 0))],
-        out_specs=pl.BlockSpec((WIDE, cn, lanes), lambda n: (n, 0, 0)),
+        functools.partial(grad_attention_kernel, start),
+        grid=(4,),
+        in_specs=[
+            whole((rows, c)), pl.BlockSpec((rows, c), lambda i: (0, jnp.minimum(i, 2))), whole((rows, c)), whole((rows, c)),
+        ] + [whole(a.shape) for a in head],
+        out_specs=pl.BlockSpec(shape, lambda i: (0, 0, 0)),
         out_shape=jax.ShapeDtypeStruct(shape, BF16),
+        scratch_shapes=scratch,
         compiler_params=params(),
-        cost_estimate=cost(0, [(shape, BF16)] * 2),
-        name="pack_attention",
-    )(gq, gp)
-
-
-def pack_first_kernel(gq, gp, small, sb, cb, hid0, hid1, out, shared):
-    gather_attention(gq, gp, 16, out)
-    c = gp.shape[1]
-    cw = c // WIDE
-
-    @pl.when(pl.program_id(0) == 0)
-    def _():
-        shared[...] = jnp.zeros_like(shared)
-        shared[pl.ds(0, 1), :] = sb[:, pl.ds(0, c)]
-        shared[pl.ds(1, 1), :] = sb[:, pl.ds(2 * c, c)]
-        for k in range(3):
-            shared[pl.ds(2 + k, 1), :] = cb[:, pl.ds(k * c, c)]
-        for j, hid in enumerate((hid0, hid1)):
-            for w in range(WIDE):
-                for q in range(4):
-                    shared[pl.ds(5 + 4 * j + q, 1), pl.ds(cw * w, cw)] = hid[:, pl.ds(4 * cw * w + cw * q, cw)]
-
-    out[:, pl.ds(0, 16), :] = jnp.zeros((WIDE, 16, out.shape[2]), BF16)
-    for w in range(WIDE):
-        out[w, pl.ds(0, 16), pl.ds(0, cw)] = small[0, :, pl.ds(cw * w, cw)].astype(BF16)
-        out[w, pl.ds(0, 16), pl.ds(LANES, cw)] = shared[:, pl.ds(cw * w, cw)].astype(BF16)
-
-
-def pack_first(gq, gp, small, sb, cb, hid0, hid1):
-    c = gp.shape[0]
-    cn, lanes = c // NARROW, c // 2
-    rows = cn + 16
-    shape = (WIDE * NARROW, rows, lanes)
-    return pl.pallas_call(
-        pack_first_kernel,
-        grid=(NARROW,),
-        in_specs=[
-            pl.BlockSpec((cn, 3 * c), lambda n: (n, 0)), pl.BlockSpec((cn, c), lambda n: (n, 0)),
-            pl.BlockSpec((1, 16, c), lambda n: (n, 0, 0)),
-        ] + [whole(a.shape) for a in (sb, cb, hid0, hid1)],
-        out_specs=pl.BlockSpec((WIDE, rows, lanes), lambda n: (n, 0, 0)),
-        out_shape=jax.ShapeDtypeStruct(shape, BF16),
-        scratch_shapes=[pltpu.VMEM((16, c), F32)],
-        compiler_params=params(),
-        cost_estimate=cost(0, [(shape, BF16)] * 2),
-        name="pack_first",
-    )(gq, gp, small, sb, cb, hid0, hid1)
+        cost_estimate=cost(8 * rows * c * c, [(a.shape, BF16) for a in flat] + [(shape, BF16)]),
+        name=name,
+    )(*flat, *head)
 
 
 def attention_piece(qkv, proj):
@@ -1162,8 +1194,8 @@
 
 
 def gather_first_kernel(
-    plan, conv_weight, conv_bias, norm_gain, norm_bias, qkv0, qkv1, proj, mlp_in, attn_bias, hidden_bias, out_bias,
-    got, chan, in0, in1, piece, *sems,
+    plan, conv_weight, conv_bias, norm_gain, norm_bias, qkv0, qkv1, proj, attn_bias, hidden_bias, out_bias,
+    got, chan, piece, *sems,
 ):
     cw = conv_bias.shape[1]
     cn = qkv0.shape[1]
@@ -1182,8 +1214,6 @@
     items = plan.items([piece], [got], sems)
     meet(ring_peers())
     gather_step(items, (0,), ())
-    in0[...] = turned(mlp_in[0])
-    in1[...] = turned(mlp_in[1])
     chan[:, pl.ds(0, 3 * cw)] = turned(qkv1[...])
     chan[:, pl.ds(3 * cw, cw)] = turned(proj[1])
     for rings, crosses in GATHER_STEPS[1:]:
@@ -1197,13 +1227,13 @@
     lanes = rows * 4 // 3
     shape = (16 + cn, lanes)
     plan = Beside(1, [None], halves(0, "slot", shape))
-    outs = plan.outs + [((cn, lanes), BF16)] * 3
-    args = [p[k] for k in NAMES if k != "mlp_out"]
+    outs = plan.outs + [((cn, lanes), BF16)]
+    args = [p[k] for k in NAMES if not k.startswith("mlp")]
     vmem = pl.BlockSpec(memory_space=pltpu.VMEM)
     return pl.pallas_call(
         functools.partial(gather_first_kernel, plan),
         in_specs=[vmem] * len(args),
-        out_specs=[plan.out_spec] + [vmem] * 3,
+        out_specs=[plan.out_spec, vmem],
         out_shape=[jax.ShapeDtypeStruct(s, d) for s, d in outs],
         scratch_shapes=[pltpu.VMEM(shape, BF16)] + plan.scratch,
         compiler_params=pltpu.CompilerParams(collective_id=1, has_side_effects=True, vmem_limit_bytes=VMEM_LIMIT),
@@ -1218,7 +1248,8 @@
 ):
     cw = conv_bias.shape[1]
     cn = qkv0.shape[1]
-    conv_weight[0] = att0[pl.ds(0, 9), pl.ds(0, cw)]
+    for k in range(9):
+        conv_weight[k] = att0[pl.ds(k, 1), pl.ds(0, cw)]
     for k, row in enumerate((conv_bias, norm_gain, norm_bias, out_bias)):
         row[...] = att0[pl.ds(9 + k, 1), pl.ds(0, cw)]
     attn_bias[...] = att0[pl.ds(0, 5), pl.ds(LANES, cw)]
@@ -1229,8 +1260,8 @@
     proj[0] = att0[pl.ds(16, cn), pl.ds(3 * cw, cw)].T
     qkv1[...] = att1[:, pl.ds(0, 3 * cw)].T
     proj[1] = att1[:, pl.ds(3 * cw, cw)].T
-    mlp_in[0] = in0[...].T
-    mlp_in[1] = in1[...].T
+    mlp_in[0] = in0[...]
+    mlp_in[1] = in1[...]
     mlp_out[0] = out0[...]
     mlp_out[1] = out1[...]
 
@@ -1241,11 +1272,11 @@
     cw = lanes // 4
     row = (1, cw)
     shapes = [
-        (1, 9, cw), row, row, row, (3 * cw, cn), (3 * cw, cn), (2, cw, cn), (2, lanes, cn), (2, cw, 2 * lanes),
+        (9, 1, cw), row, row, row, (3 * cw, cn), (3 * cw, cn), (2, cw, cn), (2, cn, lanes), (2, cw, 2 * lanes),
         (5, cw), (2, lanes), row,
     ]
     vmem = pl.BlockSpec(memory_space=pltpu.VMEM)
-    return pl.pallas_call(
+    outs = pl.pallas_call(
         finish_kernel,
         in_specs=[vmem] * 6,
         out_specs=[vmem] * len(shapes),
@@ -1254,24 +1285,29 @@
         cost_estimate=cost(0, [(s, F32) for s in shapes]),
         name="finish",
     )(*reduced)
+    outs = list(outs)
+    outs[0] = outs[0].transpose(1, 0, 2)
+    outs[7] = outs[7].transpose(0, 2, 1)
+    return outs
 
 
 class Direct:
     def __init__(self, p):
-        got, self.chan, self.in0, self.in1 = gather_first(p)
-        self.second = p["mlp_out"]
+        got, self.chan = gather_first(p)
+        self.first, self.second = p["mlp_in"].transpose(0, 2, 1), p["mlp_out"]
         watt0, self.lay, self.sh, self.hid = unpack_first(got)
         self.watt, self.w_in, self.w_out = [watt0, None], [None, None], [None, None]
 
     def forward_window(self, *args):
-        parts = pair(0, 1, self.in0.shape, self.second.shape[1:])
-        carry = Beside(3, [self.in0, self.second], parts, {1: 0})
+        parts = pair(0, 1, self.first.shape[1:], self.second.shape[1:])
+        carry = Beside(3, [self.first, self.second], parts, {0: 0, 1: 0})
         *outs, self.w_in[0], self.w_out[0] = forward_window(*args, carry=carry)
         return outs
 
     def forward_mlp(self, *args):
-        parts = halves(0, "slot", self.chan.shape) + halves(1, "in", self.in1.shape)
-        *outs, chan, self.w_in[1] = forward_mlp(*args, carry=Beside(4, [self.chan, self.in1], parts))
+        parts = halves(0, "slot", self.chan.shape) + halves(1, "in", self.first.shape[1:])
+        carry = Beside(4, [self.chan, self.first], parts, {1: 1})
+        *outs, chan, self.w_in[1] = forward_mlp(*args, carry=carry)
         self.watt[1] = unpack_attention(chan)
         return outs
 
@@ -1282,23 +1318,26 @@
 
     def backward_channel(self, grads, *args):
         self.go1 = grads[1]
-        parts = halves(0, "in", self.in1.shape)
+        parts = halves(0, "in", self.first.shape[1:])
         *outs, self.gi1 = backward_channel(*args, carry=Behind(6, grads[:1], parts))
         return outs
 
+    def channel_grads(self, *args):
+        return grad_attention("channel_grads", *args)
+
     def backward_mlp(self, grads, *args):
-        self.att1 = pack_attention(*grads)
+        self.att1 = grads
         parts = halves(0, "out", self.second.shape[1:])
         *outs, self.go1 = backward_mlp(*args, carry=Behind(7, [self.go1], parts))
         return outs
 
     def backward_window(self, grads, *args):
-        parts = pair(0, 1, self.in0.shape, self.second.shape[1:]) + halves(2, "slot", self.chan.shape)
+        parts = pair(0, 1, self.first.shape[1:], self.second.shape[1:]) + halves(2, "slot", self.chan.shape)
         *outs, self.gi0, self.go0, self.att1 = backward_window(*args, carry=Behind(8, list(grads) + [self.att1], parts))
         return outs
 
     def reduce_last(self, grads, smalls, sb, cb, hid0, hid1):
-        packed = pack_first(*grads, jnp.stack(smalls), sb, cb, hid0, hid1)
+        packed = grad_attention("window_grads", *grads, (jnp.stack(smalls), sb, cb, hid0, hid1))
         (att0,) = reduce_now("reduce_last", Behind(2, [packed], halves(0, "slot", packed.shape[1:])))
         return tuple(finish(att0, self.att1, self.gi0, self.gi1, self.go0, self.go1))
 
@@ -1356,6 +1395,9 @@
         self.mlp0 = (self.matrix(grads[0], False), self.matrix(grads[1], True))
         return backward_window(*args)
 
+    def channel_grads(self, *args):
+        return grad_pair("channel_grads", *args)
+
     def matrix(self, grad, rows_wide):
         n, w = self.narrow, self.wide
         a, b = (w, n) if rows_wide else (n, w)
@@ -1366,6 +1408,7 @@
 
     def reduce_last(self, grads, smalls, sb, cb, hid0, hid1):
         c, cw, fw, n, w = self.c, self.cw, self.fw, self.narrow, self.wide
+        grads = grad_pair("window_grads", *grads)
         first = (self.matrix(grads[0], False), self.matrix(grads[1], False)) + self.mlp0
         rest = self.att1 + self.mlp1
         small = jnp.stack(smalls).reshape(n, self.layers * 16, w, cw).transpose(0, 2, 1, 3)
@@ -1397,6 +1440,7 @@
     cotangent = rest[-1]
     lay, sh, hid = weights.lay, weights.sh, weights.hid
     mask = token_mask(heights, widths)
+    inputs, cotangent = cells_first(inputs), cells_first(cotangent)
     n1, z1, r1, q1, o1, p1, x2 = weights.forward_window(inputs, mask, lay, sh, weights.watt[0])
     n2, z2, r2, u1, d1, x4 = weights.forward_mlp(x2, mask, lay, hid, weights.w_in[0], weights.w_out[0])
     n3, z3, r3, q3, o3, a3, x6 = weights.forward_channel(x4, mask, lay, sh, weights.watt[1])
@@ -1405,15 +1449,14 @@
     grads = grad_pair("last_mlp_grads", n4, gh2, gy2, u2)
     g4, ga3, dq3, small2, cb = weights.backward_channel(
         grads, g6, x4, z3, r3, q3, a3, mask, lay, weights.watt[1])
-    grads = grad_pair("channel_grads", n3, dq3, o3, ga3)
+    grads = weights.channel_grads(n3, dq3, o3, ga3)
     g2, gy1, gh1, small1, hid0 = weights.backward_mlp(
         grads, g4, x2, z2, r2, d1, mask, lay, weights.w_in[0], weights.w_out[0])
     grads = grad_pair("mlp_grads", n2, gh1, gy1, u1)
     input_grad, ga1, dq1, small0, sb = weights.backward_window(
         grads, g2, inputs, z1, r1, q1, p1, mask, lay, weights.watt[0])
-    grads = grad_pair("window_grads", n1, dq1, o1, ga1)
-    last = weights.reduce_last(grads, (small0, small1, small2, small3), sb, cb, hid0, hid1)
-    return (out, input_grad) + tuple(last)
+    last = weights.reduce_last((n1, dq1, o1, ga1), (small0, small1, small2, small3), sb, cb, hid0, hid1)
+    return (images_first(out), images_first(input_grad)) + tuple(last)
 
 
 def solution(mesh):

time: 634 us -> 620 us (0.978)
  local copies, waits for them, and re-layouts: 21.5 us -> 2.67 us
    pallas_call x4 -> x2, Pallas kernels: 81.2 us -> 50.2 us  [grad_pair(): pl.pallas_call(functools.partial(grad_pair_kernel, first), grid=(first +...]
    pallas_call x2, Pallas kernels: 12.5 us -> 35 us  [grad_attention(): pl.pallas_call(functools.partial(grad_attention_kernel, start), grid=(4,)...]
    unnamed x17 -> x9, local copies, waits for them, and re-layouts: 20.2 us -> 1.44 us
    pallas_call x7, Pallas kernels: 429 us -> 437 us  [image_call(): pl.pallas_call(body, grid=(images,), in_specs=ins, out_specs=out_specs, o...]
where the time goes in v6:
time: 620 us; the launch traced here: 611 us
  Pallas kernels  605 us (98%)
    pallas_call x7, Pallas kernels, image_call(): pl.pallas_call(body, grid=(images,), in_specs=ins, out_specs=out_specs, o...  437 us
    pallas_call x2, Pallas kernels, grad_pair(): pl.pallas_call(functools.partial(grad_pair_kernel, first), grid=(first +...  50.2 us
    pallas_call x1, Pallas kernels, reduce_now(): pl.pallas_call(functools.partial(reduce_kernel, plan), in_specs=[pl.Block...  36.1 us
    pallas_call x2, Pallas kernels, grad_attention(): pl.pallas_call(functools.partial(grad_attention_kernel, start), grid=(4,)...  35 us
    pallas_call x1, Pallas kernels, gather_first(): pl.pallas_call(functools.partial(gather_first_kernel, plan), in_specs=[vm...  30.8 us

profile of v6, /device:TPU:0, one launch (start us, length us, event | category | flops | bytes accessed | tf_op | source)
XLA Modules:
  0.0 611.1 jit_solution(5629779111721073923)
XLA Ops:
  0.7 0.7 and_convert_fusion
  1.4 1.2 broadcast_in_dim.2.refs_1_.mask.refs_6_.refs_5_
  2.7 30.8 %gather_first.1 = (bf16[32,208,384]{2,1,0:T(8,128)(2,1)}, bf16[192,384]{1,0:T(8,128)(2,1)}) custom-call(bf16[1,9,96]{2,1,0:T(8,128)(2,1)} %conv_weight.1, bf16[1,96]{1,0:T(2,128)(2,1)} %conv_bias.1, bf16[1,96]{1,0:T(2,128)(2,1)} %norm_gain.1, bf16[1,96]{1,0:T(2,128)(2,1)} %norm_bias.1, bf16[288,192]{1,0:T(8,128)(2,1)} %qkv0.1, bf16[288,192]{1,0:T(8,128)(2,1)} %qkv1.1, ...), custom_call_target="tpu_custom_call" | custom-call | bytes 5259264 | tf_op jit(solution)/shard_map/gather_first/pallas_call | solution.py:1233
  33.5 6.4 %unpack_first.1 = (bf16[768,3072]{1,0:T(8,128)(2,1)}, f32[4,16,768]{2,1,0:T(8,128)}, f32[16,768]{1,0:T(8,128)}, f32[2,1,3072]{2,1,0:T(1,128)}) custom-call(bf16[32,208,384]{2,1,0:T(8,128)(2,1)} %get-tuple-element.89.got), custom_call_target="tpu_custom_call" | custom-call | bytes 10100736 | tf_op jit(solution)/shard_map/unpack_first/pallas_call | solution.py:1081
  39.9 71.7 %window_forward.1 = (bf16[8,224,768]{2,1,0:T(8,128)(2,1)}, f32[8,224,768]{2,1,0:T(8,128)}, f32[8,224,128]{2,1,0:T(8,128)}, bf16[8,224,2304]{2,1,0:T(8,128)(2,1)}...) custom-call(bf16[1568,768]{1,0:T(8,128)(2,1)} %bitcast.35, ...), custom_call_target="tpu_custom_call" | custom-call | flops 10569646080 | bytes 48824320 | tf_op jit(solution)/shard_map/window_forward/pallas_call | solution.py:572
  111.6 60.8 %mlp_forward.1 = (bf16[8,224,768]{2,1,0:T(8,128)(2,1)}, f32[8,224,768]{2,1,0:T(8,128)}, f32[8,224,128]{2,1,0:T(8,128)}, bf16[8,224,3072]{2,1,0:T(8,128)(2,1)}, b...) custom-call(f32[8,224,768]{2,1,0:T(8,128)} %get-tuple-element.93.ref, ...), custom_call_target="tpu_custom_call" | custom-call | flops 16911433728 | bytes 62660608 | tf_op jit(solution)/shard_map/mlp_forward/pallas_call | solution.py:572
  172.4 6.1 unpack_attention.1.refs_4_.refs_8_
  178.5 43.1 %channel_forward.1 = (bf16[8,224,768]{2,1,0:T(8,128)(2,1)}, f32[8,224,768]{2,1,0:T(8,128)}, f32[8,224,128]{2,1,0:T(8,128)}, bf16[8,224,2304]{2,1,0:T(8,128)(2,1)...) custom-call(f32[8,224,768]{2,1,0:T(8,128)} %get-tuple-element.98.ref, ...), custom_call_target="tpu_custom_call" | custom-call | flops 9512681472 | bytes 45236224 | tf_op jit(solution)/shard_map/channel_forward/pallas_call | solution.py:572
  221.6 74.0 %last_mlp.1 = (bf16[1568,768]{1,0:T(8,128)(2,1)}, f32[8,224,768]{2,1,0:T(8,128)}, bf16[8,224,768]{2,1,0:T(8,128)(2,1)}, bf16[8,224,3072]{2,1,0:T(8,128)(2,1)}, b...) custom-call(f32[8,224,768]{2,1,0:T(8,128)} %get-tuple-element.100.x_in, ...), custom_call_target="tpu_custom_call" | custom-call | flops 33822867456 | bytes 53989376 | tf_op jit(solution)/shard_map/last_mlp/pallas_call | solution.py:572
  295.5 25.2 %last_mlp_grads.1 = (bf16[768,3072]{1,0:T(8,128)(2,1)}, bf16[768,3072]{1,0:T(8,128)(2,1)}) custom-call(bf16[1792,768]{1,0:T(8,128)(2,1)} %bitcast.61, bf16[1792,3072]{1,0:T(8,128)(2,1)} %bitcast.54, bf16[1792,768]{1,0:T(8,128)(2,1)} %bitcast.62, bf16[1792,3072]{1,0:T(8,128)(2,1)} %bitcast.53), custom_call_target="tpu_custom_call" | custom-call | flops 16911433728 | bytes 36962304 | tf_op jit(solution)/shard_map/last_mlp_grads/pallas_call | solution.py:697
  320.7 46.4 %channel_backward.1 = (f32[8,224,768]{2,1,0:T(8,128)}, bf16[8,224,768]{2,1,0:T(8,128)(2,1)}, bf16[8,224,2304]{2,1,0:T(8,128)(2,1)}, f32[16,768]{1,0:T(8,128)}, f32[1,2304]{1,0:T(1,128)}, /*index=5*/f32[192,384]{1,0:T(8,128)}) custom-call(f32[8,224,768]{2,1,0:T(8,128)} %get-tuple-element.104.refs_0_, f32[8,224,768]{2,1,0:T(8,128)} %get-tuple-element.98.refs_0_.refs_1_, ...), custom_call_target="tpu_custom_call" | custom-call | flops 10569646080 | bytes 56255488 | tf_op jit(solution)/shard_map/channel_backward/pallas_call | solution.py:572
  367.1 44.8 %mlp_backward.1 = (f32[8,224,768]{2,1,0:T(8,128)}, bf16[8,224,768]{2,1,0:T(8,128)(2,1)}, bf16[8,224,3072]{2,1,0:T(8,128)(2,1)}, f32[16,768]{1,0:T(8,128)}, f32[1,3072]{1,0:T(1,128)}, /*index=5*/f32[96,768]{1,0:T(8,128)}) custom-call(f32[8,224,768]{2,1,0:T(8,128)} %get-tuple-element.114.refs_0_, f32[8,224,768]{2,1,0:T(8,128)} %get-tuple-element.93.refs_0_.refs_1_, ...), custom_call_target="tpu_custom_call" | custom-call | flops 16911433728 | bytes 63336448 | tf_op jit(solution)/shard_map/mlp_backward/pallas_call | solution.py:572
  411.9 25.1 %mlp_grads.1 = (bf16[768,3072]{1,0:T(8,128)(2,1)}, bf16[768,3072]{1,0:T(8,128)(2,1)}) custom-call(bf16[1792,768]{1,0:T(8,128)(2,1)} %bitcast.57, bf16[1792,3072]{1,0:T(8,128)(2,1)} %bitcast.52, bf16[1792,768]{1,0:T(8,128)(2,1)} %bitcast.60, bf16[1792,3072]{1,0:T(8,128)(2,1)} %bitcast.51), custom_call_target="tpu_custom_call" | custom-call | flops 16911433728 | bytes 36962304 | tf_op jit(solution)/shard_map/mlp_grads/pallas_call | solution.py:697
  437.0 17.4 %channel_grads.1.refs_11_ = bf16[32,192,384]{2,1,0:T(8,128)(2,1)} custom-call(bf16[1792,768]{1,0:T(8,128)(2,1)} %bitcast.58, bf16[1792,2304]{1,0:T(8,128)(2,1)} %bitcast.42, bf16[1792,768]{1,0:T(8,128)(2,1)} %bitcast.59, bf16[1792,768]{1,0:T(8,128)(2,1)} %bitcast.44), custom_call_target="tpu_custom_call" | custom-call | flops 8455716864 | bytes 21233664 | tf_op jit(solution)/shard_map/channel_grads/pallas_call | solution.py:1173
  454.4 0.0 copy-start.1
  454.4 0.0 copy-start.2
  454.4 0.0 copy-start.3
  454.4 96.7 %window_backward.1 = (bf16[1568,768]{1,0:T(8,128)(2,1)}, bf16[8,224,768]{2,1,0:T(8,128)(2,1)}, bf16[8,224,2304]{2,1,0:T(8,128)(2,1)}, f32[16,768]{1,0:T(8,128)},...) custom-call(f32[8,224,768]{2,1,0:T(8,128)} %get-tuple-element.119.refs_0_, ...), custom_call_target="tpu_custom_call" | custom-call | flops 12683575296 | bytes 61760512 | tf_op jit(solution)/shard_map/window_backward/pallas_call | solution.py:572
  551.2 0.0 copy-done.1
  551.2 0.0 copy-done.2
  551.2 0.0 copy-done.3
  551.2 1.5 pad_maximum_fusion.refs_0_
  552.7 17.7 %window_grads.1.refs_0_ = bf16[32,208,384]{2,1,0:T(8,128)(2,1)} custom-call(bf16[1792,768]{1,0:T(8,128)(2,1)} %bitcast.55, bf16[1792,2304]{1,0:T(8,128)(2,1)} %bitcast.43, bf16[1792,768]{1,0:T(8,128)(2,1)} %bitcast.56, bf16[1792,768]{1,0:T(8,128)(2,1)} %bitcast.45, f32[4,16,768]{2,1,0:T(8,128)} %pad_maximum_fusion.refs_0_, ...), custom_call_target="tpu_custom_call" | custom-call | flops 8455716864 | bytes 21626880 | tf_op jit(solution)/shard_map/window_grads/pallas_call | solution.py:1173
  570.3 0.0 copy-start
  570.3 36.1 %reduce_last.1.att0 = f32[208,384]{1,0:T(8,128)} custom-call(bf16[32,208,384]{2,1,0:T(8,128)(2,1)} %window_grads.1.refs_0_), custom_call_target="tpu_custom_call" | custom-call | bytes 5111808 | tf_op jit(solution)/shard_map/reduce_last/pallas_call | solution.py:1036
  606.4 3.0 finish.1
  609.4 0.0 copy-done
  609.5 1.4 copy.31
  (2 shorter events, 0.0 us)
Async XLA Ops:
  454.4 96.8 %copy-start.1 = (f32[16,768]{1,0:T(8,128)S(1)}, f32[16,768]{1,0:T(8,128)}, u32[]{:S(2)}) copy-start(f32[16,768]{1,0:T(8,128)} %get-tuple-element.142) | copy-start | bytes 147460
  454.4 96.8 %copy-start.2 = (f32[16,768]{1,0:T(8,128)S(1)}, f32[16,768]{1,0:T(8,128)}, u32[]{:S(2)}) copy-start(f32[16,768]{1,0:T(8,128)} %get-tuple-element.141) | copy-start | bytes 147460
  454.4 96.8 %copy-start.3 = (f32[16,768]{1,0:T(8,128)S(1)}, f32[16,768]{1,0:T(8,128)}, u32[]{:S(2)}) copy-start(f32[16,768]{1,0:T(8,128)} %get-tuple-element.140) | copy-start | bytes 147460
  570.3 39.1 %copy-start = (bf16[1568,768]{1,0:T(8,128)(2,1)S(1)}, bf16[1568,768]{1,0:T(8,128)(2,1)}, u32[]{:S(2)}) copy-start(bf16[1568,768]{1,0:T(8,128)(2,1)} %get-tuple-element.134) | copy-start | bytes 7225348

commit v7 on v6

--- a/solution.py
+++ b/solution.py
@@ -355,8 +355,8 @@
     g8[...] = g8[...] * mask[0, :, 0:1]
     gy_out[0] = g8[...].astype(BF16)
     sums[pl.ds(12 * SUB, SUB), :] = sums[pl.ds(12 * SUB, SUB), :] + fold_rows(gy_out[0].astype(F32))
-    for c in range(w_in.shape[1] // FFC):
-        lanes = pl.ds(c * FFC, FFC)
+    for c in range(1):
+        lanes = pl.ds(0, w_in.shape[1])
         h = dot(n_out[0], w_in[:, lanes], DIMS_NN) + hb[0, :, lanes]
         du = dot(gy_out[0], w_out[:, lanes], DIMS_NN)
         u, d = gelu_pair(h)
@@ -924,6 +924,108 @@
                 item.finish()
 
 
+PHASE_STEPS = ((0, 1, 2, 3, 4, 5), (4, 5, 7, 8, 9, 10), (8, 9, 11, 12, 14, 15))
+
+
+def two_phase_kernel(plans, counts, *refs):
+    ins, outs, refs = refs[: counts[0]], refs[counts[0] : counts[0] + counts[1]], refs[counts[0] + counts[1] :]
+    x_in, mask, lay1, lay2, hb, w_in, w_out, sh, chan, first, second = ins
+    n1, z1, r1, u1, d1, x4, n2, z2, r2, q2, o2, a2, x6, watt, got, in1, out1 = outs
+    x1, acc, xs, stage, sem, refs = *refs[:5], refs[5:]
+    step = pl.program_id(0)
+    sets = []
+    for i, (plan, own, dest) in enumerate(zip(plans, (chan, first, second), (got, in1, out1))):
+        sets.append(plan.items([own], [dest], refs[3 * i : 3 * i + 3]))
+    for s in range(2 * CARRY_STEPS):
+        due = [(items, steps.index(s)) for items, steps in zip(sets, PHASE_STEPS) if s in steps]
+
+        @pl.when(step == s)
+        def _(s=s, due=due):
+            if s == 0:
+                meet(ring_peers())
+            for items, k in due:
+                gather_step(items, *GATHER_STEPS[k])
+            if s == CARRY_STEPS:
+                for item in sets[0]:
+                    item.finish()
+                copy = pltpu.make_async_copy(got, stage, sem.at[0])
+                copy.start()
+                copy.wait()
+                cn = chan.shape[0]
+                for n in range(NARROW):
+                    copy_attention(stage.at[pl.ds(n * WIDE, WIDE)], 0, watt.at[pl.ds(n * cn, cn)])
+
+    @pl.when(step < CARRY_STEPS)
+    def _():
+        mlp_forward_kernel(x_in, mask, lay1, hb, w_in, w_out, n1, z1, r1, u1, d1, x4, x1, acc)
+        xs[pl.ds(step, 1)] = x4[...]
+
+    @pl.when(step >= CARRY_STEPS)
+    def _():
+        x = xs.at[pl.ds(step - CARRY_STEPS, 1)]
+        channel_forward_kernel(x, mask, lay2, sh, watt, n2, z2, r2, q2, o2, a2, x6, x1)
+
+    @pl.when(last_step())
+    def _():
+        for items in sets[1:]:
+            for item in items:
+                item.finish()
+
+
+def forward_two(ident, x, mask, lay, hid, w_in, w_out, sh, chan, first, second):
+    images, t, c = x.shape
+    ff = w_in.shape[1]
+    plans = [
+        Beside(ident, [chan], halves(0, "slot", chan.shape)),
+        Beside(ident, [first], halves(0, "in", first.shape[1:]), {0: 1}),
+        Beside(ident, [second], halves(0, "out", second.shape[1:]), {0: 1}),
+    ]
+
+    def before(shape):
+        rest = (0,) * (len(shape) - 1)
+        return pl.BlockSpec((1,) + tuple(shape[1:]), lambda i: (jnp.minimum(i, images - 1),) + rest)
+
+    def after(shape):
+        rest = (0,) * (len(shape) - 1)
+        return pl.BlockSpec((1,) + tuple(shape[1:]), lambda i: (jnp.maximum(i - images, 0),) + rest)
+
+    each = pl.BlockSpec((1, t, LANES), lambda i: (lax.rem(i, images), 0, 0))
+    anywhere = pl.BlockSpec(memory_space=pl.ANY)
+    args = [x, mask, lay, lay, hid, w_in, w_out, sh, chan, first, second]
+    in_specs = [
+        before(x.shape), each, one_layer(lay.shape, 1), one_layer(lay.shape, 2), one_layer(hid.shape, 0),
+        whole(w_in.shape), whole(w_out.shape), whole(sh.shape), anywhere, anywhere, anywhere,
+    ]
+    low = [
+        ((images, t, c), BF16), ((images, t, c), F32), ((images, t, LANES), F32), ((images, t, ff), BF16),
+        ((images, t, ff), BF16), ((images, t, c), F32),
+    ]
+    high = [
+        ((images, t, c), BF16), ((images, t, c), F32), ((images, t, LANES), F32), ((images, t, 3 * c), BF16),
+        ((images, t, c), BF16), ((images, c // GROUP, GROUP, GROUP), BF16), ((images, t, c), F32),
+    ]
+    outs = low + high + [((c, 4 * c), BF16)] + [o for plan in plans for o in plan.outs]
+    out_specs = [before(s) for s, _ in low] + [after(s) for s, _ in high] + [whole((c, 4 * c))] + [anywhere] * 3
+    scratch = [
+        pltpu.VMEM((t, c), F32), pltpu.VMEM((t, c), F32), pltpu.VMEM((images, t, c), F32),
+        pltpu.VMEM(plans[0].outs[0][0], BF16), pltpu.SemaphoreType.DMA((1,)),
+    ]
+    scratch += [item for plan in plans for item in plan.scratch]
+    return pl.pallas_call(
+        functools.partial(two_phase_kernel, plans, (len(args), len(outs))),
+        grid=(2 * images,),
+        in_specs=in_specs,
+        out_specs=out_specs,
+        out_shape=[jax.ShapeDtypeStruct(s, d) for s, d in outs],
+        scratch_shapes=scratch,
+        compiler_params=pltpu.CompilerParams(
+            dimension_semantics=("arbitrary",), vmem_limit_bytes=VMEM_LIMIT, collective_id=ident, has_side_effects=True,
+        ),
+        cost_estimate=cost(4 * images * t * c * ff + 9 * images * t * c * c, [(a.shape, a.dtype) for a in args] + outs),
+        name="mlp_channel_forward",
+    )(*args)
+
+
 class Reduce:
     def __init__(self, index, part, src, out, bufs, sems):
         self.index, self.part, self.src, self.out = index, part, src, out
@@ -1056,7 +1158,7 @@
         dst[:, pl.ds(3 * c + cw * w, cw)] = src[w, pl.ds(start, cn), pl.ds(3 * cw, cw)]
 
 
-def unpack_first_kernel(got, watt, lay, sh, hid):
+def unpack_first_kernel(got, heights, widths, watt, lay, sh, hid, mask):
     copy_attention(got, 16, watt)
     cw = got.shape[2] // 4
     for w in range(WIDE):
@@ -1072,45 +1174,43 @@
                     row = 5 + 4 * j + q
                     hid[j, :, pl.ds(4 * cw * w + cw * q, cw)] = part[row : row + 1]
 
-
-def unpack_first(got):
+    @pl.when(pl.program_id(0) == 1)
+    def _():
+        t = lax.broadcasted_iota(jnp.int32, mask.shape[1:], 0)
+        window = whole_part(t >= WTOK) + whole_part(t >= 2 * WTOK) + whole_part(t >= 3 * WTOK)
+        rest = t - window * WTOK
+        low = lax.shift_right_logical(rest, 3)
+        col8 = rest - low * SUB
+        lower = whole_part(window >= 2)
+        row = lower * WIN + low
+        col = (window - 2 * lower) * WIN + col8
+        for i in range(mask.shape[0]):
+            valid = (row < heights[i]) & (col < widths[i]) & (col8 < WIN)
+            mask[i] = jnp.where(valid, 1.0, 0.0)
+
+
+def unpack_first(got, heights, widths):
     rows, lanes = got.shape[1:]
     c = 2 * lanes
     cn = c // NARROW
-    outs = [((c, 4 * c), BF16), ((NARROW, 16, c), F32), ((16, c), F32), ((2, 1, 4 * c), F32)]
+    images = heights.shape[0]
+    outs = [
+        ((c, 4 * c), BF16), ((NARROW, 16, c), F32), ((16, c), F32), ((2, 1, 4 * c), F32), ((images, 4 * WTOK, LANES), F32),
+    ]
     return pl.pallas_call(
         unpack_first_kernel,
         grid=(NARROW,),
-        in_specs=[pl.BlockSpec((WIDE, rows, lanes), lambda n: (n, 0, 0))],
+        in_specs=[pl.BlockSpec((WIDE, rows, lanes), lambda n: (n, 0, 0))] + [pl.BlockSpec(memory_space=pltpu.SMEM)] * 2,
         out_specs=[
             pl.BlockSpec((cn, 4 * c), lambda n: (n, 0)), pl.BlockSpec((1, 16, c), lambda n: (n, 0, 0)),
             pl.BlockSpec((16, c), lambda n: (0, 0)), pl.BlockSpec((2, 1, 4 * c), lambda n: (0, 0, 0)),
+            pl.BlockSpec((images, 4 * WTOK, LANES), lambda n: (0, 0, 0)),
         ],
         out_shape=[jax.ShapeDtypeStruct(s, d) for s, d in outs],
         compiler_params=params(),
         cost_estimate=cost(0, [(got.shape, BF16)] + outs),
         name="unpack_first",
-    )(got)
-
-
-def unpack_attention_kernel(got, watt):
-    copy_attention(got, 0, watt)
-
-
-def unpack_attention(got):
-    rows, lanes = got.shape[1:]
-    c = 2 * lanes
-    shape = (c, 4 * c)
-    return pl.pallas_call(
-        unpack_attention_kernel,
-        grid=(NARROW,),
-        in_specs=[pl.BlockSpec((WIDE, rows, lanes), lambda n: (n, 0, 0))],
-        out_specs=pl.BlockSpec((c // NARROW, 4 * c), lambda n: (n, 0)),
-        out_shape=jax.ShapeDtypeStruct(shape, BF16),
-        compiler_params=params(),
-        cost_estimate=cost(0, [(shape, BF16)] * 2),
-        name="unpack_attention",
-    )(got)
+    )(got, heights, widths)
 
 
 def grad_attention_kernel(start, left0, right0, left1, right1, *refs):
@@ -1144,8 +1244,9 @@
                     pack_small(*head, out, refs[-1])
 
 
-def pack_small(small, sb, cb, hid0, hid1, out, shared):
-    c = small.shape[2]
+def pack_small(small0, small1, small2, small3, sb, cb, hid0, hid1, out, shared):
+    smalls = (small0, small1, small2, small3)
+    c = small0.shape[1]
     cw = c // WIDE
     shared[...] = jnp.zeros_like(shared)
     shared[pl.ds(0, 1), :] = sb[:, pl.ds(0, c)]
@@ -1159,7 +1260,7 @@
     out[:, pl.ds(0, 16), :] = jnp.zeros((WIDE * NARROW, 16, out.shape[2]), BF16)
     for w in range(WIDE):
         for n in range(NARROW):
-            out[n * WIDE + w, pl.ds(0, 16), pl.ds(0, cw)] = small[n, :, pl.ds(cw * w, cw)].astype(BF16)
+            out[n * WIDE + w, pl.ds(0, 16), pl.ds(0, cw)] = smalls[n][:, pl.ds(cw * w, cw)].astype(BF16)
             out[n * WIDE + w, pl.ds(0, 16), pl.ds(LANES, cw)] = shared[:, pl.ds(cw * w, cw)].astype(BF16)
 
 
@@ -1292,10 +1393,10 @@
 
 
 class Direct:
-    def __init__(self, p):
+    def __init__(self, p, heights, widths):
         got, self.chan = gather_first(p)
         self.first, self.second = p["mlp_in"].transpose(0, 2, 1), p["mlp_out"]
-        watt0, self.lay, self.sh, self.hid = unpack_first(got)
+        watt0, self.lay, self.sh, self.hid, self.mask = unpack_first(got, heights, widths)
         self.watt, self.w_in, self.w_out = [watt0, None], [None, None], [None, None]
 
     def forward_window(self, *args):
@@ -1304,16 +1405,9 @@
         *outs, self.w_in[0], self.w_out[0] = forward_window(*args, carry=carry)
         return outs
 
-    def forward_mlp(self, *args):
-        parts = halves(0, "slot", self.chan.shape) + halves(1, "in", self.first.shape[1:])
-        carry = Beside(4, [self.chan, self.first], parts, {1: 1})
-        *outs, chan, self.w_in[1] = forward_mlp(*args, carry=carry)
-        self.watt[1] = unpack_attention(chan)
-        return outs
-
-    def forward_channel(self, *args):
-        parts = halves(0, "out", self.second.shape[1:])
-        *outs, self.w_out[1] = forward_channel(*args, carry=Beside(5, [self.second], parts, {0: 1}))
+    def forward_two(self, *args):
+        *outs, self.watt[1], _, self.w_in[1], self.w_out[1] = forward_two(
+            4, *args, self.sh, self.chan, self.first, self.second)
         return outs
 
     def backward_channel(self, grads, *args):
@@ -1337,13 +1431,14 @@
         return outs
 
     def reduce_last(self, grads, smalls, sb, cb, hid0, hid1):
-        packed = grad_attention("window_grads", *grads, (jnp.stack(smalls), sb, cb, hid0, hid1))
+        packed = grad_attention("window_grads", *grads, (*smalls, sb, cb, hid0, hid1))
         (att0,) = reduce_now("reduce_last", Behind(2, [packed], halves(0, "slot", packed.shape[1:])))
         return tuple(finish(att0, self.att1, self.gi0, self.gi1, self.go0, self.go1))
 
 
 class Plain:
-    def __init__(self, p):
+    def __init__(self, p, heights, widths):
+        self.mask = token_mask(heights, widths)
         self.layers, self.cw = p["conv_bias"].shape
         wide = p["attn_bias"].shape
         self.narrow = 4 // self.layers
@@ -1377,11 +1472,9 @@
     def forward_window(self, *args):
         return forward_window(*args)
 
-    def forward_mlp(self, *args):
-        return forward_mlp(*args)
-
-    def forward_channel(self, *args):
-        return forward_channel(*args)
+    def forward_two(self, x, mask, lay, hid, w_in, w_out):
+        low = forward_mlp(x, mask, lay, hid, w_in, w_out)
+        return list(low) + list(forward_channel(low[-1], mask, lay, self.sh, self.watt[1]))
 
     def backward_channel(self, grads, *args):
         self.mlp1 = (self.matrix(grads[0], False), self.matrix(grads[1], True))
@@ -1436,14 +1529,14 @@
 def local(plan, inputs, heights, widths, *rest):
     if inputs.shape[0] != CARRY_STEPS:
         plan = Plain
-    weights = plan(dict(zip(NAMES, rest[:-1])))
+    weights = plan(dict(zip(NAMES, rest[:-1])), heights, widths)
     cotangent = rest[-1]
     lay, sh, hid = weights.lay, weights.sh, weights.hid
-    mask = token_mask(heights, widths)
+    mask = weights.mask
     inputs, cotangent = cells_first(inputs), cells_first(cotangent)
     n1, z1, r1, q1, o1, p1, x2 = weights.forward_window(inputs, mask, lay, sh, weights.watt[0])
-    n2, z2, r2, u1, d1, x4 = weights.forward_mlp(x2, mask, lay, hid, weights.w_in[0], weights.w_out[0])
-    n3, z3, r3, q3, o3, a3, x6 = weights.forward_channel(x4, mask, lay, sh, weights.watt[1])
+    n2, z2, r2, u1, d1, x4, n3, z3, r3, q3, o3, a3, x6 = weights.forward_two(
+        x2, mask, lay, hid, weights.w_in[0], weights.w_out[0])
     out, g6, n4, u2, gy2, gh2, small3, hid1 = last_mlp(
         x6, cotangent, mask, lay, hid, weights.w_in[1], weights.w_out[1])
     grads = grad_pair("last_mlp_grads", n4, gh2, gy2, u2)

time: 620 us -> 589 us (0.950)
  Pallas kernels: 605 us -> 581 us
    pallas_call x7 -> x5, Pallas kernels: 437 us -> 330 us  [image_call(): pl.pallas_call(body, grid=(images,), in_specs=ins, out_specs=out_specs, o...]
    pallas_call x1, Pallas kernels: 6.08 us -> 89.8 us  [forward_two(): pl.pallas_call(functools.partial(two_phase_kernel, plans, (len(args), len...]
where the time goes in v7:
time: 589 us; the launch traced here: 584 us
  Pallas kernels  581 us (99%)
    pallas_call x5, Pallas kernels, image_call(): pl.pallas_call(body, grid=(images,), in_specs=ins, out_specs=out_specs, o...  330 us
    pallas_call x1, Pallas kernels, forward_two(): pl.pallas_call(functools.partial(two_phase_kernel, plans, (len(args), len...  89.8 us
    pallas_call x2, Pallas kernels, grad_pair(): pl.pallas_call(functools.partial(grad_pair_kernel, first), grid=(first +...  50 us
    pallas_call x1, Pallas kernels, reduce_now(): pl.pallas_call(functools.partial(reduce_kernel, plan), in_specs=[pl.Block...  36 us
    pallas_call x2, Pallas kernels, grad_attention(): pl.pallas_call(functools.partial(grad_attention_kernel, start), grid=(4,)...  34.9 us
    pallas_call x1, Pallas kernels, gather_first(): pl.pallas_call(functools.partial(gather_first_kernel, plan), in_specs=[vm...  30.9 us

profile of v7, /device:TPU:0, one launch (start us, length us, event | category | flops | bytes accessed | tf_op | source)
XLA Modules:
  0.0 583.9 jit_solution(10856969414914660204)
XLA Ops:
  0.6 30.9 %gather_first.1 = (bf16[32,208,384]{2,1,0:T(8,128)(2,1)}, bf16[192,384]{1,0:T(8,128)(2,1)}) custom-call(bf16[1,9,96]{2,1,0:T(8,128)(2,1)} %conv_weight.1, bf16[1,96]{1,0:T(2,128)(2,1)} %conv_bias.1, bf16[1,96]{1,0:T(2,128)(2,1)} %norm_gain.1, bf16[1,96]{1,0:T(2,128)(2,1)} %norm_bias.1, bf16[288,192]{1,0:T(8,128)(2,1)} %qkv0.1, bf16[288,192]{1,0:T(8,128)(2,1)} %qkv1.1, ...), custom_call_target="tpu_custom_call" | custom-call | bytes 5259264 | tf_op jit(solution)/shard_map/gather_first/pallas_call | solution.py:1334
  31.5 6.6 %unpack_first.1 = (bf16[768,3072]{1,0:T(8,128)(2,1)}, f32[4,16,768]{2,1,0:T(8,128)}, f32[16,768]{1,0:T(8,128)}, f32[2,1,3072]{2,1,0:T(1,128)}, f32[8,224,128]{2,1,0:T(8,128)}) custom-call(bf16[32,208,384]{2,1,0:T(8,128)(2,1)} %get-tuple-element.90.got, s32[8]{0:T(128)} %heights.1, s32[8]{0:T(128)} %widths.1), custom_call_target="tpu_custom_call" | custom-call | bytes 11018240 | tf_op jit(solution)/shard_map/unpack_first/pallas_call | solution.py:1200
  38.1 71.7 %window_forward.1 = (bf16[8,224,768]{2,1,0:T(8,128)(2,1)}, f32[8,224,768]{2,1,0:T(8,128)}, f32[8,224,128]{2,1,0:T(8,128)}, bf16[8,224,2304]{2,1,0:T(8,128)(2,1)}...) custom-call(bf16[1568,768]{1,0:T(8,128)(2,1)} %bitcast.31, ...), custom_call_target="tpu_custom_call" | custom-call | flops 10569646080 | bytes 48824320 | tf_op jit(solution)/shard_map/window_forward/pallas_call | solution.py:572
  109.8 89.8 %mlp_channel_forward.1 = (bf16[8,224,768]{2,1,0:T(8,128)(2,1)}, f32[8,224,768]{2,1,0:T(8,128)}, f32[8,224,128]{2,1,0:T(8,128)}, bf16[8,224,3072]{2,1,0:T(8,128)(...) custom-call(f32[8,224,768]{2,1,0:T(8,128)} %get-tuple-element.95.ref, ...), custom_call_target="tpu_custom_call" | custom-call | flops 26424115200 | bytes 101474304 | tf_op jit(solution)/shard_map/mlp_channel_forward/pallas_call | solution.py:1014
  199.7 71.8 %last_mlp.1 = (bf16[1568,768]{1,0:T(8,128)(2,1)}, f32[8,224,768]{2,1,0:T(8,128)}, bf16[8,224,768]{2,1,0:T(8,128)(2,1)}, bf16[8,224,3072]{2,1,0:T(8,128)(2,1)}, b...) custom-call(f32[8,224,768]{2,1,0:T(8,128)} %get-tuple-element.100.x_in, ...), custom_call_target="tpu_custom_call" | custom-call | flops 33822867456 | bytes 53989376 | tf_op jit(solution)/shard_map/last_mlp/pallas_call | solution.py:572
  271.5 24.9 %last_mlp_grads.1 = (bf16[768,3072]{1,0:T(8,128)(2,1)}, bf16[768,3072]{1,0:T(8,128)(2,1)}) custom-call(bf16[1792,768]{1,0:T(8,128)(2,1)} %bitcast.53, bf16[1792,3072]{1,0:T(8,128)(2,1)} %bitcast.46, bf16[1792,768]{1,0:T(8,128)(2,1)} %bitcast.54, bf16[1792,3072]{1,0:T(8,128)(2,1)} %bitcast.45), custom_call_target="tpu_custom_call" | custom-call | flops 16911433728 | bytes 36962304 | tf_op jit(solution)/shard_map/last_mlp_grads/pallas_call | solution.py:697
  296.4 45.6 %channel_backward.1 = (f32[8,224,768]{2,1,0:T(8,128)}, bf16[8,224,768]{2,1,0:T(8,128)(2,1)}, bf16[8,224,2304]{2,1,0:T(8,128)(2,1)}, f32[16,768]{1,0:T(8,128)}, f32[1,2304]{1,0:T(1,128)}, /*index=5*/f32[192,384]{1,0:T(8,128)}) custom-call(f32[8,224,768]{2,1,0:T(8,128)} %get-tuple-element.104.refs_0_, f32[8,224,768]{2,1,0:T(8,128)} %get-tuple-element.105.refs_1_, ...), custom_call_target="tpu_custom_call" | custom-call | flops 10569646080 | bytes 56255488 | tf_op jit(solution)/shard_map/channel_backward/pallas_call | solution.py:572
  342.0 44.0 %mlp_backward.1 = (f32[8,224,768]{2,1,0:T(8,128)}, bf16[8,224,768]{2,1,0:T(8,128)(2,1)}, bf16[8,224,3072]{2,1,0:T(8,128)(2,1)}, f32[16,768]{1,0:T(8,128)}, f32[1,3072]{1,0:T(1,128)}, /*index=5*/f32[96,768]{1,0:T(8,128)}) custom-call(f32[8,224,768]{2,1,0:T(8,128)} %get-tuple-element.116.refs_0_, f32[8,224,768]{2,1,0:T(8,128)} %get-tuple-element.95.refs_0_.refs_1_, ...), custom_call_target="tpu_custom_call" | custom-call | flops 16911433728 | bytes 63336448 | tf_op jit(solution)/shard_map/mlp_backward/pallas_call | solution.py:572
  386.0 25.1 %mlp_grads.1 = (bf16[768,3072]{1,0:T(8,128)(2,1)}, bf16[768,3072]{1,0:T(8,128)(2,1)}) custom-call(bf16[1792,768]{1,0:T(8,128)(2,1)} %bitcast.51, bf16[1792,3072]{1,0:T(8,128)(2,1)} %bitcast.44, bf16[1792,768]{1,0:T(8,128)(2,1)} %bitcast.52, bf16[1792,3072]{1,0:T(8,128)(2,1)} %bitcast.43), custom_call_target="tpu_custom_call" | custom-call | flops 16911433728 | bytes 36962304 | tf_op jit(solution)/shard_map/mlp_grads/pallas_call | solution.py:697
  411.1 17.1 %channel_grads.1.refs_11_ = bf16[32,192,384]{2,1,0:T(8,128)(2,1)} custom-call(bf16[1792,768]{1,0:T(8,128)(2,1)} %bitcast.49, bf16[1792,2304]{1,0:T(8,128)(2,1)} %bitcast.34, bf16[1792,768]{1,0:T(8,128)(2,1)} %bitcast.50, bf16[1792,768]{1,0:T(8,128)(2,1)} %bitcast.36), custom_call_target="tpu_custom_call" | custom-call | flops 8455716864 | bytes 21233664 | tf_op jit(solution)/shard_map/channel_grads/pallas_call | solution.py:1274
  428.3 97.0 %window_backward.1 = (bf16[1568,768]{1,0:T(8,128)(2,1)}, bf16[8,224,768]{2,1,0:T(8,128)(2,1)}, bf16[8,224,2304]{2,1,0:T(8,128)(2,1)}, f32[16,768]{1,0:T(8,128)},...) custom-call(f32[8,224,768]{2,1,0:T(8,128)} %get-tuple-element.121.refs_0_, ...), custom_call_target="tpu_custom_call" | custom-call | flops 12683575296 | bytes 61760512 | tf_op jit(solution)/shard_map/window_backward/pallas_call | solution.py:572
  525.3 17.8 %window_grads.1.refs_0_ = bf16[32,208,384]{2,1,0:T(8,128)(2,1)} custom-call(bf16[1792,768]{1,0:T(8,128)(2,1)} %bitcast.47, bf16[1792,2304]{1,0:T(8,128)(2,1)} %bitcast.35, bf16[1792,768]{1,0:T(8,128)(2,1)} %bitcast.48, bf16[1792,768]{1,0:T(8,128)(2,1)} %bitcast.37, f32[16,768]{1,0:T(8,128)} %get-tuple-element.141.refs_0_, ...), custom_call_target="tpu_custom_call" | custom-call | flops 8455716864 | bytes 21626880 | tf_op jit(solution)/shard_map/window_grads/pallas_call | solution.py:1274
  543.1 0.0 copy-start
  543.1 36.0 %reduce_last.1.att0 = f32[208,384]{1,0:T(8,128)} custom-call(bf16[32,208,384]{2,1,0:T(8,128)(2,1)} %window_grads.1.refs_0_), custom_call_target="tpu_custom_call" | custom-call | bytes 5111808 | tf_op jit(solution)/shard_map/reduce_last/pallas_call | solution.py:1138
  579.0 3.0 finish.1
  582.0 0.0 copy-done
  582.0 1.4 copy.31
Async XLA Ops:
  543.1 39.0 %copy-start = (bf16[1568,768]{1,0:T(8,128)(2,1)S(1)}, bf16[1568,768]{1,0:T(8,128)(2,1)}, u32[]{:S(2)}) copy-start(bf16[1568,768]{1,0:T(8,128)(2,1)} %get-tuple-element.136) | copy-start | bytes 7225348

commit v8 on v7

--- a/solution.py
+++ b/solution.py
@@ -231,12 +231,12 @@
     return h * cdf, cdf + h * pdf
 
 
-def first_step():
-    return pl.program_id(0) == 0
-
-
-def last_step():
-    return pl.program_id(0) == pl.num_programs(0) - 1
+def first_step(steps=None):
+    return pl.program_id(0) == (steps[0] if steps else 0)
+
+
+def last_step(steps=None):
+    return pl.program_id(0) == (steps[1] if steps else pl.num_programs(0)) - 1
 
 
 def window_forward_kernel(
@@ -385,8 +385,9 @@
     g_in, x_in, z_in, r_in, d_in, mask, lay, w_in, w_out,
     g_out, gy_out, gh_out, small_out, hidden_out,
     dn, g1, sums, hsums,
+    steps=None,
 ):
-    @pl.when(first_step())
+    @pl.when(first_step(steps))
     def _():
         sums[...] = jnp.zeros_like(sums)
         hsums[...] = jnp.zeros_like(hsums)
@@ -404,7 +405,7 @@
     norm_backward(dn, z_in.at[0], r_in.at[0], lay, g_in.at[0], sums, 10 * SUB, g1)
     conv_backward(x_in.at[0], g1, mask, lay, sums, g_out.at[0])
 
-    @pl.when(last_step())
+    @pl.when(last_step(steps))
     def _():
         finish_sums(sums, small_out)
         finish_sums(hsums, hidden_out)
@@ -414,10 +415,11 @@
     g_in, x_in, z_in, r_in, q_in, a_in, mask, lay, watt,
     g_out, ga_out, dq_out, small_out, bias_out,
     dn, g1, sums, bsums,
+    steps=None,
 ):
     features = dn.shape[1]
 
-    @pl.when(first_step())
+    @pl.when(first_step(steps))
     def _():
         sums[...] = jnp.zeros_like(sums)
         bsums[...] = jnp.zeros_like(bsums)
@@ -441,7 +443,7 @@
     norm_backward(dn, z_in.at[0], r_in.at[0], lay, g_in.at[0], sums, 10 * SUB, g1)
     conv_backward(x_in.at[0], g1, mask, lay, sums, g_out.at[0])
 
-    @pl.when(last_step())
+    @pl.when(last_step(steps))
     def _():
         finish_sums(sums, small_out)
         finish_sums(bsums, bias_out)
@@ -1119,6 +1121,112 @@
                 item.finish()
 
 
+BACK_STEPS = ((0, 1, 2, 3, 4, 5, 6, 7), (4, 6, 7, 8, 10, 11, 13, 15))
+
+
+def two_phase_back_kernel(plans, counts, *refs):
+    ins, outs, refs = refs[: counts[0]], refs[counts[0] : counts[0] + counts[1]], refs[counts[0] + counts[1] :]
+    g_in, xa, za, ra, q, a, mask, lay2, watt, xb, zb, rb, d, lay1, w_in, w_out, src0, src1 = ins
+    ga, dq, small2, cb, g_out, gy, gh, small1, hid, red0, red1 = outs
+    dn, g1, gs, sums_a, bsums, sums_b, hsums, refs = *refs[:7], refs[7:]
+    step = pl.program_id(0)
+    first = len(plans[0].scratch)
+    sets = [plans[0].items([src0], [red0], refs[:first]), plans[1].items([src1], [red1], refs[first:])]
+    for s in range(2 * CARRY_STEPS):
+        due = [(items, steps.index(s)) for items, steps in zip(sets, BACK_STEPS) if s in steps]
+        if not due:
+            continue
+
+        @pl.when(step == s)
+        def _(s=s, due=due):
+            if s == 0:
+                meet(chip_peers())
+            for items, k in due:
+                if k == 0:
+                    for rel in reversed(STAGES):
+                        for item in items:
+                            item.begin(rel)
+                for rel in REDUCE_STEPS[k]:
+                    for item in items:
+                        item.stage(rel)
+
+    @pl.when(step < CARRY_STEPS)
+    def _():
+        middle = gs.at[pl.ds(step, 1)]
+        channel_backward_kernel(
+            g_in, xa, za, ra, q, a, mask, lay2, watt, middle, ga, dq, small2, cb, dn, g1, sums_a, bsums,
+            steps=(0, CARRY_STEPS),
+        )
+
+    @pl.when(step >= CARRY_STEPS)
+    def _():
+        middle = gs.at[pl.ds(step - CARRY_STEPS, 1)]
+        mlp_backward_kernel(
+            middle, xb, zb, rb, d, mask, lay1, w_in, w_out, g_out, gy, gh, small1, hid, dn, g1, sums_b, hsums,
+            steps=(CARRY_STEPS, 2 * CARRY_STEPS),
+        )
+
+    @pl.when(last_step())
+    def _():
+        for items in sets:
+            for item in items:
+                item.finish()
+
+
+def backward_two(ident, grads, g, xa, za, ra, q, a, mask, lay, watt, xb, zb, rb, d, w_in, w_out):
+    images, t, c = g.shape
+    ff = w_in.shape[1]
+    plans = [
+        Behind(ident, grads[:1], halves(0, "in", (grads[0].shape[0] // NARROW, grads[0].shape[1] // WIDE))),
+        Behind(ident, grads[1:], halves(0, "out", (grads[1].shape[0] // WIDE, grads[1].shape[1] // NARROW))),
+    ]
+
+    def before(shape):
+        rest = (0,) * (len(shape) - 1)
+        return pl.BlockSpec((1,) + tuple(shape[1:]), lambda i: (jnp.minimum(i, images - 1),) + rest)
+
+    def after(shape):
+        rest = (0,) * (len(shape) - 1)
+        return pl.BlockSpec((1,) + tuple(shape[1:]), lambda i: (jnp.maximum(i - images, 0),) + rest)
+
+    def still(shape):
+        return pl.BlockSpec(tuple(shape), lambda i: (0, 0))
+
+    each = pl.BlockSpec((1, t, LANES), lambda i: (lax.rem(i, images), 0, 0))
+    anywhere = pl.BlockSpec(memory_space=pl.ANY)
+    args = [g, xa, za, ra, q, a, mask, lay, watt, xb, zb, rb, d, lay, w_in, w_out] + list(grads)
+    in_specs = [before(v.shape) for v in (g, xa, za, ra, q, a)]
+    in_specs += [each, one_layer(lay.shape, 2), whole(watt.shape)]
+    in_specs += [after(v.shape) for v in (xb, zb, rb, d)]
+    in_specs += [one_layer(lay.shape, 1), whole(w_in.shape), whole(w_out.shape), anywhere, anywhere]
+    outs = [((images, t, c), BF16), ((images, t, 3 * c), BF16), ((16, c), F32), ((1, 3 * c), F32)]
+    out_specs = [before(outs[0][0]), before(outs[1][0]), still(outs[2][0]), still(outs[3][0])]
+    more = [((images, t, c), F32), ((images, t, c), BF16), ((images, t, ff), BF16), ((16, c), F32), ((1, ff), F32)]
+    out_specs += [after(v) for v, _ in more[:3]] + [still(v) for v, _ in more[3:]]
+    reds = [o for plan in plans for o in plan.outs]
+    out_specs += [still(v) for v, _ in reds]
+    outs = outs + more + reds
+    scratch = [
+        pltpu.VMEM(v, F32) for v in (
+            (t, c), (t, c), (images, t, c), (16 * SUB, c), (SUB, 3 * c), (16 * SUB, c), (SUB, ff),
+        )
+    ]
+    scratch += [item for plan in plans for item in plan.scratch]
+    return pl.pallas_call(
+        functools.partial(two_phase_back_kernel, plans, (len(args), len(outs))),
+        grid=(2 * images,),
+        in_specs=in_specs,
+        out_specs=out_specs,
+        out_shape=[jax.ShapeDtypeStruct(s, d) for s, d in outs],
+        scratch_shapes=scratch,
+        compiler_params=pltpu.CompilerParams(
+            dimension_semantics=("arbitrary",), vmem_limit_bytes=VMEM_LIMIT, collective_id=ident, has_side_effects=True,
+        ),
+        cost_estimate=cost(4 * images * t * c * ff + 10 * images * t * c * c, [(v.shape, v.dtype) for v in args] + outs),
+        name="channel_mlp_backward",
+    )(*args)
+
+
 def reduce_kernel(plan, *refs):
     ins, refs = refs[: len(plan.args)], refs[len(plan.args) :]
     outs, scratch = refs[: len(plan.outs)], refs[len(plan.outs) :]
@@ -1410,20 +1518,12 @@
             4, *args, self.sh, self.chan, self.first, self.second)
         return outs
 
-    def backward_channel(self, grads, *args):
-        self.go1 = grads[1]
-        parts = halves(0, "in", self.first.shape[1:])
-        *outs, self.gi1 = backward_channel(*args, carry=Behind(6, grads[:1], parts))
+    def backward_two(self, grads, *args):
+        *outs, self.gi1, self.go1 = backward_two(6, grads, *args)
         return outs
 
     def channel_grads(self, *args):
-        return grad_attention("channel_grads", *args)
-
-    def backward_mlp(self, grads, *args):
-        self.att1 = grads
-        parts = halves(0, "out", self.second.shape[1:])
-        *outs, self.go1 = backward_mlp(*args, carry=Behind(7, [self.go1], parts))
-        return outs
+        self.att1 = grad_attention("channel_grads", *args)
 
     def backward_window(self, grads, *args):
         parts = pair(0, 1, self.first.shape[1:], self.second.shape[1:]) + halves(2, "slot", self.chan.shape)
@@ -1476,20 +1576,18 @@
         low = forward_mlp(x, mask, lay, hid, w_in, w_out)
         return list(low) + list(forward_channel(low[-1], mask, lay, self.sh, self.watt[1]))
 
-    def backward_channel(self, grads, *args):
+    def backward_two(self, grads, g, xa, za, ra, q, a, mask, lay, watt, xb, zb, rb, d, w_in, w_out):
         self.mlp1 = (self.matrix(grads[0], False), self.matrix(grads[1], True))
-        return backward_channel(*args)
-
-    def backward_mlp(self, grads, *args):
-        self.att1 = (self.matrix(grads[0], False), self.matrix(grads[1], False))
-        return backward_mlp(*args)
+        high = backward_channel(g, xa, za, ra, q, a, mask, lay, watt)
+        return list(high[1:]) + list(backward_mlp(high[0], xb, zb, rb, d, mask, lay, w_in, w_out))
 
     def backward_window(self, grads, *args):
         self.mlp0 = (self.matrix(grads[0], False), self.matrix(grads[1], True))
         return backward_window(*args)
 
     def channel_grads(self, *args):
-        return grad_pair("channel_grads", *args)
+        grads = grad_pair("channel_grads", *args)
+        self.att1 = (self.matrix(grads[0], False), self.matrix(grads[1], False))
 
     def matrix(self, grad, rows_wide):
         n, w = self.narrow, self.wide
@@ -1540,11 +1638,9 @@
     out, g6, n4, u2, gy2, gh2, small3, hid1 = last_mlp(
         x6, cotangent, mask, lay, hid, weights.w_in[1], weights.w_out[1])
     grads = grad_pair("last_mlp_grads", n4, gh2, gy2, u2)
-    g4, ga3, dq3, small2, cb = weights.backward_channel(
-        grads, g6, x4, z3, r3, q3, a3, mask, lay, weights.watt[1])
-    grads = weights.channel_grads(n3, dq3, o3, ga3)
-    g2, gy1, gh1, small1, hid0 = weights.backward_mlp(
-        grads, g4, x2, z2, r2, d1, mask, lay, weights.w_in[0], weights.w_out[0])
+    ga3, dq3, small2, cb, g2, gy1, gh1, small1, hid0 = weights.backward_two(
+        grads, g6, x4, z3, r3, q3, a3, mask, lay, weights.watt[1], x2, z2, r2, d1, weights.w_in[0], weights.w_out[0])
+    weights.channel_grads(n3, dq3, o3, ga3)
     grads = grad_pair("mlp_grads", n2, gh1, gy1, u1)
     input_grad, ga1, dq1, small0, sb = weights.backward_window(
         grads, g2, inputs, z1, r1, q1, p1, mask, lay, weights.watt[0])

time: 589 us -> 592 us (level)
    pallas_call x0 -> x1, Pallas kernels: none -> 91.5 us  [backward_two(): pl.pallas_call(functools.partial(two_phase_back_kernel, plans, (len(args)...]
    pallas_call x5 -> x3, Pallas kernels: 330 us -> 241 us  [image_call(): pl.pallas_call(body, grid=(images,), in_specs=ins, out_specs=out_specs, o...]
where the time goes in v8:
time: 592 us; the launch traced here: 587 us
  Pallas kernels  584 us (99%)
    pallas_call x3, Pallas kernels, image_call(): pl.pallas_call(body, grid=(images,), in_specs=ins, out_specs=out_specs, o...  241 us
    pallas_call x1, Pallas kernels, backward_two(): pl.pallas_call(functools.partial(two_phase_back_kernel, plans, (len(args)...  91.5 us
    pallas_call x1, Pallas kernels, forward_two(): pl.pallas_call(functools.partial(two_phase_kernel, plans, (len(args), len...  89.9 us
    pallas_call x2, Pallas kernels, grad_pair(): pl.pallas_call(functools.partial(grad_pair_kernel, first), grid=(first +...  50 us
    pallas_call x1, Pallas kernels, reduce_now(): pl.pallas_call(functools.partial(reduce_kernel, plan), in_specs=[pl.Block...  36.1 us
    pallas_call x2, Pallas kernels, grad_attention(): pl.pallas_call(functools.partial(grad_attention_kernel, start), grid=(4,)...  35.2 us
    pallas_call x1, Pallas kernels, gather_first(): pl.pallas_call(functools.partial(gather_first_kernel, plan), in_specs=[vm...  30.8 us

profile of v8, /device:TPU:0, one launch (start us, length us, event | category | flops | bytes accessed | tf_op | source)
XLA Modules:
  0.0 586.8 jit_solution(7861234746416235029)
XLA Ops:
  0.6 30.8 %gather_first.1 = (bf16[32,208,384]{2,1,0:T(8,128)(2,1)}, bf16[192,384]{1,0:T(8,128)(2,1)}) custom-call(bf16[1,9,96]{2,1,0:T(8,128)(2,1)} %conv_weight.1, bf16[1,96]{1,0:T(2,128)(2,1)} %conv_bias.1, bf16[1,96]{1,0:T(2,128)(2,1)} %norm_gain.1, bf16[1,96]{1,0:T(2,128)(2,1)} %norm_bias.1, bf16[288,192]{1,0:T(8,128)(2,1)} %qkv0.1, bf16[288,192]{1,0:T(8,128)(2,1)} %qkv1.1, ...), custom_call_target="tpu_custom_call" | custom-call | bytes 5259264 | tf_op jit(solution)/shard_map/gather_first/pallas_call | solution.py:1442
  31.5 6.6 %unpack_first.1 = (bf16[768,3072]{1,0:T(8,128)(2,1)}, f32[4,16,768]{2,1,0:T(8,128)}, f32[16,768]{1,0:T(8,128)}, f32[2,1,3072]{2,1,0:T(1,128)}, f32[8,224,128]{2,1,0:T(8,128)}) custom-call(bf16[32,208,384]{2,1,0:T(8,128)(2,1)} %get-tuple-element.89.got, s32[8]{0:T(128)} %heights.1, s32[8]{0:T(128)} %widths.1), custom_call_target="tpu_custom_call" | custom-call | bytes 11018240 | tf_op jit(solution)/shard_map/unpack_first/pallas_call | solution.py:1308
  38.1 71.7 %window_forward.1 = (bf16[8,224,768]{2,1,0:T(8,128)(2,1)}, f32[8,224,768]{2,1,0:T(8,128)}, f32[8,224,128]{2,1,0:T(8,128)}, bf16[8,224,2304]{2,1,0:T(8,128)(2,1)}...) custom-call(bf16[1568,768]{1,0:T(8,128)(2,1)} %bitcast.31, ...), custom_call_target="tpu_custom_call" | custom-call | flops 10569646080 | bytes 48824320 | tf_op jit(solution)/shard_map/window_forward/pallas_call | solution.py:574
  109.8 89.9 %mlp_channel_forward.1 = (bf16[8,224,768]{2,1,0:T(8,128)(2,1)}, f32[8,224,768]{2,1,0:T(8,128)}, f32[8,224,128]{2,1,0:T(8,128)}, bf16[8,224,3072]{2,1,0:T(8,128)(...) custom-call(f32[8,224,768]{2,1,0:T(8,128)} %get-tuple-element.94.ref, ...), custom_call_target="tpu_custom_call" | custom-call | flops 26424115200 | bytes 101474304 | tf_op jit(solution)/shard_map/mlp_channel_forward/pallas_call | solution.py:1016
  199.7 71.8 %last_mlp.1 = (bf16[1568,768]{1,0:T(8,128)(2,1)}, f32[8,224,768]{2,1,0:T(8,128)}, bf16[8,224,768]{2,1,0:T(8,128)(2,1)}, bf16[8,224,3072]{2,1,0:T(8,128)(2,1)}, b...) custom-call(f32[8,224,768]{2,1,0:T(8,128)} %get-tuple-element.99.x_in, ...), custom_call_target="tpu_custom_call" | custom-call | flops 33822867456 | bytes 53989376 | tf_op jit(solution)/shard_map/last_mlp/pallas_call | solution.py:574
  271.5 25.0 %last_mlp_grads.1 = (bf16[768,3072]{1,0:T(8,128)(2,1)}, bf16[768,3072]{1,0:T(8,128)(2,1)}) custom-call(bf16[1792,768]{1,0:T(8,128)(2,1)} %bitcast.53, bf16[1792,3072]{1,0:T(8,128)(2,1)} %bitcast.44, bf16[1792,768]{1,0:T(8,128)(2,1)} %bitcast.54, bf16[1792,3072]{1,0:T(8,128)(2,1)} %bitcast.43), custom_call_target="tpu_custom_call" | custom-call | flops 16911433728 | bytes 36962304 | tf_op jit(solution)/shard_map/last_mlp_grads/pallas_call | solution.py:699
  296.6 91.5 %channel_mlp_backward.1 = (bf16[8,224,768]{2,1,0:T(8,128)(2,1)}, bf16[8,224,2304]{2,1,0:T(8,128)(2,1)}, f32[16,768]{1,0:T(8,128)}, f32[1,2304]{1,0:T(1,128)}, f3...) custom-call(f32[8,224,768]{2,1,0:T(8,128)} %get-tuple-element.103.re, ...), custom_call_target="tpu_custom_call" | custom-call | flops 27481079808 | bytes 107664384 | tf_op jit(solution)/shard_map/channel_mlp_backward/pallas_call | solution.py:1215
  388.1 17.3 %channel_grads.1.refs_11_ = bf16[32,192,384]{2,1,0:T(8,128)(2,1)} custom-call(bf16[1792,768]{1,0:T(8,128)(2,1)} %bitcast.49, bf16[1792,2304]{1,0:T(8,128)(2,1)} %bitcast.45, bf16[1792,768]{1,0:T(8,128)(2,1)} %bitcast.50, bf16[1792,768]{1,0:T(8,128)(2,1)} %bitcast.52), custom_call_target="tpu_custom_call" | custom-call | flops 8455716864 | bytes 21233664 | tf_op jit(solution)/shard_map/channel_grads/pallas_call | solution.py:1382
  405.4 25.0 %mlp_grads.1 = (bf16[768,3072]{1,0:T(8,128)(2,1)}, bf16[768,3072]{1,0:T(8,128)(2,1)}) custom-call(bf16[1792,768]{1,0:T(8,128)(2,1)} %bitcast.48, bf16[1792,3072]{1,0:T(8,128)(2,1)} %bitcast.42, bf16[1792,768]{1,0:T(8,128)(2,1)} %bitcast.51, bf16[1792,3072]{1,0:T(8,128)(2,1)} %bitcast.41), custom_call_target="tpu_custom_call" | custom-call | flops 16911433728 | bytes 36962304 | tf_op jit(solution)/shard_map/mlp_grads/pallas_call | solution.py:699
  430.3 97.6 %window_backward.1 = (bf16[1568,768]{1,0:T(8,128)(2,1)}, bf16[8,224,768]{2,1,0:T(8,128)(2,1)}, bf16[8,224,2304]{2,1,0:T(8,128)(2,1)}, f32[16,768]{1,0:T(8,128)},...) custom-call(f32[8,224,768]{2,1,0:T(8,128)} %get-tuple-element.119.refs_0_, ...), custom_call_target="tpu_custom_call" | custom-call | flops 12683575296 | bytes 61760512 | tf_op jit(solution)/shard_map/window_backward/pallas_call | solution.py:574
  528.0 17.8 %window_grads.1.refs_0_ = bf16[32,208,384]{2,1,0:T(8,128)(2,1)} custom-call(bf16[1792,768]{1,0:T(8,128)(2,1)} %bitcast.46, bf16[1792,2304]{1,0:T(8,128)(2,1)} %bitcast.34, bf16[1792,768]{1,0:T(8,128)(2,1)} %bitcast.47, bf16[1792,768]{1,0:T(8,128)(2,1)} %bitcast.35, f32[16,768]{1,0:T(8,128)} %get-tuple-element.139.refs_0_, ...), custom_call_target="tpu_custom_call" | custom-call | flops 8455716864 | bytes 21626880 | tf_op jit(solution)/shard_map/window_grads/pallas_call | solution.py:1382
  545.8 0.0 copy-start
  545.8 36.1 %reduce_last.1.att0 = f32[208,384]{1,0:T(8,128)} custom-call(bf16[32,208,384]{2,1,0:T(8,128)(2,1)} %window_grads.1.refs_0_), custom_call_target="tpu_custom_call" | custom-call | bytes 5111808 | tf_op jit(solution)/shard_map/reduce_last/pallas_call | solution.py:1246
  581.9 3.0 finish.1
  584.9 0.0 copy-done
  584.9 1.4 copy.31
Async XLA Ops:
  545.8 39.2 %copy-start = (bf16[1568,768]{1,0:T(8,128)(2,1)S(1)}, bf16[1568,768]{1,0:T(8,128)(2,1)}, u32[]{:S(2)}) copy-start(bf16[1568,768]{1,0:T(8,128)(2,1)} %get-tuple-element.134) | copy-start | bytes 7225348
